TPU v7x, 32 devices: a whole 2x2x4 slice. The times are simulated.
32 devices in a mesh: seq: 8 (over z, x), fsdp: 4 (over y, core).
Axes of the slice: x: 2, y: 2, z: 4, core: 2. Of those that a mesh axis runs over, the one named last changes fastest.
Arguments:
- hidden: bfloat16 [4, 2048, 1536], P('fsdp', 'seq'), may hold values from -6 to 6
- cotangent: bfloat16 [4, 2048, 1536], P('fsdp', 'seq'), may hold values from -6 to 6
- norm_gain: bfloat16 [1536], P('fsdp'), may hold values from 0.5 to 1.5
- in_weight: bfloat16 [1536, 6448], P('fsdp'), may hold values from -0.15625 to 0.15625
- conv_weight: bfloat16 [3328, 4], P('fsdp'), may hold values from -3 to 3
- conv_bias: bfloat16 [3328], P('fsdp'), may hold values from -3 to 3
- dt_bias: bfloat16 [48], P('fsdp'), may hold values from -9 to -1
- a_log: bfloat16 [48], P('fsdp'), may hold values from -3 to 1.5
- skip_d: bfloat16 [48], P('fsdp'), may hold values from 0.5 to 1.5
- inner_gain: bfloat16 [3072], P('fsdp'), may hold values from 0.5 to 1.5
- out_weight: bfloat16 [3072, 1536], P('fsdp'), may hold values from -0.109375 to 0.109375
Outputs:
- block_out: float32 [4, 2048, 1536], P('fsdp', 'seq')
- grad_hidden: float32 [4, 2048, 1536], P('fsdp', 'seq')
- grad_norm_gain: float32 [1536], P('fsdp')
- grad_in_weight: float32 [1536, 6448], P('fsdp')
- grad_conv_weight: float32 [3328, 4], P('fsdp')
- grad_conv_bias: float32 [3328], P('fsdp')
- grad_dt_bias: float32 [48], P('fsdp')
- grad_a_log: float32 [48], P('fsdp')
- grad_skip_d: float32 [48], P('fsdp')
- grad_inner_gain: float32 [3072], P('fsdp')
- grad_out_weight: float32 [3072, 1536], P('fsdp')
All inputs are finite; a program needn't handle non-finite values.
Results may differ from a plain program's by a relative error of at most 0.0049.
The roundings to bfloat16 on the way count: a program that leaves them out, or rounds other values in their place, can miss the bound.
Values may be sent and summed in bfloat16 or wider, within the bound.
No kernel may reach another device: no remote copies, remote signals or barrier semaphores. Data moves between devices by JAX's collectives and lax.ppermute only.
A program may use at most 384 MiB of HBM per device.

v0:
```python
import jax
import jax.numpy as jnp
from jax import lax
from jax.sharding import PartitionSpec as P

D = 1536
KCONV = 4
SPAN = 256
DI = 3072
H = 48
CONVW = 3328
PROJ = 6448


def passed_along(value, axis, steps):
    count = lax.axis_size(axis)
    first, last = (max(0, -steps), min(count, count - steps))
    return lax.ppermute(value, axis, [(source, source + steps) for source in range(first, last)])


def rms_norm(values, gain_vec):
    scale = lax.rsqrt(jnp.mean(values * values, axis=-1, keepdims=True) + 1e-05)
    return values * scale * gain_vec


def gated_norm(mixed, gate_in, gain_vec):
    gated = mixed * jax.nn.silu(gate_in)
    return rms_norm(gated, gain_vec)


def conv_silu(padded, weight, shift_bias):
    out_rows = padded.shape[0] - weight.shape[1] + 1
    running = shift_bias[None, :] + padded[0:out_rows] * weight[:, 0]
    for offset in range(1, weight.shape[1]):
        running = running + padded[offset : offset + out_rows] * weight[:, offset]
    return jax.nn.silu(running)


def ssd_scan(inputs_x, raw_step, bc_rows, log_rate, step_bias, skip_vec):
    seq_len, head_count = raw_step.shape
    head_width = inputs_x.shape[1] // head_count
    state_width = bc_rows.shape[1] // 2
    block_count = seq_len // SPAN
    step_size = jax.nn.softplus(raw_step + step_bias)
    decay_rate = -jnp.exp(log_rate)
    x_blocks = inputs_x.reshape(block_count, SPAN, head_count, head_width)
    step_blocks = step_size.reshape(block_count, SPAN, head_count)
    b_blocks = bc_rows[:, :state_width].reshape(block_count, SPAN, state_width)
    c_blocks = bc_rows[:, state_width:].reshape(block_count, SPAN, state_width)
    lower_mask = (jnp.arange(SPAN)[:, None] >= jnp.arange(SPAN)[None, :])[:, :, None]
    highest = lax.Precision.HIGHEST

    def advance(carry_state, block_in):
        x_block, step_block, b_block, c_block = block_in
        log_decay = jnp.cumsum(step_block * decay_rate, axis=0)
        log_gap = log_decay[:, None, :] - log_decay[None, :, :]
        decay_mat = jnp.where(lower_mask, jnp.exp(jnp.where(lower_mask, log_gap, 0.0)), 0.0)
        intersection = jnp.dot(c_block, b_block.T, precision=highest)
        mixing = intersection[:, :, None] * decay_mat * step_block[None, :, :]
        local_part = jnp.einsum("ijh,jhp->ihp", mixing, x_block, precision=highest)
        carried = (
            jnp.einsum("in,hnp->ihp", c_block, carry_state, precision=highest)
            * jnp.exp(log_decay)[:, :, None]
        )
        to_end = jnp.exp(log_decay[-1][None, :] - log_decay) * step_block
        fresh = jnp.einsum("jn,jh,jhp->hnp", b_block, to_end, x_block, precision=highest)
        next_state = carry_state * jnp.exp(log_decay[-1])[:, None, None] + fresh
        output = local_part + carried + skip_vec[None, :, None] * x_block
        return (next_state, output)

    start_state = jnp.zeros((head_count, state_width, head_width), jnp.float32)
    _, outputs = lax.scan(
        jax.checkpoint(advance), start_state, (x_blocks, step_blocks, b_blocks, c_blocks)
    )
    return outputs.reshape(seq_len, head_count * head_width)


def across_rows(left, right):
    return lax.dot_general(
        left, right, (((0,), (0,)), ((), ())), preferred_element_type=jnp.float32
    )


def against_cols(left, right):
    return lax.dot_general(
        left, right, (((1,), (1,)), ((), ())), preferred_element_type=jnp.float32
    )


def body(
    hidden,
    cotangent,
    norm_gain,
    in_weight,
    conv_weight,
    conv_bias,
    dt_bias,
    a_log,
    skip_d,
    inner_gain,
    out_weight,
):
    seq_count = lax.axis_size("seq")
    owner_count = lax.axis_size("fsdp")
    seq_rank = lax.axis_index("seq")
    gain_n, w_in, w_conv, b_conv, bias_dt, log_a, skip_vec, gain_i, w_out = (
        lax.all_gather(norm_gain, "fsdp", axis=0, tiled=True),
        lax.all_gather(in_weight, "fsdp", axis=0, tiled=True),
        lax.all_gather(conv_weight, "fsdp", axis=0, tiled=True),
        lax.all_gather(conv_bias, "fsdp", axis=0, tiled=True),
        lax.all_gather(dt_bias, "fsdp", axis=0, tiled=True),
        lax.all_gather(a_log, "fsdp", axis=0, tiled=True),
        lax.all_gather(skip_d, "fsdp", axis=0, tiled=True),
        lax.all_gather(inner_gain, "fsdp", axis=0, tiled=True),
        lax.all_gather(out_weight, "fsdp", axis=0, tiled=True),
    )
    hidden_f = hidden[0].astype(jnp.float32)
    cot_rows = cotangent[0]
    token_count = hidden_f.shape[0]
    normed, norm_pull = jax.vjp(rms_norm, hidden_f, gain_n.astype(jnp.float32))
    normed_b = normed.astype(jnp.bfloat16)
    projected = jnp.dot(normed_b, w_in, preferred_element_type=jnp.float32).astype(jnp.bfloat16)
    gate_in = projected[:, :DI]
    conv_in = projected[:, DI : DI + CONVW]
    raw_step = projected[:, DI + CONVW :]
    rim_rows = passed_along(conv_in[token_count - KCONV + 1 :], "seq", 1)
    padded = jnp.concatenate([rim_rows, conv_in], 0).astype(jnp.float32)
    conv_out, conv_pull = jax.vjp(
        conv_silu, padded, w_conv.astype(jnp.float32), b_conv.astype(jnp.float32)
    )
    conv_act = conv_out.astype(jnp.bfloat16)
    head_x, head_step = (
        lax.all_to_all(conv_act[:, :DI], "seq", split_axis=1, concat_axis=0, tiled=True),
        lax.all_to_all(raw_step, "seq", split_axis=1, concat_axis=0, tiled=True),
    )
    whole_bc = lax.all_gather(conv_act[:, DI:], "seq", axis=0, tiled=True)
    group_size = H // seq_count
    first_head = seq_rank * group_size
    log_part = lax.dynamic_slice_in_dim(log_a.astype(jnp.float32), first_head, group_size)
    bias_part = lax.dynamic_slice_in_dim(bias_dt.astype(jnp.float32), first_head, group_size)
    skip_part = lax.dynamic_slice_in_dim(skip_vec.astype(jnp.float32), first_head, group_size)
    mixed, ssd_pull = jax.vjp(
        ssd_scan,
        head_x.astype(jnp.float32),
        head_step.astype(jnp.float32),
        whole_bc.astype(jnp.float32),
        log_part,
        bias_part,
        skip_part,
    )
    mixed_home = lax.all_to_all(
        mixed.astype(jnp.bfloat16), "seq", split_axis=0, concat_axis=1, tiled=True
    )
    gated, gate_pull = jax.vjp(
        gated_norm,
        mixed_home.astype(jnp.float32),
        gate_in.astype(jnp.float32),
        gain_i.astype(jnp.float32),
    )
    gated_b = gated.astype(jnp.bfloat16)
    block_out = hidden_f + jnp.dot(gated_b, w_out, preferred_element_type=jnp.float32)
    grad_w_out = across_rows(gated_b, cot_rows)
    d_gated = against_cols(cot_rows, w_out)
    d_mixed, d_gate, grad_gain_i = gate_pull(d_gated)
    d_mixed_heads = lax.all_to_all(
        d_mixed.astype(jnp.bfloat16), "seq", split_axis=1, concat_axis=0, tiled=True
    )
    d_x, d_step, d_bc, grad_log, grad_bias, grad_skip = ssd_pull(d_mixed_heads.astype(jnp.float32))
    d_bc_home = lax.psum_scatter(d_bc, "seq", scatter_dimension=0, tiled=True)
    d_x_home, d_step_home = (
        lax.all_to_all(d_x.astype(jnp.bfloat16), "seq", split_axis=0, concat_axis=1, tiled=True),
        lax.all_to_all(d_step.astype(jnp.bfloat16), "seq", split_axis=0, concat_axis=1, tiled=True),
    )
    d_conv = jnp.concatenate([d_x_home.astype(jnp.float32), d_bc_home], 1)
    d_padded, grad_w_conv, grad_b_conv = conv_pull(d_conv)
    spill_rows = passed_along(d_padded[: KCONV - 1], "seq", -1)
    d_conv_in = d_padded[KCONV - 1 :].at[token_count - KCONV + 1 :].add(spill_rows)
    d_proj = jnp.concatenate([d_gate, d_conv_in, d_step_home.astype(jnp.float32)], 1).astype(
        jnp.bfloat16
    )
    grad_w_in = across_rows(normed_b, d_proj)
    d_normed = against_cols(d_proj, w_in)
    d_hidden, grad_gain_n = norm_pull(d_normed)
    grad_hidden = cot_rows.astype(jnp.float32) + d_hidden
    head_zeros = jnp.zeros((H,), jnp.float32)
    full_bias = lax.dynamic_update_slice(head_zeros, grad_bias, (first_head,))
    full_log = lax.dynamic_update_slice(head_zeros, grad_log, (first_head,))
    full_skip = lax.dynamic_update_slice(head_zeros, grad_skip, (first_head,))
    big_in = grad_w_in.reshape(owner_count, -1)
    big_out = grad_w_out.reshape(owner_count, -1)
    small_pack = jnp.concatenate(
        [
            grad_gain_n.reshape(owner_count, -1),
            grad_w_conv.reshape(owner_count, -1),
            grad_b_conv.reshape(owner_count, -1),
            full_bias.reshape(owner_count, -1),
            full_log.reshape(owner_count, -1),
            full_skip.reshape(owner_count, -1),
            grad_gain_i.reshape(owner_count, -1),
        ],
        axis=1,
    )
    padding = -small_pack.shape[1] % seq_count
    small_pack = jnp.pad(small_pack, ((0, 0), (0, padding)))
    owned = (
        lax.psum_scatter(big_in, "fsdp", scatter_dimension=0, tiled=True),
        lax.psum_scatter(big_out, "fsdp", scatter_dimension=0, tiled=True),
        lax.psum_scatter(small_pack, "fsdp", scatter_dimension=0, tiled=True),
    )
    summed = lax.psum((owned[0], owned[1], owned[2]), "seq")
    flat_pack = summed[2].reshape(-1)
    widths = [
        D // owner_count,
        CONVW // owner_count * KCONV,
        CONVW // owner_count,
        H // owner_count,
        H // owner_count,
        H // owner_count,
        DI // owner_count,
    ]
    pieces_out = []
    cursor = 0
    for width_now in widths:
        pieces_out.append(flat_pack[cursor : cursor + width_now])
        cursor = cursor + width_now
    return (
        block_out[None],
        grad_hidden[None],
        pieces_out[0],
        summed[0].reshape(D // owner_count, PROJ),
        pieces_out[1].reshape(CONVW // owner_count, KCONV),
        pieces_out[2],
        pieces_out[3],
        pieces_out[4],
        pieces_out[5],
        pieces_out[6],
        summed[1].reshape(DI // owner_count, D),
    )


def solution(mesh):
    return jax.shard_map(
        body,
        mesh=mesh,
        in_specs=(
            P("fsdp", "seq", None),
            P("fsdp", "seq", None),
            P("fsdp"),
            P("fsdp", None),
            P("fsdp", None),
            P("fsdp"),
            P("fsdp"),
            P("fsdp"),
            P("fsdp"),
            P("fsdp"),
            P("fsdp", None),
        ),
        out_specs=(
            P("fsdp", "seq", None),
            P("fsdp", "seq", None),
            P("fsdp"),
            P("fsdp", None),
            P("fsdp", None),
            P("fsdp"),
            P("fsdp"),
            P("fsdp"),
            P("fsdp"),
            P("fsdp"),
            P("fsdp", None),
        ),
        check_vma=False,
    )
```

profile of v0, /device:TPU:0, one launch (start us, length us, event | category | flops | bytes accessed | tf_op | source)
XLA Modules:
  0.0 2510.5 jit_solution(16886511870413851377)
XLA Ops:
  8.0 6.2 all-gather
  14.2 5.5 all-gather.1
  20.2 117.0 %all-gather.7.cloned.1.call-done = bf16[1536,6448]{0,1:T(8,128)(2,1)} async-done(((bf16[384,6448]{0,1:T(8,128)(2,1)}), bf16[1536,6448]{0,1:T(8,128)(2,1)}) %all-gather.7.cloned.1.call-update) | async-done | bytes 19808272 | tf_op jit(solution)/shard_map/all_gather | solution.py:108
  137.2 10.1 convolution_convert_fusion
  156.2 6.1 all-reduce.22
  164.0 7.0 multiply_convert_fusion
  172.3 4.6 all-to-all-start
  178.2 5.6 all-to-all-done
  183.8 4.3 all-to-all-start.1
  190.4 39.8 %all-gather.9.cloned.1.call-done = bf16[2048,256]{0,1:T(8,128)(2,1)} async-done(((bf16[256,256]{0,1:T(8,128)(2,1)}), bf16[2048,256]{0,1:T(8,128)(2,1)}) %all-gather.9.cloned.1.call-update) | async-done | bytes 1048592 | tf_op jit(solution)/shard_map/all_gather | solution.py:136
  237.3 87.6 %while.47 = (s32[]{:T(128)}, f32[6,128,64]{1,2,0:T(8,128)S(1)}, bf16[8,256,6,64]{1,3,2,0:T(8,128)(2,1)}, f32[8,6,128,64]{2,3,1,0:T(8,128)}, f32[8,256,6]{1,2,0:T...) while((s32[]{:T(128)}, f32[6,128,64]{1,2,0:T(8,128)S(1)}, ...), condition=%wide.region_4.5_spmd.clone.clone, body=%wide.region_1.4_spmd.clone.clone.sunk | while | flops 707449344 | bytes 4791139 | solution.py:72
  325.0 5.7 all-to-all-start.2
  330.7 5.2 all-gather.2
  335.9 30.8 %all-to-all-done.2 = bf16[8,256,384]{1,2,0:T(8,128)(2,1)} async-done(((bf16[8,256,384]{1,2,0:T(8,128)(2,1)}), bf16[8,256,384]{1,2,0:T(8,128)(2,1)}, u32[]{:S(2)}, u32[]{:S(2)}) %all-to-all-start.2) | async-done | bytes 1572896 | tf_op jit(solution)/shard_map/all_to_all | solution.py:151
  369.7 7.5 multiply_reduce_fusion.9
  377.3 4.9 fusion.117
  386.2 36.8 %all-to-all-done.3 = bf16[256,8,384]{0,2,1:T(8,128)(2,1)S(1)} async-done(((bf16[256,8,384]{0,2,1:T(8,128)(2,1)}), bf16[256,8,384]{0,2,1:T(8,128)(2,1)S(1)}, u32[]{:S(2)}, u32[]{:S(2)}) %all-to-all-start.3) | async-done | bytes 1572896 | tf_op jit(solution)/shard_map/all_to_all | solution.py:165
  428.4 199.6 %while.46 = (s32[]{:T(128)}, f32[6]{0:T(128)S(1)}, f32[6]{0:T(128)S(1)}, f32[6,128,64]{1,2,0:T(8,128)S(1)}, bf16[8,256,6,64]{1,3,2,0:T(8,128)(2,1)}, /*index=5*/...) while((s32[]{:T(128)}, f32[6]{0:T(128)S(1)}, ...), condition=%wide.region_21.22_spmd.clone, body=%wide.region_7.21_spmd.clone.sunk | while | flops 1670820352 | bytes 13765989 | solution.py:72
  440.7 7.6 reduce-window.74
  465.7 7.6 reduce-window.74
  490.6 7.6 reduce-window.74
  515.6 7.6 reduce-window.74
  540.5 7.6 reduce-window.74
  565.5 7.6 reduce-window.74
  590.5 7.6 reduce-window.74
  615.4 7.6 reduce-window.74
  632.9 10.4 all_to_all.69
  643.3 4.3 all-to-all-start.4
  647.6 18.0 fusion.129
  665.6 28.0 %reshape.411 = f32[4,1179648]{1,0:T(4,128)} reshape(f32[3072,1536]{1,0:T(8,128)} %fusion.129) | data formatting | bytes 37748736 | tf_op jit(solution)/shard_map/reshape | solution.py:190
  698.4 18.6 reduce-scatter.2.cloned.1.call-done
  717.0 13.1 multiply_reduce_fusion.8
  743.7 4.3 slice.242
  757.3 10.5 scatter-add.4
  767.8 17.8 fusion.127
  785.6 14.1 fusion.122
  799.7 41.8 %reshape.494 = f32[9904128]{0:T(1024)} reshape(f32[1536,6448]{1,0:T(8,128)} %fusion.127) | data formatting | bytes 79233024
  841.5 47.3 %reshape.408 = f32[4,2476032]{1,0:T(4,128)} reshape(f32[9904128]{0:T(1024)} %reshape.494) | data formatting | bytes 79233024 | tf_op jit(solution)/shard_map/reshape | solution.py:189
  889.7 962.8 %all-reduce.28.cloned.1.call-done = (f32[4,5352]{1,0:T(4,128)}, f32[4,2476032]{1,0:T(4,128)}, f32[4,1179648]{1,0:T(4,128)}) async-done(((f32[4,5352]{1,0:T(4,128)}, f32[4,2476032]{1,0:T(4,128)}, f32[4,1179648]{1,0:T(4,128)}), (f32[4,5352]{1,0:T(4,128)}, f32[4,2476032]{1,0:T(4,128)}, f32[4,1179648]{1,0:T(4,128)})) %all-reduce.28.cloned.1.call-update) | async-done | bytes 58576528
  1852.4 53.1 %dynamic-slice_reduce_fusion.1 = f32[1179648]{0:T(1024)} fusion(f32[4,1179648]{1,0:T(4,128)} %get-tuple-element.934, u32[]{:T(128)} %bitcast.84), kind=kLoop, calls=%fused_computation.143 | loop fusion | bytes 9437188
  1905.6 108.5 %dynamic-slice_reduce_fusion = f32[2476032]{0:T(1024)} fusion(f32[4,2476032]{1,0:T(4,128)} %get-tuple-element.933, u32[]{:T(128)} %bitcast.84), kind=kLoop, calls=%fused_computation.134 | loop fusion | bytes 19808260
  2014.1 5.8 reshape.412
  2019.9 11.4 reshape.409
  2031.3 7.8 fusion.118
  2042.4 39.3 %psum.21 = f32[1,5352]{1,0:T(1,128)S(1)} all-reduce(f32[1,5352]{1,0:T(1,128)S(1)} %constant_dynamic-slice_fusion), channel_id=1, replica_groups=mesh['seq'=8,'fsdp'=4] {'seq'}, use_global_device_ids=true, to_apply=%region_33.34 | all-reduce | flops 5352 | bytes 42816 | tf_op jit(solution)/shard_map/psum | solution.py:210
  2085.5 402.3 %all-reduce.26.cloned.1.call-done = (f32[384,6448]{1,0:T(8,128)}, f32[768,1536]{1,0:T(8,128)}) async-done(((f32[384,6448]{1,0:T(8,128)}, f32[768,1536]{1,0:T(8,128)}), (f32[384,6448]{1,0:T(8,128)}, f32[768,1536]{1,0:T(8,128)})) %all-reduce.26.cloned.1.call-update) | async-done | bytes 14622736 | tf_op jit(solution)/shard_map/psum | solution.py:210
  2487.7 10.7 copy.207
  2498.4 4.8 copy.344
  (660 shorter events, 300.6 us)
Async XLA Ops:
  7.2 0.8 copy-start.18
  7.2 7.0 copy-start.14
  7.2 12.7 copy-start.5
  7.2 130.0 %all-gather.7.cloned.1.call-start = ((), (), s32[]{:S(2)}) async-start(), calls=%async_computation.7 | async-start | bytes 24760320 | tf_op jit(solution)/shard_map/all_gather | solution.py:108
  7.9 222.3 %all-gather.9.cloned.1.call-start = ((), (), s32[]{:S(2)}) async-start(), calls=%async_computation.8 | async-start | bytes 1179648 | tf_op jit(solution)/shard_map/all_gather | solution.py:136
  20.1 127.2 %copy-start.11 = (f32[256]{0:T(256)}, f32[256]{0:T(256)S(1)}, u32[]{:S(2)}) copy-start(f32[256]{0:T(256)S(1)} %fusion.125) | copy-start | bytes 3076
  20.1 133.2 %copy-start.15 = (u32[32]{0:T(128)S(1)}, u32[32]{0:T(128)}, u32[]{:S(2)}) copy-start(u32[32]{0:T(128)} %constant.195) | copy-start | bytes 388
  20.2 135.1 %copy-start.21 = (bf16[12]{0:T(256)(128)(2,1)S(1)}, bf16[12]{0:T(256)(128)(2,1)}, u32[]{:S(2)}) copy-start(bf16[12]{0:T(256)(128)(2,1)} %param.25) | copy-start | bytes 76
  20.2 135.3 %copy-start.22 = (bf16[12]{0:T(256)(128)(2,1)S(1)}, bf16[12]{0:T(256)(128)(2,1)}, u32[]{:S(2)}) copy-start(bf16[12]{0:T(256)(128)(2,1)} %param.23) | copy-start | bytes 76
  20.2 135.5 %copy-start.23 = (bf16[12]{0:T(256)(128)(2,1)S(1)}, bf16[12]{0:T(256)(128)(2,1)}, u32[]{:S(2)}) copy-start(bf16[12]{0:T(256)(128)(2,1)} %param.24) | copy-start | bytes 76
  20.2 135.8 %copy-start.16 = (bf16[832]{0:T(1024)(128)(2,1)S(1)}, bf16[832]{0:T(1024)(128)(2,1)}, u32[]{:S(2)}) copy-start(bf16[832]{0:T(1024)(128)(2,1)} %param.22) | copy-start | bytes 4996
  147.3 1.7 copy-start.7
  149.3 13.6 slice-start
  149.6 12.8 collective-permute-start
  162.4 26.7 %copy-start.24 = (bf16[48]{0:T(256)(128)(2,1)}, bf16[48]{0:T(256)(128)(2,1)S(1)}, u32[]{:S(2)}) copy-start(bf16[48]{0:T(256)(128)(2,1)S(1)} %get-tuple-element.937) | copy-start | bytes 292
  164.0 7.0 copy-start
  164.0 7.7 slice-start.1
  172.3 11.5 all-to-all-start
  183.8 50.5 %all-to-all-start.1 = ((bf16[256,8,384]{0,2,1:T(8,128)(2,1)}), bf16[256,8,384]{0,2,1:T(8,128)(2,1)}, u32[]{:S(2)}, u32[]{:S(2)}) async-start(bf16[256,8,384]{0,2,1:T(8,128)(2,1)} %bitcast.7), calls=%async_computation.1 | async-start | bytes 3145728 | tf_op jit(solution)/shard_map/all_to_all | solution.py:133
  188.1 181.6 %all-gather.11.cloned.1.call-start = ((), (), s32[]{:S(2)}) async-start(), calls=%async_computation.9 | async-start | bytes 11796480 | tf_op jit(solution)/shard_map/all_gather | solution.py:115
  188.9 44.1 %copy-start.19 = (f32[48]{0:T(128)}, f32[48]{0:T(128)S(1)}, u32[]{:S(2)}) copy-start(f32[48]{0:T(128)S(1)} %convert_element_type.134) | copy-start | bytes 580
  325.0 10.9 copy-start.4
  325.0 5.7 copy-start.17
  325.0 41.8 %all-to-all-start.2 = ((bf16[8,256,384]{1,2,0:T(8,128)(2,1)}), bf16[8,256,384]{1,2,0:T(8,128)(2,1)}, u32[]{:S(2)}, u32[]{:S(2)}) async-start(bf16[8,256,384]{1,2,0:T(8,128)(2,1)} %bitcast.492), calls=%async_computation.2 | async-start | bytes 3145728 | tf_op jit(solution)/shard_map/all_to_all | solution.py:151
  369.7 7.6 copy-start.1
  369.7 7.6 copy-start.8
  382.2 3.8 copy-start.25
  382.2 3.9 copy-start.20
  382.2 40.7 %all-to-all-start.3 = ((bf16[256,8,384]{0,2,1:T(8,128)(2,1)}), bf16[256,8,384]{0,2,1:T(8,128)(2,1)S(1)}, u32[]{:S(2)}, u32[]{:S(2)}) async-start(bf16[256,8,384]{0,2,1:T(8,128)(2,1)} %bitcast.493), calls=%async_computation.3 | async-start | bytes 3145728 | tf_op jit(solution)/shard_map/all_to_all | solution.py:165
  386.0 331.0 %reduce-scatter.2.cloned.1.call-start = ((), (), s32[]{:S(2)}) async-start(), calls=%async_computation.10 | async-start | bytes 2359296 | tf_op jit(solution)/shard_map/reduce_scatter | solution.py:169
  632.6 15.0 copy-start.2
  643.3 51.8 %all-to-all-start.4 = ((bf16[8,256,384]{1,2,0:T(8,128)(2,1)}), bf16[8,256,384]{1,2,0:T(8,128)(2,1)}, u32[]{:S(2)}, u32[]{:S(2)}) async-start(bf16[8,256,384]{1,2,0:T(8,128)(2,1)} %bitcast.491), calls=%async_computation.4 | async-start | bytes 3145728 | tf_op jit(solution)/shard_map/all_to_all | solution.py:171
  647.6 1204.9 %all-reduce.28.cloned.1.call-start = ((), (), s32[]{:S(2)}) async-start(), calls=%async_computation.12 | async-start | bytes 117153792
  736.8 2.3 copy-start.3
  742.3 10.2 collective-permute-start.1
  841.5 47.3 %copy-start.13 = (f32[4,12]{1,0:T(4,128)S(1)}, f32[4,12]{1,0:T(4,128)}, u32[]{:S(2)}) copy-start(f32[4,12]{1,0:T(4,128)} %reshape.406) | copy-start | bytes 580
  889.6 1598.1 %all-reduce.26.cloned.1.call-start = ((), (), s32[]{:S(2)}) async-start(), calls=%async_computation.11 | async-start | bytes 29491200 | tf_op jit(solution)/shard_map/psum | solution.py:210
  2031.3 7.9 copy-start.12
  2031.3 7.9 copy-start.6
  2031.3 7.9 copy-start.9
  2031.3 7.9 copy-start.10
Sparse Core Ops, SparseCore 0:
  9.6 127.5 all-gather.6
  171.8 58.3 all-gather.8
  231.8 64.5 all-gather.10
  632.8 84.1 reduce-scatter.1
  889.8 962.6 all-reduce.27
  2031.4 456.2 all-reduce.25
where the time goes:
time: 2520 us; the launch traced here: 2510 us
  waiting for transfers between devices  1620 us (64%)
  local copies, waits for them, and re-layouts  400 us (16%)
  matrix products  220 us (9%)
  other arithmetic  157 us (6%)
  blocking collectives  72.7 us (3%)
  starting transfers between devices  27.7 us (1%)
    unnamed x7, waiting for transfers between devices  964 us
    psum x1, waiting for transfers between devices, body(): summed = lax.psum((owned[0], owned[1], owned[2]), 'seq')  402 us
    unnamed x72, local copies, waits for them, and re-layouts  230 us
    all_gather x1, waiting for transfers between devices, body(): lax.all_gather(in_weight, 'fsdp', axis=0, tiled=True)  117 us
    another operation x73, other arithmetic  97 us
    dot_general x24, matrix products, advance(): local_part = jnp.einsum('ijh,jhp->ihp', mixing, x_block, precision=highest)  65.6 us
  transfers between devices with their start and end apart: 13, of which 8 were waited for; matrix products, arithmetic and copies ran while one was open for 7% of the time, Pallas kernels for 0%

commit v1 on v0

v1 whole, which is shorter than its diff:
```python
import functools

import jax
import jax.numpy as jnp
from jax import lax
from jax.experimental import pallas as pl
from jax.experimental.pallas import tpu as pltpu
from jax.sharding import PartitionSpec as P


EPS = 1e-05
LANES = 128
GROUP = 8
WIDE = True
BF16 = jnp.bfloat16
F32 = jnp.float32
HIGHEST = lax.Precision.HIGHEST


def dims(left, right, contract):
    return lax.dot_general(left, right, (contract, ((), ())), preferred_element_type=F32)


def across_rows(left, right):
    return dims(left, right, ((0,), (0,)))


def against_cols(left, right):
    return dims(left, right, ((1,), (1,)))


def plain_dot(left, right):
    return dims(left, right, ((1,), (0,)))


def halves(values):
    high = values.astype(BF16)
    return high, (values - high.astype(F32)).astype(BF16)


def rounded(values):
    return lax.reduce_precision(values, 8, 7)


def host_halves(values):
    high = rounded(values)
    return high.astype(BF16), (values - high).astype(BF16)


def per_head_lanes(columns, first, head_width, rows):
    per_tile = LANES // head_width
    lane = lax.broadcasted_iota(jnp.int32, (rows, LANES), 1)
    spread = jnp.broadcast_to(columns[:, first : first + 1], (rows, LANES))
    for extra in range(1, per_tile):
        column = columns[:, first + extra : first + extra + 1]
        spread = jnp.where(lane < extra * head_width, spread, column)
    return spread


def state_kernel(head_width, x_ref, bt_ref, te_ref, out_ref):
    rows = x_ref.shape[0]
    te_cols = te_ref[...].T
    per_tile = LANES // head_width
    for tile in range(x_ref.shape[1] // LANES):
        lanes = slice(tile * LANES, (tile + 1) * LANES)
        spread = per_head_lanes(te_cols, tile * per_tile, head_width, rows)
        high, low = halves(x_ref[:, lanes].astype(F32) * spread)
        out_ref[:, lanes] = plain_dot(bt_ref[...], high) + plain_dot(bt_ref[...], low)


def local_state(x_rows, b_cols, to_end, head_width):
    rows, width = x_rows.shape
    states = b_cols.shape[0]
    block = GROUP * head_width
    return pl.pallas_call(
        functools.partial(state_kernel, head_width),
        out_shape=jax.ShapeDtypeStruct((states, width), F32),
        grid=(width // block,),
        in_specs=[
            pl.BlockSpec((rows, block), lambda g: (0, g)),
            pl.BlockSpec((states, rows), lambda g: (0, 0)),
            pl.BlockSpec((GROUP, rows), lambda g: (g, 0)),
        ],
        out_specs=pl.BlockSpec((states, block), lambda g: (0, g)),
        name="local_state",
    )(x_rows, b_cols, to_end)


def tile_exponent(row_part, col_part, diagonal, lower):
    gap = row_part - col_part if lower else col_part - row_part
    if diagonal:
        first = lax.broadcasted_iota(jnp.int32, gap.shape, 0)
        second = lax.broadcasted_iota(jnp.int32, gap.shape, 1)
        keep = first >= second if not lower else second >= first
        gap = jnp.where(keep, gap, -1e30)
    return jnp.exp(gap)


def inner_kernel(head_width, x_ref, b_ref, c_ref, decay_ref, source_ref, out_ref, meet_ref):
    rows = x_ref.shape[0]
    tiles = rows // LANES

    @pl.when(pl.program_id(0) == 0)
    def _():
        meet_ref[...] = against_cols(c_ref[...], b_ref[...])

    decay_cols = decay_ref[...].T
    for late in range(tiles):
        out_rows = slice(late * LANES, (late + 1) * LANES)
        for head in range(GROUP):
            lanes = slice(head * head_width, (head + 1) * head_width)
            total = None
            for early in range(late + 1):
                in_rows = slice(early * LANES, (early + 1) * LANES)
                weight = tile_exponent(
                    source_ref[head : head + 1, in_rows],
                    decay_cols[out_rows, head : head + 1],
                    early == late,
                    False,
                )
                high, low = halves(meet_ref[out_rows, in_rows] * weight)
                x_now = x_ref[in_rows, lanes]
                part = plain_dot(high, x_now) + plain_dot(low, x_now)
                total = part if total is None else total + part
            out_ref[out_rows, lanes] = total


def inner_part(x_rows, b_rows, c_rows, decay, source, head_width):
    rows, width = x_rows.shape
    states = b_rows.shape[1]
    block = GROUP * head_width
    return pl.pallas_call(
        functools.partial(inner_kernel, head_width),
        out_shape=jax.ShapeDtypeStruct((rows, width), F32),
        grid=(width // block,),
        in_specs=[
            pl.BlockSpec((rows, block), lambda g: (0, g)),
            pl.BlockSpec((rows, states), lambda g: (0, 0)),
            pl.BlockSpec((rows, states), lambda g: (0, 0)),
            pl.BlockSpec((GROUP, rows), lambda g: (g, 0)),
            pl.BlockSpec((GROUP, rows), lambda g: (g, 0)),
        ],
        out_specs=pl.BlockSpec((rows, block), lambda g: (0, g)),
        scratch_shapes=[pltpu.VMEM((rows, rows), F32)],
        name="inner_part",
    )(x_rows, b_rows, c_rows, decay, source)


def middle_kernel(
    inner_ref,
    x_ref,
    gate_ref,
    dgated_ref,
    c_ref,
    state_ref,
    rest_ref,
    decay_ref,
    spread_ref,
    fold_ref,
    skip_ref,
    gain_ref,
    gated_ref,
    dmixed_ref,
    dgate_ref,
    dstate_ref,
    rowsum_ref,
    dgain_ref,
    dskip_ref,
):
    @pl.when(pl.program_id(0) == 0)
    def _():
        dstate_ref[...] = jnp.zeros_like(dstate_ref)
        dgain_ref[...] = jnp.zeros_like(dgain_ref)
        dskip_ref[...] = jnp.zeros_like(dskip_ref)

    decay = plain_dot(decay_ref[...], spread_ref[...])
    carried = plain_dot(c_ref[...], state_ref[...]) + plain_dot(c_ref[...], rest_ref[...])
    scanned = inner_ref[...] + carried * decay
    x_now = x_ref[...].astype(F32)
    mixed = (scanned + skip_ref[...] * x_now).astype(BF16).astype(F32)
    gate = gate_ref[...].astype(F32)
    sig = jax.nn.sigmoid(gate)
    act = gate * sig
    product = mixed * act
    scale = lax.rsqrt(jnp.mean(product * product, axis=-1, keepdims=True) + EPS)
    gain = gain_ref[...]
    unit = product * scale
    gated_ref[...] = (unit * gain).astype(BF16)
    d_gated = dgated_ref[...]
    dgain_ref[...] += jnp.sum(d_gated * unit, axis=0, keepdims=True)
    d_unit = d_gated * gain
    d_product = scale * (d_unit - unit * jnp.mean(d_unit * unit, axis=-1, keepdims=True))
    d_mixed_b = (d_product * act).astype(BF16)
    d_mixed = d_mixed_b.astype(F32)
    dmixed_ref[...] = d_mixed_b
    dgate_ref[...] = (d_product * mixed * (sig + act * (1.0 - sig))).astype(BF16)
    dskip_ref[...] += jnp.sum(d_mixed * x_now, axis=0, keepdims=True)
    high, low = halves(decay * d_mixed)
    dstate_ref[...] += across_rows(c_ref[...], high) + across_rows(c_ref[...], low)
    high, low = halves(d_mixed * scanned)
    rowsum_ref[...] = plain_dot(high, fold_ref[...]) + plain_dot(low, fold_ref[...])


def middle(inner, x_rows, gate, d_gated, c_rows, state, rest, decay, spread, fold, skip, gain, row_block):
    rows, width = x_rows.shape
    states, heads = c_rows.shape[1], fold.shape[1]
    blocked = lambda cols: pl.BlockSpec((row_block, cols), lambda i: (i, 0))
    whole = lambda array: pl.BlockSpec(array.shape, lambda i: (0, 0))
    kept = lambda *shape: pl.BlockSpec(shape, lambda i: (0, 0))
    return pl.pallas_call(
        middle_kernel,
        out_shape=(
            jax.ShapeDtypeStruct((rows, width), BF16),
            jax.ShapeDtypeStruct((rows, width), BF16),
            jax.ShapeDtypeStruct((rows, width), BF16),
            jax.ShapeDtypeStruct((states, width), F32),
            jax.ShapeDtypeStruct((rows, heads), F32),
            jax.ShapeDtypeStruct((1, width), F32),
            jax.ShapeDtypeStruct((1, width), F32),
        ),
        grid=(rows // row_block,),
        in_specs=[
            blocked(width),
            blocked(width),
            blocked(width),
            blocked(width),
            blocked(states),
            whole(state),
            whole(rest),
            blocked(decay.shape[1]),
            whole(spread),
            whole(fold),
            whole(skip),
            whole(gain),
        ],
        out_specs=(
            blocked(width),
            blocked(width),
            blocked(width),
            kept(states, width),
            blocked(heads),
            kept(1, width),
            kept(1, width),
        ),
        name="middle",
    )(inner, x_rows, gate, d_gated, c_rows, state, rest, decay, spread, fold, skip, gain)


def inner_grad_kernel(
    head_width,
    x_ref,
    dy_ref,
    b_ref,
    c_ref,
    decay_ref,
    source_ref,
    grown_ref,
    state_ref,
    dx_ref,
    dmeet_ref,
    dc_ref,
    meet_ref,
):
    rows = x_ref.shape[0]
    tiles = rows // LANES
    per_tile = LANES // head_width

    @pl.when(pl.program_id(0) == 0)
    def _():
        meet_ref[...] = against_cols(b_ref[...], c_ref[...])
        dmeet_ref[...] = jnp.zeros_like(dmeet_ref)
        dc_ref[...] = jnp.zeros_like(dc_ref)

    source_cols = source_ref[...].T
    grown_cols = grown_ref[...].T
    for early in range(tiles):
        in_rows = slice(early * LANES, (early + 1) * LANES)
        for late in range(early, tiles):
            out_rows = slice(late * LANES, (late + 1) * LANES)
            meet = meet_ref[in_rows, out_rows]
            total = dmeet_ref[in_rows, out_rows]
            for head in range(GROUP):
                lanes = slice(head * head_width, (head + 1) * head_width)
                weight = tile_exponent(
                    decay_ref[head : head + 1, out_rows],
                    source_cols[in_rows, head : head + 1],
                    early == late,
                    True,
                )
                dy = dy_ref[out_rows, lanes]
                high, low = halves(meet * weight)
                part = plain_dot(high, dy) + plain_dot(low, dy)
                if late == early:
                    dx_ref[in_rows, lanes] = part
                else:
                    dx_ref[in_rows, lanes] += part
                total = total + against_cols(x_ref[in_rows, lanes], dy) * weight
            dmeet_ref[in_rows, out_rows] = total
    for tile in range(x_ref.shape[1] // LANES):
        lanes = slice(tile * LANES, (tile + 1) * LANES)
        spread = per_head_lanes(grown_cols, tile * per_tile, head_width, rows)
        scaled = (dy_ref[:, lanes].astype(F32) * spread).astype(BF16)
        dc_ref[...] += against_cols(scaled, state_ref[:, lanes])


def inner_grad(x_rows, dy, b_rows, c_rows, decay, source, grown, state, head_width):
    rows, width = x_rows.shape
    states = b_rows.shape[1]
    block = GROUP * head_width
    group_rows = pl.BlockSpec((GROUP, rows), lambda g: (g, 0))
    return pl.pallas_call(
        functools.partial(inner_grad_kernel, head_width),
        out_shape=(
            jax.ShapeDtypeStruct((rows, width), F32),
            jax.ShapeDtypeStruct((rows, rows), F32),
            jax.ShapeDtypeStruct((rows, states), F32),
        ),
        grid=(width // block,),
        in_specs=[
            pl.BlockSpec((rows, block), lambda g: (0, g)),
            pl.BlockSpec((rows, block), lambda g: (0, g)),
            pl.BlockSpec((rows, states), lambda g: (0, 0)),
            pl.BlockSpec((rows, states), lambda g: (0, 0)),
            group_rows,
            group_rows,
            group_rows,
            pl.BlockSpec((states, block), lambda g: (0, g)),
        ],
        out_specs=(
            pl.BlockSpec((rows, block), lambda g: (0, g)),
            pl.BlockSpec((rows, rows), lambda g: (0, 0)),
            pl.BlockSpec((rows, states), lambda g: (0, 0)),
        ),
        scratch_shapes=[pltpu.VMEM((rows, rows), F32)],
        name="inner_grad",
    )(x_rows, dy, b_rows, c_rows, decay, source, grown, state)


def outer_grad_kernel(
    inner_ref,
    x_ref,
    dy_ref,
    b_ref,
    dstate_ref,
    toend_ref,
    spread_ref,
    fold_ref,
    skip_ref,
    dx_ref,
    colsum_ref,
    endsum_ref,
    db_ref,
):
    to_end = plain_dot(toend_ref[...], spread_ref[...])
    x_now = x_ref[...].astype(F32)
    through = to_end * plain_dot(b_ref[...], dstate_ref[...])
    d_scanned = inner_ref[...] + through
    dx_ref[...] = (d_scanned + skip_ref[...] * dy_ref[...].astype(F32)).astype(BF16)
    fold = fold_ref[...]
    high, low = halves(x_now * d_scanned)
    colsum_ref[...] = plain_dot(high, fold) + plain_dot(low, fold)
    high, low = halves(x_now * through)
    endsum_ref[...] = plain_dot(high, fold) + plain_dot(low, fold)
    db_ref[...] = against_cols((to_end * x_now).astype(BF16), dstate_ref[...])


def outer_grad(inner, x_rows, dy, b_rows, dstate, to_end, spread, fold, skip, row_block):
    rows, width = x_rows.shape
    states, heads = b_rows.shape[1], fold.shape[1]
    blocked = lambda cols: pl.BlockSpec((row_block, cols), lambda i: (i, 0))
    whole = lambda array: pl.BlockSpec(array.shape, lambda i: (0, 0))
    return pl.pallas_call(
        outer_grad_kernel,
        out_shape=(
            jax.ShapeDtypeStruct((rows, width), BF16),
            jax.ShapeDtypeStruct((rows, heads), F32),
            jax.ShapeDtypeStruct((rows, heads), F32),
            jax.ShapeDtypeStruct((rows, states), F32),
        ),
        grid=(rows // row_block,),
        in_specs=[
            blocked(width),
            blocked(width),
            blocked(width),
            blocked(states),
            whole(dstate),
            blocked(to_end.shape[1]),
            whole(spread),
            whole(fold),
            whole(skip),
        ],
        out_specs=(blocked(width), blocked(heads), blocked(heads), blocked(states)),
        name="outer_grad",
    )(inner, x_rows, dy, b_rows, dstate, to_end, spread, fold, skip)


def passed_along(value, axis, steps):
    count = lax.axis_size(axis)
    first, last = (max(0, -steps), min(count, count - steps))
    return lax.ppermute(value, axis, [(source, source + steps) for source in range(first, last)])


def three_parts(values):
    first = rounded(values)
    second = rounded(values - first)
    return first.astype(BF16), second.astype(BF16), (values - first - second).astype(BF16)


def carried_states(local, log_total, axis, backward, beside=None):
    count = lax.axis_size(axis)
    states, width = local.shape
    part = width // count
    wire = BF16 if backward or not WIDE else F32
    logs = three_parts(log_total) if wire == BF16 else (log_total,)
    packed = jnp.concatenate([local.astype(wire), *(p[None] for p in logs)], 0)
    split = packed.reshape(packed.shape[0], count, part).transpose(1, 0, 2)
    held = lax.all_to_all(split, axis, split_axis=0, concat_axis=0, tiled=True)
    if beside is not None:
        held = after(held, beside)
    own = held[:, :states].astype(F32)
    logs = jnp.sum(held[:, states:].astype(F32), axis=1)
    decay = jnp.exp(logs)
    order = range(count - 1, -1, -1) if backward else range(count)
    running = jnp.zeros((states, part), F32)
    entering = [None] * count
    for device in order:
        entering[device] = running.astype(wire)
        running = running * decay[device][None, :] + own[device]
    home = lax.all_to_all(jnp.stack(entering), axis, split_axis=0, concat_axis=0, tiled=True)
    return home


def joined(home):
    count, states, part = home.shape
    return home.transpose(1, 0, 2).reshape(states, count * part)


def swapped(value, axis, mask):
    count = lax.axis_size(axis)
    return lax.ppermute(value, axis, [(source, source ^ mask) for source in range(count)])


def flip_order(count):
    order = [0]
    mask = count // 2
    while mask:
        order += [flip ^ mask for flip in order]
        mask //= 2
    return order


def gathered(value, axis):
    first = []
    mask = lax.axis_size(axis) // 2
    while mask:
        first.append(swapped(value, axis, mask))
        mask //= 2
    return value, first


def passed_on(started, axis, held_for=None):
    value, first = started
    if held_for is not None:
        first = after(first, held_for)
    blocks = [value]
    mask = lax.axis_size(axis) // 2
    for arrived in first:
        blocks += [arrived] + [swapped(block, axis, mask) for block in blocks[1:]]
        mask //= 2
    return blocks


def after(value, earlier):
    return lax.optimization_barrier((value, earlier))[0]


def weight_parts(shard, side):
    place = lax.axis_index(side) % 2
    rows = shard.shape[0]
    third = rows // 3 // 16 * 16
    alone = rows - 2 * third
    return (alone + place * third, 0, alone + (1 - place) * third), (third, alone, third)


def weight_sent(shard, axis, side):
    offsets, sizes = weight_parts(shard, side)
    shared, own = (
        lax.dynamic_slice_in_dim(shard, o, n, 0) for o, n in zip(offsets[:2], sizes[:2])
    )
    mask = lax.axis_size(axis) // 2
    if mask == 1:
        return (swapped(shard, axis, 1),)
    arrived = swapped(shared, axis, mask)
    return swapped(shard, axis, 1), arrived, swapped(own, axis, mask)


def weight_gathered(shard, sent, axis, side):
    count, rank = lax.axis_size(axis), lax.axis_index(axis)
    rows = shard.shape[0]
    offsets, sizes = weight_parts(shard, side)
    held = {0: tuple(lax.dynamic_slice_in_dim(shard, o, n, 0) for o, n in zip(offsets, sizes))}
    whole = jnp.zeros((count * rows, shard.shape[1]), shard.dtype)
    mask = count // 2
    while mask > 1:
        for flip, (shared, own, _) in tuple(held.items()):
            if flip or mask < count // 2:
                arrived, direct = swapped(shared, axis, mask), swapped(own, axis, mask)
            else:
                arrived, direct = sent[1:]
            held[flip ^ mask] = (arrived, direct, swapped(arrived, side, 1))
        mask //= 2
    for flip, block in ((0, shard), (1, sent[0])):
        whole = lax.dynamic_update_slice_in_dim(whole, block, (rank ^ flip) * rows, 0)
    for flip, blocks in held.items():
        if flip:
            for block, offset in zip(blocks, offsets):
                start = (rank ^ flip) * rows + offset
                whole = lax.dynamic_update_slice_in_dim(whole, block, start, 0)
                start = (rank ^ flip ^ 1) * rows + offset
                whole = lax.dynamic_update_slice_in_dim(whole, swapped(block, axis, 1), start, 0)
    return whole


def exchanged(value, axis):
    count, rank = lax.axis_size(axis), lax.axis_index(axis)
    part = value.shape[1] // count
    blocks = []
    for flip in flip_order(count):
        piece = lax.dynamic_slice_in_dim(value, (rank ^ flip) * part, part, 1)
        blocks.append(swapped(piece, axis, flip) if flip else piece)
    return blocks


def product_kernel(place_ref, *refs):
    count = (len(refs) - 3) // 2
    left_refs, right_refs = refs[:count], refs[count : 2 * count]
    near_ref, away_ref, turned_ref = refs[2 * count :]
    tokens = left_refs[0].shape[0]

    @pl.when(pl.program_id(0) == 0)
    def _():
        for index, left_ref in enumerate(left_refs):
            turned_ref[:, index * tokens : (index + 1) * tokens] = left_ref[...].T

    half = near_ref.shape[0]
    for upper in range(2):
        rows = slice(upper * half, (upper + 1) * half)
        total = None
        for index, right_ref in enumerate(right_refs):
            part = plain_dot(
                turned_ref[rows, index * tokens : (index + 1) * tokens], right_ref[...]
            )
            total = part if total is None else total + part

        @pl.when(place_ref[0] == upper)
        def _():
            near_ref[...] = total

        @pl.when(place_ref[0] != upper)
        def _():
            away_ref[...] = total.astype(BF16)


def weight_product(lefts, rights, axis):
    place = (lax.axis_index(axis) % 2).astype(jnp.int32).reshape(1)
    tokens, rows = lefts[0].shape
    width = rights[0].shape[1]
    block = 512
    return pl.pallas_call(
        product_kernel,
        out_shape=(
            jax.ShapeDtypeStruct((rows // 2, width), F32),
            jax.ShapeDtypeStruct((rows // 2, width), BF16),
        ),
        grid_spec=pltpu.PrefetchScalarGridSpec(
            num_scalar_prefetch=1,
            grid=(pl.cdiv(width, block),),
            in_specs=[pl.BlockSpec((tokens, rows), lambda i, place: (0, 0)) for _ in lefts]
            + [pl.BlockSpec((tokens, block), lambda i, place: (0, i)) for _ in rights],
            out_specs=tuple(
                pl.BlockSpec((rows // 2, block), lambda i, place: (0, i)) for _ in range(2)
            ),
            scratch_shapes=[pltpu.VMEM((rows, tokens * len(lefts)), BF16)],
        ),
        name="weight_product",
    )(place, *lefts, *rights)


def seq_owned(near, arrived, axis):
    count, rank = lax.axis_size(axis), lax.axis_index(axis)
    line = rank // 2
    block = near.shape[0] // (count // 2)
    pair = near + arrived.astype(F32)
    total = lax.dynamic_slice_in_dim(pair, line * block, block, 0)
    for flip in range(1, count // 2):
        piece = lax.dynamic_slice_in_dim(pair, (line ^ flip) * block, block, 0).astype(BF16)
        total = total + swapped(piece, axis, 2 * flip).astype(F32)
    return total.astype(BF16)


def seq_spread(owned, axis):
    count = lax.axis_size(axis)
    blocks = [owned] + [swapped(owned, axis, 2 * flip) for flip in range(1, count // 2)]
    mine = jnp.stack(blocks)
    return mine, swapped(mine, axis, 1)


def place_kernel(ranks_ref, *refs):
    out_ref = refs[-1]
    count = pl.num_programs(0)
    mine = pl.program_id(0) // (count // 2) == ranks_ref[0]
    cursor = 0
    for pair in range(len(refs) // 2):
        near_ref, far_ref = refs[2 * pair], refs[2 * pair + 1]
        width = min(near_ref.shape[2], out_ref.shape[-1] - cursor)

        @pl.when(mine)
        def _():
            out_ref[..., cursor : cursor + width] = near_ref[:, :, :width].astype(F32).reshape(
                (*out_ref.shape[:-1], width)
            )

        @pl.when(jnp.logical_not(mine))
        def _():
            out_ref[..., cursor : cursor + width] = far_ref[:, :, :width].astype(F32).reshape(
                (*out_ref.shape[:-1], width)
            )

        cursor += width


def placed(spreads, axis, width):
    count, rank = lax.axis_size(axis), lax.axis_index(axis)
    ranks = jnp.stack([rank % 2, rank // 2]).astype(jnp.int32)
    flat = [array for pair in spreads for array in pair]
    rows = flat[0].shape[1]
    pick = lambda i, ranks: ((i % (count // 2)) ^ ranks[1], 0, 0)
    if rows % 8:
        shape, out_spec = (count, rows, width), pl.BlockSpec((1, rows, width), lambda i, r: (i, 0, 0))
    else:
        shape, out_spec = (count * rows, width), pl.BlockSpec((rows, width), lambda i, r: (i, 0))
    out = pl.pallas_call(
        place_kernel,
        out_shape=jax.ShapeDtypeStruct(shape, F32),
        grid_spec=pltpu.PrefetchScalarGridSpec(
            num_scalar_prefetch=1,
            grid=(count,),
            in_specs=[pl.BlockSpec((1, rows, a.shape[2]), pick) for a in flat],
            out_specs=out_spec,
        ),
        name="placed",
    )(ranks, *flat)
    return out.reshape(count * rows, width)


def turned_kernel(ranks_ref, near_a_ref, far_a_ref, near_b_ref, far_b_ref, out_ref, held_ref):
    line, rows = near_a_ref.shape[0], near_a_ref.shape[1]

    def fill(near_ref, far_ref):
        for index in range(2 * line):
            source = (index % line) ^ ranks_ref[1]
            mine = ranks_ref[0] == index // line
            block = jnp.where(mine, near_ref[source].astype(F32), far_ref[source].astype(F32))
            held_ref[index * rows : (index + 1) * rows, :] = block

    first = pl.program_id(0) < ranks_ref[2]

    @pl.when(first)
    def _():
        fill(near_a_ref, far_a_ref)

    @pl.when(jnp.logical_not(first))
    def _():
        fill(near_b_ref, far_b_ref)

    out_ref[...] = held_ref[...].T


def placed_turned(first, second, axis, width):
    count, rank = lax.axis_size(axis), lax.axis_index(axis)
    rows, columns = first[0].shape[1:]
    block = next(b for b in (512, 256, 128) if columns % b == 0)
    ahead = columns // block
    ranks = jnp.stack([rank % 2, rank // 2, ahead]).astype(jnp.int32)
    shape = (count // 2, rows, block)
    first_spec = pl.BlockSpec(shape, lambda j, r: (0, 0, jnp.minimum(j, ahead - 1)))
    second_spec = pl.BlockSpec(shape, lambda j, r: (0, 0, jnp.maximum(j - ahead, 0)))
    return pl.pallas_call(
        turned_kernel,
        out_shape=jax.ShapeDtypeStruct((width, count * rows), F32),
        grid_spec=pltpu.PrefetchScalarGridSpec(
            num_scalar_prefetch=1,
            grid=(pl.cdiv(width, block),),
            in_specs=[first_spec, first_spec, second_spec, second_spec],
            out_specs=pl.BlockSpec((block, count * rows), lambda j, r: (j, 0)),
            scratch_shapes=[pltpu.VMEM((count * rows, block), F32)],
        ),
        name="placed_turned",
    )(ranks, *first, *second).T


def small_total(packed, split_axis, axis):
    count, rank = lax.axis_size(split_axis), lax.axis_index(split_axis)
    total = None
    for flip in flip_order(count):
        row = lax.dynamic_slice_in_dim(packed, rank ^ flip, 1, 0)
        row = swapped(row, split_axis, flip) if flip else row
        total = row if total is None else total + row
    mask = lax.axis_size(axis) // 2
    while mask:
        total = total + swapped(total, axis, mask)
        mask //= 2
    return total[0]


def body(
    hidden,
    cotangent,
    norm_gain,
    in_weight,
    conv_weight,
    conv_bias,
    dt_bias,
    a_log,
    skip_d,
    inner_gain,
    out_weight,
):
    owner_count = lax.axis_size("fsdp")
    taps = conv_weight.shape[1]
    model = hidden.shape[2]
    inner_width = inner_gain.shape[0] * owner_count
    heads = a_log.shape[0] * owner_count
    conv_width = conv_bias.shape[0] * owner_count
    states = (conv_width - inner_width) // 2
    head_width = inner_width // heads
    tokens = hidden.shape[1]
    row_block = 64

    small = jnp.concatenate(
        [
            norm_gain,
            inner_gain,
            conv_bias,
            conv_weight.T.reshape(-1),
            dt_bias,
            a_log,
            skip_d,
        ]
    )
    small = jnp.pad(small, (0, -small.shape[0] % LANES))
    small_held = jnp.stack(
        [swapped(small, "fsdp", flip) if flip else small for flip in range(owner_count)]
    )
    owner_rank = lax.axis_index("fsdp")
    small_all = jnp.concatenate(
        [
            lax.dynamic_slice_in_dim(small_held, owner_rank ^ owner, 1, 0)
            for owner in range(owner_count)
        ],
        0,
    )
    conv_shard, gate_shard = in_weight[:, inner_width:], in_weight[:, :inner_width]
    conv_sent = weight_sent(conv_shard, "fsdp", "seq")
    gate_sent = weight_sent(gate_shard, "fsdp", "seq")
    out_sent = weight_sent(out_weight, "fsdp", "seq")
    w_conv_in = weight_gathered(conv_shard, conv_sent, "fsdp", "seq")

    cursor = 0
    pieces = []
    for piece in (norm_gain, inner_gain, conv_bias, conv_weight, dt_bias, a_log, skip_d):
        pieces.append(small_all[:, cursor : cursor + piece.size].astype(F32))
        cursor += piece.size
    gain_n, gain_i, b_conv = (p.reshape(-1) for p in pieces[:3])
    w_taps = pieces[3].reshape(owner_count, taps, -1).transpose(1, 0, 2).reshape(taps, conv_width)
    bias_dt, log_a, skip_vec = (p.reshape(-1) for p in pieces[4:])

    hidden_f = hidden[0].astype(F32)
    cot_rows = cotangent[0]
    n_scale = lax.rsqrt(jnp.mean(hidden_f * hidden_f, axis=-1, keepdims=True) + EPS)
    n_unit = hidden_f * n_scale
    normed_b = (n_unit * gain_n).astype(BF16)

    stepped = plain_dot(normed_b, w_conv_in).astype(BF16)
    conv_in = stepped[:, :conv_width]
    raw_t = stepped[:, conv_width:].T.astype(F32)
    rim_rows = passed_along(conv_in[tokens - taps + 1 :], "seq", 1)
    gate_sent = after(gate_sent, rim_rows)
    w_gate = weight_gathered(gate_shard, gate_sent, "fsdp", "seq")
    padded = jnp.concatenate([rim_rows, conv_in], 0).astype(F32)
    pre_act = b_conv[None, :]
    for tap in range(taps):
        pre_act = pre_act + padded[tap : tap + tokens] * w_taps[tap]
    conv_act = jax.nn.silu(pre_act).astype(BF16)
    x_rows = conv_act[:, :inner_width]
    b_rows = conv_act[:, inner_width : inner_width + states]
    c_rows = conv_act[:, inner_width + states :]

    rate = -jnp.exp(log_a)[:, None]
    pre_step = raw_t + bias_dt[:, None]
    step = jax.nn.softplus(pre_step)
    ahead = jnp.triu(jnp.ones((tokens, tokens), F32))
    decay_log = jnp.dot(step * rate, ahead, precision=HIGHEST)
    source_log = decay_log - jnp.log(step)
    total_log = decay_log[:, -1]
    to_end = jnp.exp(total_log[:, None] - decay_log) * step
    grown = jnp.exp(decay_log)
    lane_head = jnp.arange(inner_width) // head_width
    one_hot = (jnp.arange(heads)[:, None] == lane_head[None, :]).astype(BF16)
    spread = jnp.concatenate([one_hot, one_hot], 0)
    fold = one_hot.T
    skip_lanes = jnp.repeat(skip_vec, head_width)[None, :]
    total_lanes = jnp.repeat(total_log, head_width)

    own_state = local_state(x_rows, b_rows.T, to_end, head_width)
    state_full = joined(carried_states(own_state, total_lanes, "seq", False))
    state_in = host_halves(state_full)
    inner = inner_part(after(x_rows, own_state), b_rows, c_rows, decay_log, source_log, head_width)
    out_sent = after(out_sent, inner)
    w_out = weight_gathered(out_weight, out_sent, "fsdp", "seq")
    sent = out_sent[-1]
    gate_in = plain_dot(normed_b, w_gate).astype(BF16)
    d_gated = against_cols(cot_rows, w_out)

    gated_b, d_mixed, d_gate, own_dstate, rowsum, grad_gain_i, skip_sums = middle(
        inner,
        x_rows,
        gate_in,
        d_gated,
        c_rows,
        *state_in,
        jnp.concatenate(host_halves(grown.T), 1),
        spread,
        fold,
        skip_lanes,
        gain_i[None, :],
        row_block,
    )
    normed_all = exchanged(after(normed_b, sent), "fsdp")
    cot_all = gathered(after(cot_rows, sent), "fsdp")
    gated_all = exchanged(gated_b, "fsdp")
    d_gate_all = gathered(d_gate, "fsdp")
    inner_dx, d_meet, dc_carried = inner_grad(
        x_rows, d_mixed, b_rows, c_rows, decay_log, source_log, grown, state_in[0], head_width
    )
    home = carried_states(own_dstate, total_lanes, "seq", True, inner_dx)
    cot_all = passed_on(cot_all, "fsdp")
    out_near, out_away = weight_product(gated_all, cot_all, "seq")
    out_arrived = swapped(out_away, "seq", 1)
    dstate = joined(after(home, out_near))
    d_x, colsum, endsum, db_carried = outer_grad(
        inner_dx,
        x_rows,
        d_mixed,
        b_rows,
        dstate,
        jnp.concatenate(host_halves(to_end.T), 1),
        spread,
        fold,
        skip_lanes,
        row_block,
    )
    d_gate_all = passed_on(d_gate_all, "fsdp", d_x)
    gate_near, gate_away = weight_product(normed_all, d_gate_all, "seq")
    gate_arrived = swapped(gate_away, "seq", 1)
    d_x = after(d_x, gate_near)
    d_meet_b = d_meet.astype(BF16)
    d_b = db_carried + plain_dot(d_meet_b, c_rows)
    d_c = dc_carried + across_rows(d_meet_b, b_rows)
    ends = jnp.sum(state_full * dstate.astype(F32), axis=0)
    ends = jnp.sum(ends.reshape(heads, head_width), axis=1) * jnp.exp(total_log)
    colsum_t = colsum.T
    d_log = rowsum.T - colsum_t
    d_last = jnp.sum(endsum, axis=0) + ends
    behind = jnp.tril(jnp.ones((tokens, tokens), F32))
    d_rate_step = jnp.dot(d_log, behind, precision=HIGHEST) + d_last[:, None]
    sig_step = jax.nn.sigmoid(pre_step)
    ratio = jnp.where(step > 0, sig_step / jnp.where(step > 0, step, 1.0), 0.0)
    d_raw = colsum_t * ratio + d_rate_step * rate * sig_step
    grad_log = jnp.sum(d_rate_step * step, axis=1) * rate[:, 0]
    grad_bias = jnp.sum(d_raw, axis=1)
    grad_skip = jnp.sum(skip_sums.reshape(heads, head_width), axis=1)

    d_conv = jnp.concatenate([d_x.astype(F32), d_b, d_c], 1)
    act_sig = jax.nn.sigmoid(pre_act)
    d_pre = d_conv * (act_sig * (1.0 + pre_act * (1.0 - act_sig)))
    after_rows = passed_along(d_pre[: taps - 1], "seq", -1)
    d_tail = jnp.concatenate([d_pre, after_rows], 0)
    d_conv_in = 0.0
    for tap in range(taps):
        shift = taps - 1 - tap
        d_conv_in = d_conv_in + d_tail[shift : shift + tokens] * w_taps[tap]
    spare = jnp.zeros((tokens, -(conv_width + heads) % LANES), BF16)
    d_step_proj = jnp.concatenate([d_conv_in.astype(BF16), d_raw.T.astype(BF16), spare], 1)
    d_step_all = passed_on(gathered(d_step_proj, "fsdp"), "fsdp")
    out_arrived = after(out_arrived, gate_near)
    out_spread = seq_spread(seq_owned(out_near, out_arrived, "seq"), "seq")
    gate_arrived = after(gate_arrived, d_step_proj)
    gate_spread = seq_spread(seq_owned(gate_near, gate_arrived, "seq"), "seq")
    step_near, step_away = weight_product(normed_all, d_step_all, "seq")
    step_arrived = swapped(step_away, "seq", 1)
    step_arrived = after(step_arrived, (gate_spread[0], out_spread[0]))
    step_spread = seq_spread(seq_owned(step_near, step_arrived, "seq"), "seq")
    d_pre = after(d_pre, d_step_proj)
    grad_w_conv = jnp.stack(
        [jnp.sum(d_pre * padded[tap : tap + tokens], axis=0) for tap in range(taps)]
    )
    grad_b_conv = jnp.sum(d_pre, axis=0)
    block_out = hidden_f + plain_dot(after(gated_b, d_step_proj), w_out)
    d_normed = against_cols(after(d_gate, d_step_proj), w_gate)
    d_normed = d_normed + against_cols(d_step_proj[:, : conv_width + heads], w_conv_in)
    d_unit = d_normed * gain_n
    d_hidden = n_scale * (d_unit - n_unit * jnp.mean(d_unit * n_unit, axis=-1, keepdims=True))
    grad_hidden = cot_rows.astype(F32) + d_hidden
    grad_gain_n = jnp.sum(d_normed * n_unit, axis=0)

    parts = (
        grad_gain_n,
        grad_gain_i[0],
        grad_b_conv,
        grad_bias,
        grad_log,
        grad_skip,
    )
    by_owner = [p.reshape(owner_count, -1) for p in parts]
    tap_part = grad_w_conv.reshape(taps, owner_count, -1).transpose(1, 0, 2)
    by_owner.append(tap_part.reshape(owner_count, -1))
    mine = small_total(jnp.concatenate(by_owner, 1), "fsdp", "seq")
    outs = []
    cursor = 0
    for part in by_owner:
        outs.append(mine[cursor : cursor + part.shape[1]])
        cursor += part.shape[1]
    return (
        block_out[None],
        grad_hidden[None],
        outs[0],
        placed_turned(gate_spread, step_spread, "seq", in_weight.shape[1]),
        outs[6].reshape(taps, -1).T,
        outs[2],
        outs[3],
        outs[4],
        outs[5],
        outs[1],
        placed((out_spread,), "seq", model),
    )


def solution(mesh):
    rows = P("fsdp", "seq", None)
    vector, matrix = P("fsdp"), P("fsdp", None)
    params = (vector, matrix, matrix, vector, vector, vector, vector, vector, matrix)
    return jax.shard_map(
        body,
        mesh=mesh,
        in_specs=(rows, rows, *params),
        out_specs=(rows, rows, *params),
        check_vma=False,
    )
```

time: 2520 us -> 739 us (0.29)
  waiting for transfers between devices: 1620 us -> 261 us
  local copies, waits for them, and re-layouts: 400 us -> 139 us
  matrix products: 220 us -> 54.1 us
  Pallas kernels: 0 us -> 95.9 us
  other arithmetic: 157 us -> 72.6 us
  starting transfers between devices: 27.7 us -> 101 us
  blocking collectives: 72.7 us -> 0 us
    unnamed x7 -> x0, waiting for transfers between devices: 964 us -> none
    psum x1 -> x0, waiting for transfers between devices: 402 us -> none  [body(): summed = lax.psum((owned[0], owned[1], owned[2]), 'seq')]
    ppermute x0 -> x69, waiting for transfers between devices: none -> 239 us  [swapped(): lax.ppermute(value, axis, [(source, source ^ mask) for source in range(co...]
    unnamed x72 -> x107, local copies, waits for them, and re-layouts: 230 us -> 5.36 us
    all_gather x3 -> x0, waiting for transfers between devices: 157 us -> none  [the longest x1 117 us: body(): lax.all_gather(in_weight, 'fsdp', axis=0, tiled=True)]
    dot_general x102 -> x10, matrix products: 205 us -> 54.1 us  [the longest x8 51.5 us: dims(): lax.dot_general(left, right, (contract, ((), ())), preferred_element_type...]
    pallas_call x0 -> x10, Pallas kernels: none -> 95.9 us  [the longest x3 26.4 us: weight_product(): pl.pallas_call(product_kernel, out_shape=(jax.ShapeDtypeStruct((rows // 2...]
    another operation x81 -> x7, other arithmetic: 97.1 us -> 4.56 us  [the longest x1 1.65 us: carried_states(): jnp.stack(entering)]
  transfers between devices with their start and end apart: 13 -> 75, of which waited for: 8 -> 24; matrix products, arithmetic and copies ran while one was open for 7% -> 35% of each run, Pallas kernels for 0% -> 10%
where the time goes in v1:
time: 739 us; the launch traced here: 727 us
  waiting for transfers between devices  261 us (35%)
  local copies, waits for them, and re-layouts  139 us (19%)
  starting transfers between devices  101 us (14%)
  Pallas kernels  95.9 us (13%)
  other arithmetic  72.6 us (10%)
  matrix products  54.1 us (7%)
    ppermute x69, waiting for transfers between devices, swapped(): lax.ppermute(value, axis, [(source, source ^ mask) for source in range(co...  239 us
    ppermute x69, starting transfers between devices, swapped(): lax.ppermute(value, axis, [(source, source ^ mask) for source in range(co...  78.4 us
    dot_general x8, matrix products, dims(): lax.dot_general(left, right, (contract, ((), ())), preferred_element_type...  51.5 us
    pallas_call x3, Pallas kernels, weight_product(): pl.pallas_call(product_kernel, out_shape=(jax.ShapeDtypeStruct((rows // 2...  26.4 us
    dynamic_update_slice x9, local copies, waits for them, and re-layouts, weight_gathered(): whole = lax.dynamic_update_slice_in_dim(whole, block, start, 0)  18.2 us
  transfers between devices with their start and end apart: 75, of which 24 were waited for; matrix products, arithmetic and copies ran while one was open for 35% of the time, Pallas kernels for 10%

profile of v1, /device:TPU:0, one launch (start us, length us, event | category | flops | bytes accessed | tf_op | source)
XLA Modules:
  0.0 726.7 jit_solution(11201263525230263069)
XLA Ops:
  1.4 4.1 concatenate.48
  12.4 4.8 broadcast_in_dim.48
  17.2 5.3 fusion.84
  33.3 4.3 broadcast_in_dim.49
  61.1 7.7 %collective-permute-done.4 = bf16[128,3376]{0,1:T(8,128)(2,1)} collective-permute-done((bf16[128,3376]{0,1:T(8,128)(2,1)}, bf16[128,3376]{0,1:T(8,128)(2,1)}, u32[]{:S(2)}, u32[]{:S(2)}) %collective-permute-start.4) | collective-permute-done | bytes 864288 | tf_op jit(solution)/shard_map/ppermute | solution.py:440
  76.5 10.9 %collective-permute-done.6 = bf16[128,3376]{0,1:T(8,128)(2,1)} collective-permute-done((bf16[128,3376]{0,1:T(8,128)(2,1)}, bf16[128,3376]{0,1:T(8,128)(2,1)}, u32[]{:S(2)}, u32[]{:S(2)}) %collective-permute-start.6) | collective-permute-done | bytes 864288 | tf_op jit(solution)/shard_map/ppermute | solution.py:440
  93.9 13.9 %collective-permute-done.8 = bf16[128,3376]{0,1:T(8,128)(2,1)S(1)} collective-permute-done((bf16[128,3376]{0,1:T(8,128)(2,1)}, bf16[128,3376]{0,1:T(8,128)(2,1)S(1)}, u32[]{:S(2)}, u32[]{:S(2)}) %collective-permute-start.8) | collective-permute-done | bytes 864288 | tf_op jit(solution)/shard_map/ppermute | solution.py:440
  111.3 7.0 convolution_convert_fusion
  142.4 7.0 local_state.1
  149.4 8.6 %inner_part.1.inner_ref = f32[256,3072]{1,0:T(8,128)} custom-call(bf16[256,3072]{1,0:T(8,128)(2,1)} %slice.333.x_ref, bf16[256,128]{1,0:T(8,128)(2,1)} %get-tuple-element.151.b_ref, bf16[256,128]{1,0:T(8,128)(2,1)} %get-tuple-element.149.c_ref, f32[48,256]{1,0:T(8,128)} %copy-done.24, f32[48,256]{1,0:T(8,128)} %copy.101.source_ref), custom_call_target="tpu_custom_call" | custom-call | tf_op jit(solution)/shard_map/inner_part/pallas_call | solution.py:132
  158.0 7.6 %collective-permute-done.20 = bf16[256,1536]{1,0:T(8,128)(2,1)} collective-permute-done((bf16[256,1536]{1,0:T(8,128)(2,1)}, bf16[256,1536]{1,0:T(8,128)(2,1)}, u32[]{:S(2)}, u32[]{:S(2)}) %collective-permute-start.20) | collective-permute-done | bytes 786464 | tf_op jit(solution)/shard_map/ppermute | solution.py:440
  170.2 4.7 all-to-all-start
  186.1 9.3 %collective-permute-done.23 = bf16[256,1536]{1,0:T(8,128)(2,1)} collective-permute-done((bf16[256,1536]{1,0:T(8,128)(2,1)}, bf16[256,1536]{1,0:T(8,128)(2,1)}, u32[]{:S(2)}, u32[]{:S(2)}) %collective-permute-start.23) | collective-permute-done | bytes 786464 | tf_op jit(solution)/shard_map/ppermute | solution.py:440
  206.9 7.7 %all-to-all-done = f32[8,129,384]{2,1,0:T(8,128)} async-done(((f32[8,129,384]{2,1,0:T(8,128)}), f32[8,129,384]{2,1,0:T(8,128)}, u32[]{:S(2)}, u32[]{:S(2)}) %all-to-all-start) | async-done | bytes 1585184 | tf_op jit(solution)/shard_map/all_to_all | solution.py:417
  227.4 4.5 all-to-all-start.1
  240.2 10.9 %convolution_convert_fusion.1.gate_ref = bf16[256,3072]{1,0:T(8,128)(2,1)} fusion(bf16[256,1536]{1,0:T(8,128)(2,1)S(1)} %copy-done.12, bf16[1536,3072]{0,1:T(8,128)(2,1)} %constant_dynamic-update-slice_fusion.11), kind=kOutput, calls=%fused_computation.4 | convolution fusion | flops 2416705536 | bytes 11796480 | tf_op jit(solution)/shard_map/dot_general | solution.py:21
  251.1 8.0 %convolution_bitcast_fusion.dgated_ref = f32[256,3072]{1,0:T(8,128)} fusion(bf16[3072,1536]{1,0:T(8,128)(2,1)} %constant_dynamic-update-slice_fusion.3, bf16[1,256,1536]{2,1,0:T(8,128)(2,1)S(1)} %copy-done.13), kind=kOutput, calls=%fused_computation.3 | convolution fusion | flops 2415919104 | bytes 13369344 | tf_op jit(solution)/shard_map/dot_general | solution.py:21
  259.1 9.4 %all-to-all-done.1 = f32[8,128,384]{2,1,0:T(8,128)} async-done(((f32[8,128,384]{2,1,0:T(8,128)}), f32[8,128,384]{2,1,0:T(8,128)}, u32[]{:S(2)}, u32[]{:S(2)}) %all-to-all-start.1) | async-done | bytes 1572896 | tf_op jit(solution)/shard_map/all_to_all | solution.py:429
  271.6 13.4 %middle.1 = (bf16[256,3072]{1,0:T(8,128)(2,1)}, bf16[256,3072]{1,0:T(8,128)(2,1)}, bf16[256,3072]{1,0:T(8,128)(2,1)}, f32[128,3072]{1,0:T(8,128)}, f32[256,48]{1...) custom-call(f32[256,3072]{1,0:T(8,128)} %inner_part.1.inner_ref, bf16[256,3072]{1,0:T(8,128)(2,1)} %slice.333.x_ref, ...), custom_call_target="tpu_custom_call" | custom-call | tf_op jit(solution)/shard_map/middle/pallas_call | solution.py:210
  287.7 4.2 all-to-all-start.2
  295.4 11.9 %inner_grad.1 = (f32[256,3072]{1,0:T(8,128)}, f32[256,256]{1,0:T(8,128)}, f32[256,128]{1,0:T(8,128)}) custom-call(bf16[256,3072]{1,0:T(8,128)(2,1)} %slice.333.x_ref, bf16[256,3072]{1,0:T(8,128)(2,1)} %get-tuple-element.59.dy_ref, bf16[256,128]{1,0:T(8,128)(2,1)} %get-tuple-element.151.b_ref, bf16[256,128]{1,0:T(8,128)(2,1)} %get-tuple-element.149.c_ref, ...), custom_call_target="tpu_custom_call" | custom-call | tf_op jit(solution)/shard_map/inner_grad/pallas_call | solution.py:311
  307.3 5.7 all-to-all-done.2
  320.5 4.4 all-to-all-start.3
  333.3 23.0 %collective-permute-done.25.refs_1_ = bf16[256,768]{1,0:T(8,128)(2,1)} collective-permute-done((bf16[256,768]{1,0:T(8,128)(2,1)}, bf16[256,768]{1,0:T(8,128)(2,1)}, u32[]{:S(2)}, u32[]{:S(2)}) %collective-permute-start.25) | collective-permute-done | bytes 393248 | tf_op jit(solution)/shard_map/ppermute | solution.py:440
  356.2 5.2 collective-permute-done.27.refs_3_
  361.4 7.4 %weight_product.3 = (f32[384,1536]{1,0:T(8,128)}, bf16[384,1536]{1,0:T(8,128)(2,1)}) custom-call(s32[1]{0:T(128)} %bitcast.13.place_ref, bf16[256,768]{1,0:T(8,128)(2,1)} %get-tuple-element.155.refs_0_, bf16[256,768]{1,0:T(8,128)(2,1)} %collective-permute-done.25.refs_1_, bf16[256,768]{1,0:T(8,128)(2,1)} %collective-permute-done.26.refs_2_, ...), custom_call_target="tpu_custom_call" | custom-call | tf_op jit(solution)/shard_map/weight_product/pallas_call | solution.py:569
  370.9 8.3 %outer_grad.1 = (bf16[256,3072]{1,0:T(8,128)(2,1)}, f32[256,48]{1,0:T(8,128)}, f32[256,48]{1,0:T(8,128)}, f32[256,128]{1,0:T(8,128)}) custom-call(f32[256,3072]{1,0:T(8,128)} %get-tuple-element.60.inner_ref, bf16[256,3072]{1,0:T(8,128)(2,1)} %slice.333.x_ref, bf16[256,3072]{1,0:T(8,128)(2,1)} %get-tuple-element.59.dy_ref, ...), custom_call_target="tpu_custom_call" | custom-call | tf_op jit(solution)/shard_map/outer_grad/pallas_call | solution.py:372
  415.3 8.8 %weight_product.4 = (f32[192,3072]{1,0:T(8,128)}, bf16[192,3072]{1,0:T(8,128)(2,1)}) custom-call(s32[1]{0:T(128)} %bitcast.13.place_ref, bf16[256,384]{1,0:T(8,128)(2,1)} %get-tuple-element.161.refs_0_, bf16[256,384]{1,0:T(8,128)(2,1)} %collective-permute-done.31.refs_1_, bf16[256,384]{1,0:T(8,128)(2,1)} %collective-permute-done.32.refs_2_, ...), custom_call_target="tpu_custom_call" | custom-call | tf_op jit(solution)/shard_map/weight_product/pallas_call | solution.py:569
  442.9 3.8 concatenate.61.refs_4_
  447.9 5.6 fusion.88
  453.6 8.8 %fusion.24 = (f32[1536]{0:T(1024)S(1)}, f32[256]{0:T(256)}, f32[256,1536]{1,0:T(8,128)}) fusion(bf16[1,256,1536]{2,1,0:T(8,128)(2,1)S(1)} %copy-done.5, f32[256]{0:T(256)S(1)} %copy-done.45, f32[1536]{0:T(1024)S(1)} %copy-done.36, f32[256,1536]{1,0:T(8,128)S(1)} %fusion.88, bf16[1536,3376]{0,1:T(8,128)(2,1)} %constant_dynamic-update-slice_fusion.19, ...), kind=kOutput, calls=%fused_computation.49 | convolution fusion | flops 2661595392 | bytes 16046080 | tf_op jit(solution)/shard_map/dot_general | solution.py:21
  463.0 3.9 multiply_reduce_fusion.3
  469.4 17.1 %collective-permute-done.52.refs_5_ = bf16[256,3456]{1,0:T(8,128)(2,1)} collective-permute-done((bf16[256,3456]{1,0:T(8,128)(2,1)}, bf16[256,3456]{1,0:T(8,128)(2,1)}, u32[]{:S(2)}, u32[]{:S(2)}) %collective-permute-start.52) | collective-permute-done | bytes 1769504 | tf_op jit(solution)/shard_map/ppermute | solution.py:440
  499.6 3.7 collective-permute-start.62
  503.3 10.2 %weight_product.5 = (f32[192,3456]{1,0:T(8,128)}, bf16[192,3456]{1,0:T(8,128)(2,1)}) custom-call(s32[1]{0:T(128)} %bitcast.13.place_ref, bf16[256,384]{1,0:T(8,128)(2,1)} %get-tuple-element.161.refs_0_, bf16[256,384]{1,0:T(8,128)(2,1)} %collective-permute-done.31.refs_1_, bf16[256,384]{1,0:T(8,128)(2,1)} %collective-permute-done.32.refs_2_, ...), custom_call_target="tpu_custom_call" | custom-call | tf_op jit(solution)/shard_map/weight_product/pallas_call | solution.py:569
  515.7 18.4 %collective-permute-done.46 = bf16[48,3072]{1,0:T(8,128)(2,1)} collective-permute-done((bf16[48,3072]{1,0:T(8,128)(2,1)}, bf16[48,3072]{1,0:T(8,128)(2,1)}, u32[]{:S(2)}, u32[]{:S(2)}) %collective-permute-start.46) | collective-permute-done | bytes 294944 | tf_op jit(solution)/shard_map/ppermute | solution.py:440
  538.2 12.9 %collective-permute-start.49 = (bf16[48,3072]{1,0:T(8,128)(2,1)S(1)}, bf16[48,3072]{1,0:T(8,128)(2,1)S(1)}, u32[]{:S(2)}, u32[]{:S(2)}) collective-permute-start(bf16[48,3072]{1,0:T(8,128)(2,1)S(1)} %add_convert_fusion.3), channel_id=1, source_target_pairs={{0,16},{4,20},{8,24},{12,28},{16,0},{20,4},{24,8},{28,12},{1,17},{... | collective-permute-start | bytes 884744 | tf_op jit(solution)/shard_map/ppermute | solution.py:440
  551.0 8.3 %collective-permute-done.61 = bf16[96,1536]{1,0:T(8,128)(2,1)S(1)} collective-permute-done((bf16[96,1536]{1,0:T(8,128)(2,1)S(1)}, bf16[96,1536]{1,0:T(8,128)(2,1)S(1)}, u32[]{:S(2)}, u32[]{:S(2)}) %collective-permute-start.61) | collective-permute-done | bytes 294944 | tf_op jit(solution)/shard_map/ppermute | solution.py:440
  560.9 10.4 %collective-permute-done.49 = bf16[48,3072]{1,0:T(8,128)(2,1)S(1)} collective-permute-done((bf16[48,3072]{1,0:T(8,128)(2,1)S(1)}, bf16[48,3072]{1,0:T(8,128)(2,1)S(1)}, u32[]{:S(2)}, u32[]{:S(2)}) %collective-permute-start.49) | collective-permute-done | bytes 294944 | tf_op jit(solution)/shard_map/ppermute | solution.py:440
  580.5 6.8 collective-permute-done.65
  587.4 17.8 %collective-permute-done.64 = bf16[48,3456]{1,0:T(8,128)(2,1)S(1)} collective-permute-done((bf16[48,3456]{1,0:T(8,128)(2,1)S(1)}, bf16[48,3456]{1,0:T(8,128)(2,1)S(1)}, u32[]{:S(2)}, u32[]{:S(2)}) %collective-permute-start.64) | collective-permute-done | bytes 331808 | tf_op jit(solution)/shard_map/ppermute | solution.py:440
  609.8 7.4 %fusion.9 = f32[1,256,1536]{2,1,0:T(8,128)} fusion(bf16[256,3072]{1,0:T(8,128)(2,1)S(1)} %copy-done.18, bf16[3072,1536]{1,0:T(8,128)(2,1)} %constant_dynamic-update-slice_fusion.3, bf16[1,256,1536]{2,1,0:T(8,128)(2,1)S(1)} %copy-done.6), kind=kOutput, calls=%fused_computation.24 | convolution fusion | flops 2416705536 | bytes 13369344 | tf_op jit(solution)/shard_map/dot_general | solution.py:21
  617.9 14.8 %collective-permute-done.67 = bf16[48,3456]{1,0:T(8,128)(2,1)S(1)} collective-permute-done((bf16[48,3456]{1,0:T(8,128)(2,1)S(1)}, bf16[48,3456]{1,0:T(8,128)(2,1)S(1)}, u32[]{:S(2)}, u32[]{:S(2)}) %collective-permute-start.67) | collective-permute-done | bytes 331808 | tf_op jit(solution)/shard_map/ppermute | solution.py:440
  638.8 26.6 %collective-permute-done.43 = f32[1,5348]{1,0:T(1,128)S(1)} collective-permute-done((f32[1,5348]{1,0:T(1,128)S(1)}, f32[1,5348]{1,0:T(1,128)S(1)}, u32[]{:S(2)}, u32[]{:S(2)}) %collective-permute-start.43) | collective-permute-done | bytes 21424 | tf_op jit(solution)/shard_map/ppermute | solution.py:440
  668.7 22.2 %collective-permute-done.70.refs_1_ = bf16[4,96,1536]{2,1,0:T(8,128)(2,1)} collective-permute-done((bf16[4,96,1536]{2,1,0:T(8,128)(2,1)S(1)}, bf16[4,96,1536]{2,1,0:T(8,128)(2,1)}, u32[]{:S(2)}, u32[]{:S(2)}) %collective-permute-start.70) | collective-permute-done | bytes 1179680 | tf_op jit(solution)/shard_map/ppermute | solution.py:440
  690.9 7.5 %placed.1 = f32[768,1536]{1,0:T(8,128)} custom-call(s32[2]{0:T(128)} %pad_add_fusion.1.ranks_ref, bf16[4,96,1536]{2,1,0:T(8,128)(2,1)} %copy-done.10, bf16[4,96,1536]{2,1,0:T(8,128)(2,1)} %collective-permute-done.70.refs_1_), custom_call_target="tpu_custom_call" | custom-call | tf_op jit(solution)/shard_map/placed/pallas_call | solution.py:642
  698.4 14.9 %collective-permute-done.51.far_a_ref = bf16[4,48,3072]{2,1,0:T(8,128)(2,1)} collective-permute-done((bf16[4,48,3072]{2,1,0:T(8,128)(2,1)}, bf16[4,48,3072]{2,1,0:T(8,128)(2,1)}, u32[]{:S(2)}, u32[]{:S(2)}) %collective-permute-start.51) | collective-permute-done | bytes 1179680 | tf_op jit(solution)/shard_map/ppermute | solution.py:440
  713.3 12.9 %placed_turned.1 = f32[6448,384]{1,0:T(8,128)} custom-call(s32[3]{0:T(128)} %pad_add_fusion.ranks_ref, bf16[4,48,3072]{2,1,0:T(8,128)(2,1)} %pad_maximum_fusion.2.near_a_ref, bf16[4,48,3072]{2,1,0:T(8,128)(2,1)} %collective-permute-done.51.far_a_ref, bf16[4,48,3456]{2,1,0:T(8,128)(2,1)} %copy-done.9, bf16[4,48,3456]{2,1,0:T(8,128)(2,1)} %collective-permute-done.69.far_b_ref), custom_call_target="tpu_custom_call" | custom-call | tf_op jit(solution)/shard_map/placed_turned/pallas_call | solution.py:688
  (412 shorter events, 262.4 us)
Async XLA Ops:
  5.6 40.1 %collective-permute-start.2 = (bf16[5376]{0:T(1024)(128)(2,1)S(1)}, bf16[5376]{0:T(1024)(128)(2,1)}, u32[]{:S(2)}, u32[]{:S(2)}) collective-permute-start(bf16[5376]{0:T(1024)(128)(2,1)S(1)} %pad.4), channel_id=1, source_target_pairs={{0,3},{1,2},{2,1},{3,0},{4,7},{5,6},{6,5},{7,4},{8,11},{9,10},{10,... | collective-permute-start | bytes 32264 | tf_op jit(solution)/shard_map/ppermute | solution.py:440
  8.1 38.3 %collective-permute-start.1 = (bf16[5376]{0:T(1024)(128)(2,1)S(1)}, bf16[5376]{0:T(1024)(128)(2,1)}, u32[]{:S(2)}, u32[]{:S(2)}) collective-permute-start(bf16[5376]{0:T(1024)(128)(2,1)S(1)} %pad.4), channel_id=1, source_target_pairs={{0,2},{1,3},{2,0},{3,1},{4,6},{5,7},{6,4},{7,5},{8,10},{9,11},{10,... | collective-permute-start | bytes 32264 | tf_op jit(solution)/shard_map/ppermute | solution.py:440
  8.7 40.3 %collective-permute-start = (bf16[5376]{0:T(1024)(128)(2,1)S(1)}, bf16[5376]{0:T(1024)(128)(2,1)S(1)}, u32[]{:S(2)}, u32[]{:S(2)}) collective-permute-start(bf16[5376]{0:T(1024)(128)(2,1)S(1)} %pad.4), channel_id=1, source_target_pairs={{0,1},{1,0},{2,3},{3,2},{4,5},{5,4},{6,7},{7,6},{8,9},{9,8},{10,11... | collective-permute-start | bytes 32264 | tf_op jit(solution)/shard_map/ppermute | solution.py:440
  11.9 58.8 %collective-permute-start.3 = (bf16[384,3376]{0,1:T(8,128)(2,1)S(1)}, bf16[384,3376]{0,1:T(8,128)(2,1)}, u32[]{:S(2)}, u32[]{:S(2)}) collective-permute-start(bf16[384,3376]{0,1:T(8,128)(2,1)S(1)} %get-tuple-element.132), channel_id=1, source_target_pairs={{0,1},{1,0},{2,3},{3,2},{4,5},{5,4},{6,7},{7,6},{8,9},{9,8},{10,11... | collective-permute-start | bytes 7778312 | tf_op jit(solution)/shard_map/ppermute | solution.py:440
  22.5 108.5 %collective-permute-start.11 = (bf16[384,3072]{0,1:T(8,128)(2,1)}, bf16[384,3072]{0,1:T(8,128)(2,1)}, u32[]{:S(2)}, u32[]{:S(2)}) collective-permute-start(bf16[384,3072]{0,1:T(8,128)(2,1)} %get-tuple-element.130), channel_id=1, source_target_pairs={{0,1},{1,0},{2,3},{3,2},{4,5},{5,4},{6,7},{7,6},{8,9},{9,8},{10,11... | collective-permute-start | bytes 7077896 | tf_op jit(solution)/shard_map/ppermute | solution.py:440
  45.6 119.9 %collective-permute-start.18 = (bf16[768,1536]{1,0:T(8,128)(2,1)}, bf16[768,1536]{1,0:T(8,128)(2,1)}, u32[]{:S(2)}, u32[]{:S(2)}) collective-permute-start(bf16[768,1536]{1,0:T(8,128)(2,1)} %param.21), channel_id=1, source_target_pairs={{0,1},{1,0},{2,3},{3,2},{4,5},{5,4},{6,7},{7,6},{8,9},{9,8},{10,11... | collective-permute-start | bytes 7077896 | tf_op jit(solution)/shard_map/ppermute | solution.py:440
  49.0 38.4 %collective-permute-start.6 = (bf16[128,3376]{0,1:T(8,128)(2,1)}, bf16[128,3376]{0,1:T(8,128)(2,1)}, u32[]{:S(2)}, u32[]{:S(2)}) collective-permute-start(bf16[128,3376]{0,1:T(8,128)(2,1)} %dynamic_slice.107), channel_id=1, source_target_pairs={{0,2},{1,3},{2,0},{3,1},{4,6},{5,7},{6,4},{7,5},{8,10},{9,11},{10,... | collective-permute-start | bytes 2592776 | tf_op jit(solution)/shard_map/ppermute | solution.py:440
  68.9 60.1 %collective-permute-start.12 = (bf16[128,3072]{0,1:T(8,128)(2,1)}, bf16[128,3072]{0,1:T(8,128)(2,1)}, u32[]{:S(2)}, u32[]{:S(2)}) collective-permute-start(bf16[128,3072]{0,1:T(8,128)(2,1)} %constant_dynamic-slice_fusion.12), channel_id=1, source_target_pairs={{0,2},{1,3},{2,0},{3,1},{4,6},{5,7},{6,4},{7,5},{8,10},{9,11},{10,... | collective-permute-start | bytes 2359304 | tf_op jit(solution)/shard_map/ppermute | solution.py:440
  92.4 37.6 %collective-permute-start.13 = (bf16[128,3072]{0,1:T(8,128)(2,1)S(1)}, bf16[128,3072]{0,1:T(8,128)(2,1)}, u32[]{:S(2)}, u32[]{:S(2)}) collective-permute-start(bf16[128,3072]{0,1:T(8,128)(2,1)S(1)} %copy-done.25), channel_id=1, source_target_pairs={{0,2},{1,3},{2,0},{3,1},{4,6},{5,7},{6,4},{7,5},{8,10},{9,11},{10,... | collective-permute-start | bytes 2359304 | tf_op jit(solution)/shard_map/ppermute | solution.py:440
  128.9 29.0 %collective-permute-start.19 = (bf16[256,1536]{1,0:T(8,128)(2,1)}, bf16[256,1536]{1,0:T(8,128)(2,1)}, u32[]{:S(2)}, u32[]{:S(2)}) collective-permute-start(bf16[256,1536]{1,0:T(8,128)(2,1)} %get-tuple-element.144), channel_id=1, source_target_pairs={{0,2},{1,3},{2,0},{3,1},{4,6},{5,7},{6,4},{7,5},{8,10},{9,11},{10,... | collective-permute-start | bytes 2359304 | tf_op jit(solution)/shard_map/ppermute | solution.py:440
  130.1 35.4 %collective-permute-start.20 = (bf16[256,1536]{1,0:T(8,128)(2,1)}, bf16[256,1536]{1,0:T(8,128)(2,1)}, u32[]{:S(2)}, u32[]{:S(2)}) collective-permute-start(bf16[256,1536]{1,0:T(8,128)(2,1)} %get-tuple-element.143), channel_id=1, source_target_pairs={{0,2},{1,3},{2,0},{3,1},{4,6},{5,7},{6,4},{7,5},{8,10},{9,11},{10,... | collective-permute-start | bytes 2359304 | tf_op jit(solution)/shard_map/ppermute | solution.py:440
  131.1 70.8 %collective-permute-start.14 = (bf16[128,3072]{0,1:T(8,128)(2,1)}, bf16[128,3072]{0,1:T(8,128)(2,1)}, u32[]{:S(2)}, u32[]{:S(2)}) collective-permute-start(bf16[128,3072]{0,1:T(8,128)(2,1)} %collective-permute-done.12), channel_id=1, source_target_pairs={{0,1},{1,0},{2,3},{3,2},{4,5},{5,4},{6,7},{7,6},{8,9},{9,8},{10,11... | collective-permute-start | bytes 2359304 | tf_op jit(solution)/shard_map/ppermute | solution.py:440
  131.7 53.9 %collective-permute-start.16 = (bf16[128,3072]{0,1:T(8,128)(2,1)}, bf16[128,3072]{0,1:T(8,128)(2,1)}, u32[]{:S(2)}, u32[]{:S(2)}) collective-permute-start(bf16[128,3072]{0,1:T(8,128)(2,1)} %collective-permute-done.12), channel_id=1, source_target_pairs={{0,4},{4,0},{8,12},{12,8},{16,20},{20,16},{24,28},{28,24},{1,5},{5... | collective-permute-start | bytes 2359304 | tf_op jit(solution)/shard_map/ppermute | solution.py:440
  165.5 29.9 %collective-permute-start.23 = (bf16[256,1536]{1,0:T(8,128)(2,1)}, bf16[256,1536]{1,0:T(8,128)(2,1)}, u32[]{:S(2)}, u32[]{:S(2)}) collective-permute-start(bf16[256,1536]{1,0:T(8,128)(2,1)} %collective-permute-done.19), channel_id=1, source_target_pairs={{0,4},{4,0},{8,12},{12,8},{16,20},{20,16},{24,28},{28,24},{1,5},{5... | collective-permute-start | bytes 2359304 | tf_op jit(solution)/shard_map/ppermute | solution.py:440
  167.2 32.5 %collective-permute-start.22 = (bf16[256,1536]{1,0:T(8,128)(2,1)}, bf16[256,1536]{1,0:T(8,128)(2,1)}, u32[]{:S(2)}, u32[]{:S(2)}) collective-permute-start(bf16[256,1536]{1,0:T(8,128)(2,1)} %collective-permute-done.20), channel_id=1, source_target_pairs={{0,1},{1,0},{2,3},{3,2},{4,5},{5,4},{6,7},{7,6},{8,9},{9,8},{10,11... | collective-permute-start | bytes 2359304 | tf_op jit(solution)/shard_map/ppermute | solution.py:440
  170.2 44.4 %all-to-all-start = ((f32[8,129,384]{2,1,0:T(8,128)}), f32[8,129,384]{2,1,0:T(8,128)}, u32[]{:S(2)}, u32[]{:S(2)}) async-start(f32[8,129,384]{2,1,0:T(8,128)} %maximum_bitcast_fusion), calls=%async_computation | async-start | bytes 3342336 | tf_op jit(solution)/shard_map/all_to_all | solution.py:417
  185.7 52.5 %collective-permute-start.17 = (bf16[128,3072]{0,1:T(8,128)(2,1)}, bf16[128,3072]{0,1:T(8,128)(2,1)}, u32[]{:S(2)}, u32[]{:S(2)}) collective-permute-start(bf16[128,3072]{0,1:T(8,128)(2,1)} %collective-permute-done.16), channel_id=1, source_target_pairs={{0,1},{1,0},{2,3},{3,2},{4,5},{5,4},{6,7},{7,6},{8,9},{9,8},{10,11... | collective-permute-start | bytes 2359304 | tf_op jit(solution)/shard_map/ppermute | solution.py:440
  195.4 40.6 %collective-permute-start.24 = (bf16[256,1536]{1,0:T(8,128)(2,1)}, bf16[256,1536]{1,0:T(8,128)(2,1)}, u32[]{:S(2)}, u32[]{:S(2)}) collective-permute-start(bf16[256,1536]{1,0:T(8,128)(2,1)} %collective-permute-done.23), channel_id=1, source_target_pairs={{0,1},{1,0},{2,3},{3,2},{4,5},{5,4},{6,7},{7,6},{8,9},{9,8},{10,11... | collective-permute-start | bytes 2359304 | tf_op jit(solution)/shard_map/ppermute | solution.py:440
  227.4 41.2 %all-to-all-start.1 = ((f32[8,128,384]{2,1,0:T(8,128)}), f32[8,128,384]{2,1,0:T(8,128)}, u32[]{:S(2)}, u32[]{:S(2)}) async-start(f32[8,128,384]{2,1,0:T(8,128)} %fusion.32), calls=%async_computation.1 | async-start | bytes 3145728 | tf_op jit(solution)/shard_map/all_to_all | solution.py:429
  293.4 31.6 %collective-permute-start.28 = (bf16[256,1536]{1,0:T(8,128)(2,1)}, bf16[256,1536]{1,0:T(8,128)(2,1)}, u32[]{:S(2)}, u32[]{:S(2)}) collective-permute-start(bf16[256,1536]{1,0:T(8,128)(2,1)} %bitcast.169), channel_id=1, source_target_pairs={{0,2},{1,3},{2,0},{3,1},{4,6},{5,7},{6,4},{7,5},{8,10},{9,11},{10,... | collective-permute-start | bytes 2359304 | tf_op jit(solution)/shard_map/ppermute | solution.py:440
  294.5 84.8 %collective-permute-start.34 = (bf16[256,3072]{1,0:T(8,128)(2,1)}, bf16[256,3072]{1,0:T(8,128)(2,1)}, u32[]{:S(2)}, u32[]{:S(2)}) collective-permute-start(bf16[256,3072]{1,0:T(8,128)(2,1)} %get-tuple-element.80.refs_4_), channel_id=1, source_target_pairs={{0,2},{1,3},{2,0},{3,1},{4,6},{5,7},{6,4},{7,5},{8,10},{9,11},{10,... | collective-permute-start | bytes 4718600 | tf_op jit(solution)/shard_map/ppermute | solution.py:440
  295.4 83.9 %collective-permute-start.35 = (bf16[256,3072]{1,0:T(8,128)(2,1)}, bf16[256,3072]{1,0:T(8,128)(2,1)}, u32[]{:S(2)}, u32[]{:S(2)}) collective-permute-start(bf16[256,3072]{1,0:T(8,128)(2,1)} %get-tuple-element.80.refs_4_), channel_id=1, source_target_pairs={{0,1},{1,0},{2,3},{3,2},{4,5},{5,4},{6,7},{7,6},{8,9},{9,8},{10,11... | collective-permute-start | bytes 4718600 | tf_op jit(solution)/shard_map/ppermute | solution.py:440
  320.5 48.3 %all-to-all-start.3 = ((bf16[8,128,384]{2,1,0:T(8,128)(2,1)}), bf16[8,128,384]{2,1,0:T(8,128)(2,1)}, u32[]{:S(2)}, u32[]{:S(2)}) async-start(bf16[8,128,384]{2,1,0:T(8,128)(2,1)} %broadcast_dynamic-update-slice_fusion.1), calls=%async_computation.3 | async-start | bytes 1572864 | tf_op jit(solution)/shard_map/all_to_all | solution.py:429
  329.8 31.6 %collective-permute-start.27 = (bf16[256,768]{1,0:T(8,128)(2,1)}, bf16[256,768]{1,0:T(8,128)(2,1)}, u32[]{:S(2)}, u32[]{:S(2)}) collective-permute-start(bf16[256,768]{1,0:T(8,128)(2,1)} %get-tuple-element.152), channel_id=1, source_target_pairs={{0,3},{1,2},{2,1},{3,0},{4,7},{5,6},{6,5},{7,4},{8,11},{9,10},{10,... | collective-permute-start | bytes 1179656 | tf_op jit(solution)/shard_map/ppermute | solution.py:440
  379.3 36.0 %collective-permute-start.36 = (bf16[256,3072]{1,0:T(8,128)(2,1)}, bf16[256,3072]{1,0:T(8,128)(2,1)}, u32[]{:S(2)}, u32[]{:S(2)}) collective-permute-start(bf16[256,3072]{1,0:T(8,128)(2,1)} %collective-permute-done.34.refs_5_), channel_id=1, source_target_pairs={{0,1},{1,0},{2,3},{3,2},{4,5},{5,4},{6,7},{7,6},{8,9},{9,8},{10,11... | collective-permute-start | bytes 4718600 | tf_op jit(solution)/shard_map/ppermute | solution.py:440
  382.7 32.6 %collective-permute-start.31 = (bf16[256,384]{1,0:T(8,128)(2,1)}, bf16[256,384]{1,0:T(8,128)(2,1)}, u32[]{:S(2)}, u32[]{:S(2)}) collective-permute-start(bf16[256,384]{1,0:T(8,128)(2,1)} %get-tuple-element.160), channel_id=1, source_target_pairs={{0,2},{1,3},{2,0},{3,1},{4,6},{5,7},{6,4},{7,5},{8,10},{9,11},{10,... | collective-permute-start | bytes 589832 | tf_op jit(solution)/shard_map/ppermute | solution.py:440
  383.8 31.5 %collective-permute-start.32 = (bf16[256,384]{1,0:T(8,128)(2,1)}, bf16[256,384]{1,0:T(8,128)(2,1)}, u32[]{:S(2)}, u32[]{:S(2)}) collective-permute-start(bf16[256,384]{1,0:T(8,128)(2,1)} %get-tuple-element.159), channel_id=1, source_target_pairs={{0,1},{1,0},{2,3},{3,2},{4,5},{5,4},{6,7},{7,6},{8,9},{9,8},{10,11... | collective-permute-start | bytes 589832 | tf_op jit(solution)/shard_map/ppermute | solution.py:440
  383.8 31.5 %collective-permute-start.33 = (bf16[256,384]{1,0:T(8,128)(2,1)}, bf16[256,384]{1,0:T(8,128)(2,1)}, u32[]{:S(2)}, u32[]{:S(2)}) collective-permute-start(bf16[256,384]{1,0:T(8,128)(2,1)} %get-tuple-element.158), channel_id=1, source_target_pairs={{0,3},{1,2},{2,1},{3,0},{4,7},{5,6},{6,5},{7,4},{8,11},{9,10},{10,... | collective-permute-start | bytes 589832 | tf_op jit(solution)/shard_map/ppermute | solution.py:440
  396.6 35.6 %collective-permute-start.56 = (bf16[384,1536]{1,0:T(8,128)(2,1)}, bf16[384,1536]{1,0:T(8,128)(2,1)}, u32[]{:S(2)}, u32[]{:S(2)}) collective-permute-start(bf16[384,1536]{1,0:T(8,128)(2,1)} %get-tuple-element.88), channel_id=1, source_target_pairs={{0,4},{4,0},{8,12},{12,8},{16,20},{20,16},{24,28},{28,24},{1,5},{5... | collective-permute-start | bytes 3538952 | tf_op jit(solution)/shard_map/ppermute | solution.py:440
  429.5 58.1 %collective-permute-start.44 = (bf16[192,3072]{1,0:T(8,128)(2,1)}, bf16[192,3072]{1,0:T(8,128)(2,1)}, u32[]{:S(2)}, u32[]{:S(2)}) collective-permute-start(bf16[192,3072]{1,0:T(8,128)(2,1)} %get-tuple-element.84), channel_id=1, source_target_pairs={{0,4},{4,0},{8,12},{12,8},{16,20},{20,16},{24,28},{28,24},{1,5},{5... | collective-permute-start | bytes 3538952 | tf_op jit(solution)/shard_map/ppermute | solution.py:440
  436.1 55.6 %collective-permute-start.59 = (bf16[96,1536]{1,0:T(8,128)(2,1)}, bf16[96,1536]{1,0:T(8,128)(2,1)}, u32[]{:S(2)}, u32[]{:S(2)}) collective-permute-start(bf16[96,1536]{1,0:T(8,128)(2,1)} %get-tuple-element.138), channel_id=1, source_target_pairs={{0,24},{4,28},{8,16},{12,20},{16,8},{20,12},{24,0},{28,4},{1,25},{... | collective-permute-start | bytes 884744 | tf_op jit(solution)/shard_map/ppermute | solution.py:440
  439.3 55.6 %collective-permute-start.58 = (bf16[96,1536]{1,0:T(8,128)(2,1)}, bf16[96,1536]{1,0:T(8,128)(2,1)}, u32[]{:S(2)}, u32[]{:S(2)}) collective-permute-start(bf16[96,1536]{1,0:T(8,128)(2,1)} %get-tuple-element.139), channel_id=1, source_target_pairs={{0,16},{4,20},{8,24},{12,28},{16,0},{20,4},{24,8},{28,12},{1,17},{... | collective-permute-start | bytes 884744 | tf_op jit(solution)/shard_map/ppermute | solution.py:440
  446.7 39.8 %collective-permute-start.52 = (bf16[256,3456]{1,0:T(8,128)(2,1)}, bf16[256,3456]{1,0:T(8,128)(2,1)}, u32[]{:S(2)}, u32[]{:S(2)}) collective-permute-start(bf16[256,3456]{1,0:T(8,128)(2,1)} %concatenate.61.refs_4_), channel_id=1, source_target_pairs={{0,2},{1,3},{2,0},{3,1},{4,6},{5,7},{6,4},{7,5},{8,10},{9,11},{10,... | collective-permute-start | bytes 5308424 | tf_op jit(solution)/shard_map/ppermute | solution.py:440
  447.9 51.7 %collective-permute-start.53 = (bf16[256,3456]{1,0:T(8,128)(2,1)}, bf16[256,3456]{1,0:T(8,128)(2,1)}, u32[]{:S(2)}, u32[]{:S(2)}) collective-permute-start(bf16[256,3456]{1,0:T(8,128)(2,1)} %concatenate.61.refs_4_), channel_id=1, source_target_pairs={{0,1},{1,0},{2,3},{3,2},{4,5},{5,4},{6,7},{7,6},{8,9},{9,8},{10,11... | collective-permute-start | bytes 5308424 | tf_op jit(solution)/shard_map/ppermute | solution.py:440
  494.9 39.2 %collective-permute-start.46 = (bf16[48,3072]{1,0:T(8,128)(2,1)}, bf16[48,3072]{1,0:T(8,128)(2,1)}, u32[]{:S(2)}, u32[]{:S(2)}) collective-permute-start(bf16[48,3072]{1,0:T(8,128)(2,1)} %get-tuple-element.142), channel_id=1, source_target_pairs={{0,16},{4,20},{8,24},{12,28},{16,0},{20,4},{24,8},{28,12},{1,17},{... | collective-permute-start | bytes 884744 | tf_op jit(solution)/shard_map/ppermute | solution.py:440
  497.3 37.5 %collective-permute-start.45 = (bf16[48,3072]{1,0:T(8,128)(2,1)}, bf16[48,3072]{1,0:T(8,128)(2,1)}, u32[]{:S(2)}, u32[]{:S(2)}) collective-permute-start(bf16[48,3072]{1,0:T(8,128)(2,1)} %get-tuple-element.140), channel_id=1, source_target_pairs={{0,8},{4,12},{8,0},{12,4},{16,24},{20,28},{24,16},{28,20},{1,9},{5... | collective-permute-start | bytes 884744 | tf_op jit(solution)/shard_map/ppermute | solution.py:440
  499.6 38.6 %collective-permute-start.62 = (bf16[96,1536]{1,0:T(8,128)(2,1)S(1)}, bf16[96,1536]{1,0:T(8,128)(2,1)S(1)}, u32[]{:S(2)}, u32[]{:S(2)}) collective-permute-start(bf16[96,1536]{1,0:T(8,128)(2,1)S(1)} %add_convert_fusion.2), channel_id=1, source_target_pairs={{0,24},{4,28},{8,16},{12,20},{16,8},{20,12},{24,0},{28,4},{1,25},{... | collective-permute-start | bytes 884744 | tf_op jit(solution)/shard_map/ppermute | solution.py:440
  503.3 56.0 %collective-permute-start.61 = (bf16[96,1536]{1,0:T(8,128)(2,1)S(1)}, bf16[96,1536]{1,0:T(8,128)(2,1)S(1)}, u32[]{:S(2)}, u32[]{:S(2)}) collective-permute-start(bf16[96,1536]{1,0:T(8,128)(2,1)S(1)} %add_convert_fusion.2), channel_id=1, source_target_pairs={{0,16},{4,20},{8,24},{12,28},{16,0},{20,4},{24,8},{28,12},{1,17},{... | collective-permute-start | bytes 884744 | tf_op jit(solution)/shard_map/ppermute | solution.py:440
  513.5 45.9 %collective-permute-start.60 = (bf16[96,1536]{1,0:T(8,128)(2,1)S(1)}, bf16[96,1536]{1,0:T(8,128)(2,1)S(1)}, u32[]{:S(2)}, u32[]{:S(2)}) collective-permute-start(bf16[96,1536]{1,0:T(8,128)(2,1)S(1)} %add_convert_fusion.2), channel_id=1, source_target_pairs={{0,8},{4,12},{8,0},{12,4},{16,24},{20,28},{24,16},{28,20},{1,9},{5... | collective-permute-start | bytes 884744 | tf_op jit(solution)/shard_map/ppermute | solution.py:440
  534.1 40.2 %collective-permute-start.55 = (bf16[192,3456]{1,0:T(8,128)(2,1)}, bf16[192,3456]{1,0:T(8,128)(2,1)S(1)}, u32[]{:S(2)}, u32[]{:S(2)}) collective-permute-start(bf16[192,3456]{1,0:T(8,128)(2,1)} %get-tuple-element.87), channel_id=1, source_target_pairs={{0,4},{4,0},{8,12},{12,8},{16,20},{20,16},{24,28},{28,24},{1,5},{5... | collective-permute-start | bytes 3981320 | tf_op jit(solution)/shard_map/ppermute | solution.py:440
  538.2 33.2 %collective-permute-start.49 = (bf16[48,3072]{1,0:T(8,128)(2,1)S(1)}, bf16[48,3072]{1,0:T(8,128)(2,1)S(1)}, u32[]{:S(2)}, u32[]{:S(2)}) collective-permute-start(bf16[48,3072]{1,0:T(8,128)(2,1)S(1)} %add_convert_fusion.3), channel_id=1, source_target_pairs={{0,16},{4,20},{8,24},{12,28},{16,0},{20,4},{24,8},{28,12},{1,17},{... | collective-permute-start | bytes 884744 | tf_op jit(solution)/shard_map/ppermute | solution.py:440
  577.5 27.7 %collective-permute-start.64 = (bf16[48,3456]{1,0:T(8,128)(2,1)S(1)}, bf16[48,3456]{1,0:T(8,128)(2,1)S(1)}, u32[]{:S(2)}, u32[]{:S(2)}) collective-permute-start(bf16[48,3456]{1,0:T(8,128)(2,1)S(1)} %get-tuple-element.136), channel_id=1, source_target_pairs={{0,16},{4,20},{8,24},{12,28},{16,0},{20,4},{24,8},{28,12},{1,17},{... | collective-permute-start | bytes 995336 | tf_op jit(solution)/shard_map/ppermute | solution.py:440
  577.5 27.7 %collective-permute-start.63 = (bf16[48,3456]{1,0:T(8,128)(2,1)S(1)}, bf16[48,3456]{1,0:T(8,128)(2,1)S(1)}, u32[]{:S(2)}, u32[]{:S(2)}) collective-permute-start(bf16[48,3456]{1,0:T(8,128)(2,1)S(1)} %get-tuple-element.134), channel_id=1, source_target_pairs={{0,8},{4,12},{8,0},{12,4},{16,24},{20,28},{24,16},{28,20},{1,9},{5... | collective-permute-start | bytes 995336 | tf_op jit(solution)/shard_map/ppermute | solution.py:440
  579.3 38.0 %collective-permute-start.41 = (f32[1,5348]{1,0:T(1,128)S(1)}, f32[1,5348]{1,0:T(1,128)S(1)}, u32[]{:S(2)}, u32[]{:S(2)}) collective-permute-start(f32[1,5348]{1,0:T(1,128)S(1)} %add_add_fusion), channel_id=1, source_target_pairs={{0,16},{4,20},{8,24},{12,28},{16,0},{20,4},{24,8},{28,12},{1,17},{... | collective-permute-start | bytes 64184 | tf_op jit(solution)/shard_map/ppermute | solution.py:440
  633.0 80.3 %collective-permute-start.69 = (bf16[4,48,3456]{2,1,0:T(8,128)(2,1)S(1)}, bf16[4,48,3456]{2,1,0:T(8,128)(2,1)}, u32[]{:S(2)}, u32[]{:S(2)}) collective-permute-start(bf16[4,48,3456]{2,1,0:T(8,128)(2,1)S(1)} %pad_maximum_fusion.1.near_b_ref), channel_id=1, source_target_pairs={{0,4},{4,0},{8,12},{12,8},{16,20},{20,16},{24,28},{28,24},{1,5},{5... | collective-permute-start | bytes 3981320 | tf_op jit(solution)/shard_map/ppermute | solution.py:440
  633.7 31.8 %collective-permute-start.43 = (f32[1,5348]{1,0:T(1,128)S(1)}, f32[1,5348]{1,0:T(1,128)S(1)}, u32[]{:S(2)}, u32[]{:S(2)}) collective-permute-start(f32[1,5348]{1,0:T(1,128)S(1)} %add.561), channel_id=1, source_target_pairs={{0,4},{4,0},{8,12},{12,8},{16,20},{20,16},{24,28},{28,24},{1,5},{5... | collective-permute-start | bytes 64184 | tf_op jit(solution)/shard_map/ppermute | solution.py:440
  635.2 55.7 %collective-permute-start.70 = (bf16[4,96,1536]{2,1,0:T(8,128)(2,1)S(1)}, bf16[4,96,1536]{2,1,0:T(8,128)(2,1)}, u32[]{:S(2)}, u32[]{:S(2)}) collective-permute-start(bf16[4,96,1536]{2,1,0:T(8,128)(2,1)S(1)} %pad_maximum_fusion.3.refs_0_), channel_id=1, source_target_pairs={{0,4},{4,0},{8,12},{12,8},{16,20},{20,16},{24,28},{28,24},{1,5},{5... | collective-permute-start | bytes 3538952 | tf_op jit(solution)/shard_map/ppermute | solution.py:440
  635.8 77.5 %collective-permute-start.51 = (bf16[4,48,3072]{2,1,0:T(8,128)(2,1)}, bf16[4,48,3072]{2,1,0:T(8,128)(2,1)}, u32[]{:S(2)}, u32[]{:S(2)}) collective-permute-start(bf16[4,48,3072]{2,1,0:T(8,128)(2,1)} %pad_maximum_fusion.2.near_a_ref), channel_id=1, source_target_pairs={{0,4},{4,0},{8,12},{12,8},{16,20},{20,16},{24,28},{28,24},{1,5},{5... | collective-permute-start | bytes 3538952 | tf_op jit(solution)/shard_map/ppermute | solution.py:440
  (79 other events, 1195.0 us)

commit v2 on v1

--- a/solution.py
+++ b/solution.py
@@ -426,8 +426,8 @@
     for device in order:
         entering[device] = running.astype(wire)
         running = running * decay[device][None, :] + own[device]
-    home = lax.all_to_all(jnp.stack(entering), axis, split_axis=0, concat_axis=0, tiled=True)
-    return home
+    entering = jnp.stack(entering)
+    return lax.all_to_all(entering, axis, split_axis=0, concat_axis=0, tiled=True), entering
 
 
 def joined(home):
@@ -491,7 +491,8 @@
     if mask == 1:
         return (swapped(shard, axis, 1),)
     arrived = swapped(shared, axis, mask)
-    return swapped(shard, axis, 1), arrived, swapped(own, axis, mask)
+    direct = swapped(own, axis, mask)
+    return swapped(shard, axis, 1), arrived, direct
 
 
 def weight_gathered(shard, sent, axis, side):
@@ -749,9 +750,8 @@
         ]
     )
     small = jnp.pad(small, (0, -small.shape[0] % LANES))
-    small_held = jnp.stack(
-        [swapped(small, "fsdp", flip) if flip else small for flip in range(owner_count)]
-    )
+    small_held = [swapped(small, "fsdp", flip) if flip else small for flip in range(owner_count)]
+    small_held = jnp.stack(small_held)
     owner_rank = lax.axis_index("fsdp")
     small_all = jnp.concatenate(
         [
@@ -813,7 +813,8 @@
     total_lanes = jnp.repeat(total_log, head_width)
 
     own_state = local_state(x_rows, b_rows.T, to_end, head_width)
-    state_full = joined(carried_states(own_state, total_lanes, "seq", False))
+    home, _ = carried_states(own_state, total_lanes, "seq", False)
+    state_full = joined(home)
     state_in = host_halves(state_full)
     inner = inner_part(after(x_rows, own_state), b_rows, c_rows, decay_log, source_log, head_width)
     out_sent = after(out_sent, inner)
@@ -843,7 +844,7 @@
     inner_dx, d_meet, dc_carried = inner_grad(
         x_rows, d_mixed, b_rows, c_rows, decay_log, source_log, grown, state_in[0], head_width
     )
-    home = carried_states(own_dstate, total_lanes, "seq", True, inner_dx)
+    home, _ = carried_states(own_dstate, total_lanes, "seq", True, inner_dx)
     cot_all = passed_on(cot_all, "fsdp")
     out_near, out_away = weight_product(gated_all, cot_all, "seq")
     out_arrived = swapped(out_away, "seq", 1)
@@ -860,6 +861,7 @@
         skip_lanes,
         row_block,
     )
+    out_arrived = after(out_arrived, d_x)
     d_gate_all = passed_on(d_gate_all, "fsdp", d_x)
     gate_near, gate_away = weight_product(normed_all, d_gate_all, "seq")
     gate_arrived = swapped(gate_away, "seq", 1)
@@ -892,21 +894,19 @@
         d_conv_in = d_conv_in + d_tail[shift : shift + tokens] * w_taps[tap]
     spare = jnp.zeros((tokens, -(conv_width + heads) % LANES), BF16)
     d_step_proj = jnp.concatenate([d_conv_in.astype(BF16), d_raw.T.astype(BF16), spare], 1)
-    d_step_all = passed_on(gathered(d_step_proj, "fsdp"), "fsdp")
-    out_arrived = after(out_arrived, gate_near)
+    block_out = hidden_f + plain_dot(after(gated_b, d_step_proj), w_out)
+    d_step_all = passed_on(gathered(d_step_proj, "fsdp"), "fsdp", block_out)
     out_spread = seq_spread(seq_owned(out_near, out_arrived, "seq"), "seq")
     gate_arrived = after(gate_arrived, d_step_proj)
     gate_spread = seq_spread(seq_owned(gate_near, gate_arrived, "seq"), "seq")
     step_near, step_away = weight_product(normed_all, d_step_all, "seq")
     step_arrived = swapped(step_away, "seq", 1)
-    step_arrived = after(step_arrived, (gate_spread[0], out_spread[0]))
     step_spread = seq_spread(seq_owned(step_near, step_arrived, "seq"), "seq")
     d_pre = after(d_pre, d_step_proj)
     grad_w_conv = jnp.stack(
         [jnp.sum(d_pre * padded[tap : tap + tokens], axis=0) for tap in range(taps)]
     )
     grad_b_conv = jnp.sum(d_pre, axis=0)
-    block_out = hidden_f + plain_dot(after(gated_b, d_step_proj), w_out)
     d_normed = against_cols(after(d_gate, d_step_proj), w_gate)
     d_normed = d_normed + against_cols(d_step_proj[:, : conv_width + heads], w_conv_in)
     d_unit = d_normed * gain_n

time: 739 us -> 758 us (1.026)
  the two profiles are of different devices: /device:TPU:0 before, /device:TPU:16 now
where the time goes in v2:
time: 758 us; the launch traced here: 746 us
  waiting for transfers between devices  269 us (35%)
  local copies, waits for them, and re-layouts  141 us (19%)
  starting transfers between devices  110 us (15%)
  Pallas kernels  95.9 us (13%)
  other arithmetic  72.9 us (10%)
  matrix products  54.7 us (7%)
    ppermute x69, waiting for transfers between devices, swapped(): lax.ppermute(value, axis, [(source, source ^ mask) for source in range(co...  257 us
    ppermute x69, starting transfers between devices, swapped(): lax.ppermute(value, axis, [(source, source ^ mask) for source in range(co...  76.5 us
    dot_general x8, matrix products, dims(): lax.dot_general(left, right, (contract, ((), ())), preferred_element_type...  52.1 us
    pallas_call x3, Pallas kernels, weight_product(): pl.pallas_call(product_kernel, out_shape=(jax.ShapeDtypeStruct((rows // 2...  26.4 us
    dynamic_update_slice x9, local copies, waits for them, and re-layouts, weight_gathered(): whole = lax.dynamic_update_slice_in_dim(whole, block, start, 0)  18.1 us
  transfers between devices with their start and end apart: 75, of which 26 were waited for; matrix products, arithmetic and copies ran while one was open for 33% of the time, Pallas kernels for 8%

profile of v2, /device:TPU:16, one launch (start us, length us, event | category | flops | bytes accessed | tf_op | source)
XLA Modules:
  0.0 745.8 jit_solution(11125045644162534324)
XLA Ops:
  11.0 4.7 broadcast_in_dim.48
  15.7 5.6 fusion.83
  59.7 7.7 %collective-permute-done.4 = bf16[128,3376]{0,1:T(8,128)(2,1)} collective-permute-done((bf16[128,3376]{0,1:T(8,128)(2,1)}, bf16[128,3376]{0,1:T(8,128)(2,1)}, u32[]{:S(2)}, u32[]{:S(2)}) %collective-permute-start.4) | collective-permute-done | bytes 864288 | tf_op jit(solution)/shard_map/ppermute | solution.py:440
  75.0 10.9 %collective-permute-done.6 = bf16[128,3376]{0,1:T(8,128)(2,1)} collective-permute-done((bf16[128,3376]{0,1:T(8,128)(2,1)}, bf16[128,3376]{0,1:T(8,128)(2,1)}, u32[]{:S(2)}, u32[]{:S(2)}) %collective-permute-start.6) | collective-permute-done | bytes 864288 | tf_op jit(solution)/shard_map/ppermute | solution.py:440
  92.3 13.9 %collective-permute-done.8 = bf16[128,3376]{0,1:T(8,128)(2,1)S(1)} collective-permute-done((bf16[128,3376]{0,1:T(8,128)(2,1)}, bf16[128,3376]{0,1:T(8,128)(2,1)S(1)}, u32[]{:S(2)}, u32[]{:S(2)}) %collective-permute-start.8) | collective-permute-done | bytes 864288 | tf_op jit(solution)/shard_map/ppermute | solution.py:440
  109.6 7.0 convolution_convert_fusion
  140.9 7.0 local_state.1
  147.9 8.6 %inner_part.1.inner_ref = f32[256,3072]{1,0:T(8,128)} custom-call(bf16[256,3072]{1,0:T(8,128)(2,1)} %slice.333.x_ref, bf16[256,128]{1,0:T(8,128)(2,1)} %get-tuple-element.153.b_ref, bf16[256,128]{1,0:T(8,128)(2,1)} %get-tuple-element.151.c_ref, f32[48,256]{1,0:T(8,128)} %copy-done.28, f32[48,256]{1,0:T(8,128)} %copy.101.source_ref), custom_call_target="tpu_custom_call" | custom-call | tf_op jit(solution)/shard_map/inner_part/pallas_call | solution.py:132
  156.5 7.7 %collective-permute-done.20 = bf16[256,1536]{1,0:T(8,128)(2,1)} collective-permute-done((bf16[256,1536]{1,0:T(8,128)(2,1)}, bf16[256,1536]{1,0:T(8,128)(2,1)}, u32[]{:S(2)}, u32[]{:S(2)}) %collective-permute-start.20) | collective-permute-done | bytes 786464 | tf_op jit(solution)/shard_map/ppermute | solution.py:440
  168.6 5.3 all-to-all-start
  185.1 7.7 %collective-permute-done.23 = bf16[256,1536]{1,0:T(8,128)(2,1)} collective-permute-done((bf16[256,1536]{1,0:T(8,128)(2,1)}, bf16[256,1536]{1,0:T(8,128)(2,1)}, u32[]{:S(2)}, u32[]{:S(2)}) %collective-permute-start.23) | collective-permute-done | bytes 786464 | tf_op jit(solution)/shard_map/ppermute | solution.py:440
  204.1 6.1 all-to-all-done
  223.0 7.8 %all-to-all-start.1 = ((f32[8,128,384]{2,1,0:T(8,128)}), f32[8,128,384]{2,1,0:T(8,128)}, u32[]{:S(2)}, u32[]{:S(2)}) async-start(f32[8,128,384]{2,1,0:T(8,128)} %fusion.31), calls=%async_computation.1 | async-start | bytes 3145728 | tf_op jit(solution)/shard_map/all_to_all | solution.py:430
  239.1 10.9 %convolution_convert_fusion.1.gate_ref = bf16[256,3072]{1,0:T(8,128)(2,1)} fusion(bf16[256,1536]{1,0:T(8,128)(2,1)S(1)} %copy-done.13, bf16[1536,3072]{0,1:T(8,128)(2,1)} %constant_dynamic-update-slice_fusion.11), kind=kOutput, calls=%fused_computation.4 | convolution fusion | flops 2416705536 | bytes 11796480 | tf_op jit(solution)/shard_map/dot_general | solution.py:21
  250.1 8.0 %convolution_bitcast_fusion.dgated_ref = f32[256,3072]{1,0:T(8,128)} fusion(bf16[3072,1536]{1,0:T(8,128)(2,1)} %constant_dynamic-update-slice_fusion.3, bf16[1,256,1536]{2,1,0:T(8,128)(2,1)S(1)} %copy-done.14), kind=kOutput, calls=%fused_computation.3 | convolution fusion | flops 2415919104 | bytes 13369344 | tf_op jit(solution)/shard_map/dot_general | solution.py:21
  258.1 6.0 all-to-all-done.1
  267.1 13.4 %middle.1 = (bf16[256,3072]{1,0:T(8,128)(2,1)}, bf16[256,3072]{1,0:T(8,128)(2,1)}, bf16[256,3072]{1,0:T(8,128)(2,1)}, f32[128,3072]{1,0:T(8,128)}, f32[256,48]{1...) custom-call(f32[256,3072]{1,0:T(8,128)} %inner_part.1.inner_ref, bf16[256,3072]{1,0:T(8,128)(2,1)} %slice.333.x_ref, ...), custom_call_target="tpu_custom_call" | custom-call | tf_op jit(solution)/shard_map/middle/pallas_call | solution.py:210
  283.2 7.5 %all-to-all-start.2 = ((bf16[8,131,384]{2,1,0:T(8,128)(2,1)}), bf16[8,131,384]{2,1,0:T(8,128)(2,1)}, u32[]{:S(2)}, u32[]{:S(2)}) async-start(bf16[8,131,384]{2,1,0:T(8,128)(2,1)} %maximum_bitcast_fusion.1), calls=%async_computation.2 | async-start | bytes 1671168 | tf_op jit(solution)/shard_map/all_to_all | solution.py:417
  293.0 16.4 %collective-permute-done.28.refs_5_ = bf16[256,1536]{1,0:T(8,128)(2,1)} collective-permute-done((bf16[256,1536]{1,0:T(8,128)(2,1)}, bf16[256,1536]{1,0:T(8,128)(2,1)}, u32[]{:S(2)}, u32[]{:S(2)}) %collective-permute-start.28) | collective-permute-done | bytes 786464 | tf_op jit(solution)/shard_map/ppermute | solution.py:440
  310.6 11.8 %inner_grad.1 = (f32[256,3072]{1,0:T(8,128)}, f32[256,256]{1,0:T(8,128)}, f32[256,128]{1,0:T(8,128)}) custom-call(bf16[256,3072]{1,0:T(8,128)(2,1)} %slice.333.x_ref, bf16[256,3072]{1,0:T(8,128)(2,1)} %get-tuple-element.60.dy_ref, bf16[256,128]{1,0:T(8,128)(2,1)} %get-tuple-element.153.b_ref, bf16[256,128]{1,0:T(8,128)(2,1)} %get-tuple-element.151.c_ref, ...), custom_call_target="tpu_custom_call" | custom-call | tf_op jit(solution)/shard_map/inner_grad/pallas_call | solution.py:311
  329.9 6.3 all-to-all-start.3
  343.9 11.6 %collective-permute-done.25.refs_1_ = bf16[256,768]{1,0:T(8,128)(2,1)} collective-permute-done((bf16[256,768]{1,0:T(8,128)(2,1)}, bf16[256,768]{1,0:T(8,128)(2,1)}, u32[]{:S(2)}, u32[]{:S(2)}) %collective-permute-start.25) | collective-permute-done | bytes 393248 | tf_op jit(solution)/shard_map/ppermute | solution.py:440
  355.4 7.5 %collective-permute-done.27.refs_3_ = bf16[256,768]{1,0:T(8,128)(2,1)} collective-permute-done((bf16[256,768]{1,0:T(8,128)(2,1)}, bf16[256,768]{1,0:T(8,128)(2,1)}, u32[]{:S(2)}, u32[]{:S(2)}) %collective-permute-start.27) | collective-permute-done | bytes 393248 | tf_op jit(solution)/shard_map/ppermute | solution.py:440
  362.9 7.4 weight_product.3
  388.8 8.3 %outer_grad.1 = (bf16[256,3072]{1,0:T(8,128)(2,1)}, f32[256,48]{1,0:T(8,128)}, f32[256,48]{1,0:T(8,128)}, f32[256,128]{1,0:T(8,128)}) custom-call(f32[256,3072]{1,0:T(8,128)} %get-tuple-element.61.inner_ref, bf16[256,3072]{1,0:T(8,128)(2,1)} %slice.333.x_ref, bf16[256,3072]{1,0:T(8,128)(2,1)} %get-tuple-element.60.dy_ref, ...), custom_call_target="tpu_custom_call" | custom-call | tf_op jit(solution)/shard_map/outer_grad/pallas_call | solution.py:372
  417.4 8.8 %weight_product.4 = (f32[192,3072]{1,0:T(8,128)}, bf16[192,3072]{1,0:T(8,128)(2,1)}) custom-call(s32[1]{0:T(128)} %bitcast.13.place_ref, bf16[256,384]{1,0:T(8,128)(2,1)} %get-tuple-element.163.refs_0_, bf16[256,384]{1,0:T(8,128)(2,1)} %collective-permute-done.31.refs_1_, bf16[256,384]{1,0:T(8,128)(2,1)} %collective-permute-done.32.refs_2_, ...), custom_call_target="tpu_custom_call" | custom-call | tf_op jit(solution)/shard_map/weight_product/pallas_call | solution.py:570
  440.9 7.7 %fusion.5 = bf16[256,3328]{1,0:T(8,128)(2,1)} fusion(f32[3,3328]{1,0:T(4,128)} %collective-permute-done.37, f32[256,3328]{1,0:T(8,128)} %copy-done, f32[3328]{0:T(1024)S(1)} %mul.480, f32[3328]{0:T(1024)} %mul.477, f32[3328]{0:T(1024)} %mul.474, f32[3328]{0:T(1024)} %mul.471), kind=kLoop, calls=%fused_computation.10 | loop fusion | flops 9371648 | bytes 5204992 | tf_op jit(solution)/shard_map/convert_element_type | solution.py:896
  454.2 5.6 fusion.87
  459.9 8.8 %fusion.23 = (f32[1536]{0:T(1024)S(1)}, f32[256]{0:T(256)}, f32[256,1536]{1,0:T(8,128)}) fusion(bf16[1,256,1536]{2,1,0:T(8,128)(2,1)S(1)} %copy-done.6, f32[256]{0:T(256)S(1)} %copy-done.47, f32[1536]{0:T(1024)S(1)} %copy-done.38, f32[256,1536]{1,0:T(8,128)S(1)} %fusion.87, bf16[1536,3376]{0,1:T(8,128)(2,1)} %constant_dynamic-update-slice_fusion.19, ...), kind=kOutput, calls=%fused_computation.48 | convolution fusion | flops 2661595392 | bytes 16046080 | tf_op jit(solution)/shard_map/dot_general | solution.py:21
  469.2 8.2 %convolution_add_fusion = f32[256,1536]{1,0:T(8,128)} fusion(bf16[256,3072]{1,0:T(8,128)(2,1)} %get-tuple-element.80, bf16[3072,1536]{1,0:T(8,128)(2,1)} %constant_dynamic-update-slice_fusion.3, bf16[1,256,1536]{2,1,0:T(8,128)(2,1)} %param.11), kind=kOutput, calls=%fused_computation.23 | convolution fusion | flops 2416705536 | bytes 13369344 | tf_op jit(solution)/shard_map/dot_general | solution.py:21
  477.4 16.3 %collective-permute-done.52.refs_5_ = bf16[256,3456]{1,0:T(8,128)(2,1)} collective-permute-done((bf16[256,3456]{1,0:T(8,128)(2,1)}, bf16[256,3456]{1,0:T(8,128)(2,1)}, u32[]{:S(2)}, u32[]{:S(2)}) %collective-permute-start.52) | collective-permute-done | bytes 1769504 | tf_op jit(solution)/shard_map/ppermute | solution.py:440
  507.8 10.1 %weight_product.5 = (f32[192,3456]{1,0:T(8,128)}, bf16[192,3456]{1,0:T(8,128)(2,1)}) custom-call(s32[1]{0:T(128)} %bitcast.13.place_ref, bf16[256,384]{1,0:T(8,128)(2,1)} %get-tuple-element.163.refs_0_, bf16[256,384]{1,0:T(8,128)(2,1)} %collective-permute-done.31.refs_1_, bf16[256,384]{1,0:T(8,128)(2,1)} %collective-permute-done.32.refs_2_, ...), custom_call_target="tpu_custom_call" | custom-call | tf_op jit(solution)/shard_map/weight_product/pallas_call | solution.py:570
  520.3 5.9 collective-permute-done.69
  526.2 4.3 collective-permute-done.68
  538.1 9.0 %collective-permute-done.44 = bf16[192,3072]{1,0:T(8,128)(2,1)S(1)} collective-permute-done((bf16[192,3072]{1,0:T(8,128)(2,1)}, bf16[192,3072]{1,0:T(8,128)(2,1)S(1)}, u32[]{:S(2)}, u32[]{:S(2)}) %collective-permute-start.44) | collective-permute-done | bytes 1179680 | tf_op jit(solution)/shard_map/ppermute | solution.py:440
  547.5 28.2 %collective-permute-done.55 = bf16[192,3456]{1,0:T(8,128)(2,1)S(1)} collective-permute-done((bf16[192,3456]{1,0:T(8,128)(2,1)}, bf16[192,3456]{1,0:T(8,128)(2,1)S(1)}, u32[]{:S(2)}, u32[]{:S(2)}) %collective-permute-start.55) | collective-permute-done | bytes 1327136 | tf_op jit(solution)/shard_map/ppermute | solution.py:440
  580.5 25.6 %collective-permute-done.58 = bf16[48,3456]{1,0:T(8,128)(2,1)S(1)} collective-permute-done((bf16[48,3456]{1,0:T(8,128)(2,1)S(1)}, bf16[48,3456]{1,0:T(8,128)(2,1)S(1)}, u32[]{:S(2)}, u32[]{:S(2)}) %collective-permute-start.58) | collective-permute-done | bytes 331808 | tf_op jit(solution)/shard_map/ppermute | solution.py:440
  606.1 4.2 collective-permute-done.57
  613.6 5.4 collective-permute-start.45
  619.1 13.8 %collective-permute-done.47 = bf16[48,3072]{1,0:T(8,128)(2,1)S(1)} collective-permute-done((bf16[48,3072]{1,0:T(8,128)(2,1)S(1)}, bf16[48,3072]{1,0:T(8,128)(2,1)S(1)}, u32[]{:S(2)}, u32[]{:S(2)}) %collective-permute-start.47) | collective-permute-done | bytes 294944 | tf_op jit(solution)/shard_map/ppermute | solution.py:440
  639.7 6.2 collective-permute-start.59
  646.0 13.8 %collective-permute-done.61 = bf16[48,3456]{1,0:T(8,128)(2,1)S(1)} collective-permute-done((bf16[48,3456]{1,0:T(8,128)(2,1)S(1)}, bf16[48,3456]{1,0:T(8,128)(2,1)S(1)}, u32[]{:S(2)}, u32[]{:S(2)}) %collective-permute-start.61) | collective-permute-done | bytes 331808 | tf_op jit(solution)/shard_map/ppermute | solution.py:440
  659.8 4.2 collective-permute-done.60
  667.3 5.4 collective-permute-start.48
  672.9 6.6 collective-permute-done.50
  689.7 7.5 %placed.1 = f32[768,1536]{1,0:T(8,128)} custom-call(s32[2]{0:T(128)} %pad_add_fusion.1.ranks_ref, bf16[4,96,1536]{2,1,0:T(8,128)(2,1)} %copy-done.11, bf16[4,96,1536]{2,1,0:T(8,128)(2,1)} %collective-permute-done.70.refs_1_), custom_call_target="tpu_custom_call" | custom-call | tf_op jit(solution)/shard_map/placed/pallas_call | solution.py:643
  697.1 35.3 %collective-permute-done.51.far_a_ref = bf16[4,48,3072]{2,1,0:T(8,128)(2,1)} collective-permute-done((bf16[4,48,3072]{2,1,0:T(8,128)(2,1)}, bf16[4,48,3072]{2,1,0:T(8,128)(2,1)}, u32[]{:S(2)}, u32[]{:S(2)}) %collective-permute-start.51) | collective-permute-done | bytes 1179680 | tf_op jit(solution)/shard_map/ppermute | solution.py:440
  732.4 12.9 %placed_turned.1 = f32[6448,384]{1,0:T(8,128)} custom-call(s32[3]{0:T(128)} %pad_add_fusion.ranks_ref, bf16[4,48,3072]{2,1,0:T(8,128)(2,1)} %pad_maximum_fusion.2.near_a_ref, bf16[4,48,3072]{2,1,0:T(8,128)(2,1)} %collective-permute-done.51.far_a_ref, bf16[4,48,3456]{2,1,0:T(8,128)(2,1)} %copy-done.10, bf16[4,48,3456]{2,1,0:T(8,128)(2,1)} %collective-permute-done.62.far_b_ref), custom_call_target="tpu_custom_call" | custom-call | tf_op jit(solution)/shard_map/placed_turned/pallas_call | solution.py:689
  (418 shorter events, 274.9 us)
Async XLA Ops:
  5.6 38.5 %collective-permute-start.2 = (bf16[5376]{0:T(1024)(128)(2,1)S(1)}, bf16[5376]{0:T(1024)(128)(2,1)}, u32[]{:S(2)}, u32[]{:S(2)}) collective-permute-start(bf16[5376]{0:T(1024)(128)(2,1)S(1)} %pad.4), channel_id=1, source_target_pairs={{0,3},{1,2},{2,1},{3,0},{4,7},{5,6},{6,5},{7,4},{8,11},{9,10},{10,... | collective-permute-start | bytes 32264 | tf_op jit(solution)/shard_map/ppermute | solution.py:440
  6.6 38.4 %collective-permute-start.1 = (bf16[5376]{0:T(1024)(128)(2,1)S(1)}, bf16[5376]{0:T(1024)(128)(2,1)}, u32[]{:S(2)}, u32[]{:S(2)}) collective-permute-start(bf16[5376]{0:T(1024)(128)(2,1)S(1)} %pad.4), channel_id=1, source_target_pairs={{0,2},{1,3},{2,0},{3,1},{4,6},{5,7},{6,4},{7,5},{8,10},{9,11},{10,... | collective-permute-start | bytes 32264 | tf_op jit(solution)/shard_map/ppermute | solution.py:440
  7.2 40.1 %collective-permute-start = (bf16[5376]{0:T(1024)(128)(2,1)S(1)}, bf16[5376]{0:T(1024)(128)(2,1)S(1)}, u32[]{:S(2)}, u32[]{:S(2)}) collective-permute-start(bf16[5376]{0:T(1024)(128)(2,1)S(1)} %pad.4), channel_id=1, source_target_pairs={{0,1},{1,0},{2,3},{3,2},{4,5},{5,4},{6,7},{7,6},{8,9},{9,8},{10,11... | collective-permute-start | bytes 32264 | tf_op jit(solution)/shard_map/ppermute | solution.py:440
  10.6 58.3 %collective-permute-start.3 = (bf16[384,3376]{0,1:T(8,128)(2,1)S(1)}, bf16[384,3376]{0,1:T(8,128)(2,1)}, u32[]{:S(2)}, u32[]{:S(2)}) collective-permute-start(bf16[384,3376]{0,1:T(8,128)(2,1)S(1)} %get-tuple-element.134), channel_id=1, source_target_pairs={{0,1},{1,0},{2,3},{3,2},{4,5},{5,4},{6,7},{7,6},{8,9},{9,8},{10,11... | collective-permute-start | bytes 7778312 | tf_op jit(solution)/shard_map/ppermute | solution.py:440
  21.3 108.5 %collective-permute-start.11 = (bf16[384,3072]{0,1:T(8,128)(2,1)}, bf16[384,3072]{0,1:T(8,128)(2,1)}, u32[]{:S(2)}, u32[]{:S(2)}) collective-permute-start(bf16[384,3072]{0,1:T(8,128)(2,1)} %get-tuple-element.132), channel_id=1, source_target_pairs={{0,1},{1,0},{2,3},{3,2},{4,5},{5,4},{6,7},{7,6},{8,9},{9,8},{10,11... | collective-permute-start | bytes 7077896 | tf_op jit(solution)/shard_map/ppermute | solution.py:440
  44.1 120.1 %collective-permute-start.18 = (bf16[768,1536]{1,0:T(8,128)(2,1)}, bf16[768,1536]{1,0:T(8,128)(2,1)}, u32[]{:S(2)}, u32[]{:S(2)}) collective-permute-start(bf16[768,1536]{1,0:T(8,128)(2,1)} %param.21), channel_id=1, source_target_pairs={{0,1},{1,0},{2,3},{3,2},{4,5},{5,4},{6,7},{7,6},{8,9},{9,8},{10,11... | collective-permute-start | bytes 7077896 | tf_op jit(solution)/shard_map/ppermute | solution.py:440
  47.3 38.6 %collective-permute-start.6 = (bf16[128,3376]{0,1:T(8,128)(2,1)}, bf16[128,3376]{0,1:T(8,128)(2,1)}, u32[]{:S(2)}, u32[]{:S(2)}) collective-permute-start(bf16[128,3376]{0,1:T(8,128)(2,1)} %dynamic_slice.107), channel_id=1, source_target_pairs={{0,2},{1,3},{2,0},{3,1},{4,6},{5,7},{6,4},{7,5},{8,10},{9,11},{10,... | collective-permute-start | bytes 2592776 | tf_op jit(solution)/shard_map/ppermute | solution.py:440
  67.4 60.2 %collective-permute-start.12 = (bf16[128,3072]{0,1:T(8,128)(2,1)}, bf16[128,3072]{0,1:T(8,128)(2,1)}, u32[]{:S(2)}, u32[]{:S(2)}) collective-permute-start(bf16[128,3072]{0,1:T(8,128)(2,1)} %constant_dynamic-slice_fusion.12), channel_id=1, source_target_pairs={{0,2},{1,3},{2,0},{3,1},{4,6},{5,7},{6,4},{7,5},{8,10},{9,11},{10,... | collective-permute-start | bytes 2359304 | tf_op jit(solution)/shard_map/ppermute | solution.py:440
  90.8 37.8 %collective-permute-start.13 = (bf16[128,3072]{0,1:T(8,128)(2,1)S(1)}, bf16[128,3072]{0,1:T(8,128)(2,1)}, u32[]{:S(2)}, u32[]{:S(2)}) collective-permute-start(bf16[128,3072]{0,1:T(8,128)(2,1)S(1)} %copy-done.29), channel_id=1, source_target_pairs={{0,2},{1,3},{2,0},{3,1},{4,6},{5,7},{6,4},{7,5},{8,10},{9,11},{10,... | collective-permute-start | bytes 2359304 | tf_op jit(solution)/shard_map/ppermute | solution.py:440
  127.6 28.9 %collective-permute-start.19 = (bf16[256,1536]{1,0:T(8,128)(2,1)}, bf16[256,1536]{1,0:T(8,128)(2,1)}, u32[]{:S(2)}, u32[]{:S(2)}) collective-permute-start(bf16[256,1536]{1,0:T(8,128)(2,1)} %get-tuple-element.146), channel_id=1, source_target_pairs={{0,2},{1,3},{2,0},{3,1},{4,6},{5,7},{6,4},{7,5},{8,10},{9,11},{10,... | collective-permute-start | bytes 2359304 | tf_op jit(solution)/shard_map/ppermute | solution.py:440
  128.6 35.6 %collective-permute-start.20 = (bf16[256,1536]{1,0:T(8,128)(2,1)}, bf16[256,1536]{1,0:T(8,128)(2,1)}, u32[]{:S(2)}, u32[]{:S(2)}) collective-permute-start(bf16[256,1536]{1,0:T(8,128)(2,1)} %get-tuple-element.145), channel_id=1, source_target_pairs={{0,2},{1,3},{2,0},{3,1},{4,6},{5,7},{6,4},{7,5},{8,10},{9,11},{10,... | collective-permute-start | bytes 2359304 | tf_op jit(solution)/shard_map/ppermute | solution.py:440
  129.7 69.3 %collective-permute-start.14 = (bf16[128,3072]{0,1:T(8,128)(2,1)}, bf16[128,3072]{0,1:T(8,128)(2,1)}, u32[]{:S(2)}, u32[]{:S(2)}) collective-permute-start(bf16[128,3072]{0,1:T(8,128)(2,1)} %collective-permute-done.12), channel_id=1, source_target_pairs={{0,1},{1,0},{2,3},{3,2},{4,5},{5,4},{6,7},{7,6},{8,9},{9,8},{10,11... | collective-permute-start | bytes 2359304 | tf_op jit(solution)/shard_map/ppermute | solution.py:440
  130.3 54.2 %collective-permute-start.16 = (bf16[128,3072]{0,1:T(8,128)(2,1)}, bf16[128,3072]{0,1:T(8,128)(2,1)}, u32[]{:S(2)}, u32[]{:S(2)}) collective-permute-start(bf16[128,3072]{0,1:T(8,128)(2,1)} %collective-permute-done.12), channel_id=1, source_target_pairs={{0,4},{4,0},{8,12},{12,8},{16,20},{20,16},{24,28},{28,24},{1,5},{5... | collective-permute-start | bytes 2359304 | tf_op jit(solution)/shard_map/ppermute | solution.py:440
  164.2 28.6 %collective-permute-start.23 = (bf16[256,1536]{1,0:T(8,128)(2,1)}, bf16[256,1536]{1,0:T(8,128)(2,1)}, u32[]{:S(2)}, u32[]{:S(2)}) collective-permute-start(bf16[256,1536]{1,0:T(8,128)(2,1)} %collective-permute-done.19), channel_id=1, source_target_pairs={{0,4},{4,0},{8,12},{12,8},{16,20},{20,16},{24,28},{28,24},{1,5},{5... | collective-permute-start | bytes 2359304 | tf_op jit(solution)/shard_map/ppermute | solution.py:440
  165.6 31.4 %collective-permute-start.22 = (bf16[256,1536]{1,0:T(8,128)(2,1)}, bf16[256,1536]{1,0:T(8,128)(2,1)}, u32[]{:S(2)}, u32[]{:S(2)}) collective-permute-start(bf16[256,1536]{1,0:T(8,128)(2,1)} %collective-permute-done.20), channel_id=1, source_target_pairs={{0,1},{1,0},{2,3},{3,2},{4,5},{5,4},{6,7},{7,6},{8,9},{9,8},{10,11... | collective-permute-start | bytes 2359304 | tf_op jit(solution)/shard_map/ppermute | solution.py:440
  168.6 41.6 %all-to-all-start = ((f32[8,129,384]{2,1,0:T(8,128)}), f32[8,129,384]{2,1,0:T(8,128)}, u32[]{:S(2)}, u32[]{:S(2)}) async-start(f32[8,129,384]{2,1,0:T(8,128)} %maximum_bitcast_fusion), calls=%async_computation | async-start | bytes 3342336 | tf_op jit(solution)/shard_map/all_to_all | solution.py:417
  184.6 52.5 %collective-permute-start.17 = (bf16[128,3072]{0,1:T(8,128)(2,1)}, bf16[128,3072]{0,1:T(8,128)(2,1)}, u32[]{:S(2)}, u32[]{:S(2)}) collective-permute-start(bf16[128,3072]{0,1:T(8,128)(2,1)} %collective-permute-done.16), channel_id=1, source_target_pairs={{0,1},{1,0},{2,3},{3,2},{4,5},{5,4},{6,7},{7,6},{8,9},{9,8},{10,11... | collective-permute-start | bytes 2359304 | tf_op jit(solution)/shard_map/ppermute | solution.py:440
  192.8 42.2 %collective-permute-start.24 = (bf16[256,1536]{1,0:T(8,128)(2,1)}, bf16[256,1536]{1,0:T(8,128)(2,1)}, u32[]{:S(2)}, u32[]{:S(2)}) collective-permute-start(bf16[256,1536]{1,0:T(8,128)(2,1)} %collective-permute-done.23), channel_id=1, source_target_pairs={{0,1},{1,0},{2,3},{3,2},{4,5},{5,4},{6,7},{7,6},{8,9},{9,8},{10,11... | collective-permute-start | bytes 2359304 | tf_op jit(solution)/shard_map/ppermute | solution.py:440
  223.0 41.2 %all-to-all-start.1 = ((f32[8,128,384]{2,1,0:T(8,128)}), f32[8,128,384]{2,1,0:T(8,128)}, u32[]{:S(2)}, u32[]{:S(2)}) async-start(f32[8,128,384]{2,1,0:T(8,128)} %fusion.31), calls=%async_computation.1 | async-start | bytes 3145728 | tf_op jit(solution)/shard_map/all_to_all | solution.py:430
  283.2 39.2 %all-to-all-start.2 = ((bf16[8,131,384]{2,1,0:T(8,128)(2,1)}), bf16[8,131,384]{2,1,0:T(8,128)(2,1)}, u32[]{:S(2)}, u32[]{:S(2)}) async-start(bf16[8,131,384]{2,1,0:T(8,128)(2,1)} %maximum_bitcast_fusion.1), calls=%async_computation.2 | async-start | bytes 1671168 | tf_op jit(solution)/shard_map/all_to_all | solution.py:417
  293.0 47.4 %collective-permute-start.29 = (bf16[256,1536]{1,0:T(8,128)(2,1)}, bf16[256,1536]{1,0:T(8,128)(2,1)}, u32[]{:S(2)}, u32[]{:S(2)}) collective-permute-start(bf16[256,1536]{1,0:T(8,128)(2,1)} %bitcast.169), channel_id=1, source_target_pairs={{0,1},{1,0},{2,3},{3,2},{4,5},{5,4},{6,7},{7,6},{8,9},{9,8},{10,11... | collective-permute-start | bytes 2359304 | tf_op jit(solution)/shard_map/ppermute | solution.py:440
  309.4 31.0 %collective-permute-start.30 = (bf16[256,1536]{1,0:T(8,128)(2,1)}, bf16[256,1536]{1,0:T(8,128)(2,1)}, u32[]{:S(2)}, u32[]{:S(2)}) collective-permute-start(bf16[256,1536]{1,0:T(8,128)(2,1)} %collective-permute-done.28.refs_5_), channel_id=1, source_target_pairs={{0,1},{1,0},{2,3},{3,2},{4,5},{5,4},{6,7},{7,6},{8,9},{9,8},{10,11... | collective-permute-start | bytes 2359304 | tf_op jit(solution)/shard_map/ppermute | solution.py:440
  309.4 87.8 %collective-permute-start.34 = (bf16[256,3072]{1,0:T(8,128)(2,1)}, bf16[256,3072]{1,0:T(8,128)(2,1)}, u32[]{:S(2)}, u32[]{:S(2)}) collective-permute-start(bf16[256,3072]{1,0:T(8,128)(2,1)} %get-tuple-element.81.refs_4_), channel_id=1, source_target_pairs={{0,2},{1,3},{2,0},{3,1},{4,6},{5,7},{6,4},{7,5},{8,10},{9,11},{10,... | collective-permute-start | bytes 4718600 | tf_op jit(solution)/shard_map/ppermute | solution.py:440
  310.3 88.1 %collective-permute-start.35 = (bf16[256,3072]{1,0:T(8,128)(2,1)}, bf16[256,3072]{1,0:T(8,128)(2,1)}, u32[]{:S(2)}, u32[]{:S(2)}) collective-permute-start(bf16[256,3072]{1,0:T(8,128)(2,1)} %get-tuple-element.81.refs_4_), channel_id=1, source_target_pairs={{0,1},{1,0},{2,3},{3,2},{4,5},{5,4},{6,7},{7,6},{8,9},{9,8},{10,11... | collective-permute-start | bytes 4718600 | tf_op jit(solution)/shard_map/ppermute | solution.py:440
  329.9 56.8 %all-to-all-start.3 = ((bf16[8,128,384]{2,1,0:T(8,128)(2,1)}), bf16[8,128,384]{2,1,0:T(8,128)(2,1)}, u32[]{:S(2)}, u32[]{:S(2)}) async-start(bf16[8,128,384]{2,1,0:T(8,128)(2,1)} %broadcast_dynamic-update-slice_fusion.1), calls=%async_computation.3 | async-start | bytes 1572864 | tf_op jit(solution)/shard_map/all_to_all | solution.py:430
  370.4 40.6 %collective-permute-start.63 = (bf16[384,1536]{1,0:T(8,128)(2,1)}, bf16[384,1536]{1,0:T(8,128)(2,1)}, u32[]{:S(2)}, u32[]{:S(2)}) collective-permute-start(bf16[384,1536]{1,0:T(8,128)(2,1)} %get-tuple-element.91), channel_id=1, source_target_pairs={{0,4},{4,0},{8,12},{12,8},{16,20},{20,16},{24,28},{28,24},{1,5},{5... | collective-permute-start | bytes 3538952 | tf_op jit(solution)/shard_map/ppermute | solution.py:440
  373.9 43.4 %collective-permute-start.31 = (bf16[256,384]{1,0:T(8,128)(2,1)}, bf16[256,384]{1,0:T(8,128)(2,1)}, u32[]{:S(2)}, u32[]{:S(2)}) collective-permute-start(bf16[256,384]{1,0:T(8,128)(2,1)} %get-tuple-element.162), channel_id=1, source_target_pairs={{0,2},{1,3},{2,0},{3,1},{4,6},{5,7},{6,4},{7,5},{8,10},{9,11},{10,... | collective-permute-start | bytes 589832 | tf_op jit(solution)/shard_map/ppermute | solution.py:440
  374.9 42.5 %collective-permute-start.32 = (bf16[256,384]{1,0:T(8,128)(2,1)}, bf16[256,384]{1,0:T(8,128)(2,1)}, u32[]{:S(2)}, u32[]{:S(2)}) collective-permute-start(bf16[256,384]{1,0:T(8,128)(2,1)} %get-tuple-element.161), channel_id=1, source_target_pairs={{0,1},{1,0},{2,3},{3,2},{4,5},{5,4},{6,7},{7,6},{8,9},{9,8},{10,11... | collective-permute-start | bytes 589832 | tf_op jit(solution)/shard_map/ppermute | solution.py:440
  437.1 63.8 %collective-permute-start.66 = (bf16[96,1536]{1,0:T(8,128)(2,1)}, bf16[96,1536]{1,0:T(8,128)(2,1)}, u32[]{:S(2)}, u32[]{:S(2)}) collective-permute-start(bf16[96,1536]{1,0:T(8,128)(2,1)} %get-tuple-element.140), channel_id=1, source_target_pairs={{0,24},{4,28},{8,16},{12,20},{16,8},{20,12},{24,0},{28,4},{1,25},{... | collective-permute-start | bytes 884744 | tf_op jit(solution)/shard_map/ppermute | solution.py:440
  437.4 63.6 %collective-permute-start.65 = (bf16[96,1536]{1,0:T(8,128)(2,1)}, bf16[96,1536]{1,0:T(8,128)(2,1)}, u32[]{:S(2)}, u32[]{:S(2)}) collective-permute-start(bf16[96,1536]{1,0:T(8,128)(2,1)} %get-tuple-element.141), channel_id=1, source_target_pairs={{0,16},{4,20},{8,24},{12,28},{16,0},{20,4},{24,8},{28,12},{1,17},{... | collective-permute-start | bytes 884744 | tf_op jit(solution)/shard_map/ppermute | solution.py:440
  440.9 61.2 %collective-permute-start.64 = (bf16[96,1536]{1,0:T(8,128)(2,1)}, bf16[96,1536]{1,0:T(8,128)(2,1)}, u32[]{:S(2)}, u32[]{:S(2)}) collective-permute-start(bf16[96,1536]{1,0:T(8,128)(2,1)} %get-tuple-element.139), channel_id=1, source_target_pairs={{0,8},{4,12},{8,0},{12,4},{16,24},{20,28},{24,16},{28,20},{1,9},{5... | collective-permute-start | bytes 884744 | tf_op jit(solution)/shard_map/ppermute | solution.py:440
  453.1 40.5 %collective-permute-start.52 = (bf16[256,3456]{1,0:T(8,128)(2,1)}, bf16[256,3456]{1,0:T(8,128)(2,1)}, u32[]{:S(2)}, u32[]{:S(2)}) collective-permute-start(bf16[256,3456]{1,0:T(8,128)(2,1)} %concatenate.61.refs_4_), channel_id=1, source_target_pairs={{0,2},{1,3},{2,0},{3,1},{4,6},{5,7},{6,4},{7,5},{8,10},{9,11},{10,... | collective-permute-start | bytes 5308424 | tf_op jit(solution)/shard_map/ppermute | solution.py:440
  454.2 39.5 %collective-permute-start.53 = (bf16[256,3456]{1,0:T(8,128)(2,1)}, bf16[256,3456]{1,0:T(8,128)(2,1)}, u32[]{:S(2)}, u32[]{:S(2)}) collective-permute-start(bf16[256,3456]{1,0:T(8,128)(2,1)} %concatenate.61.refs_4_), channel_id=1, source_target_pairs={{0,1},{1,0},{2,3},{3,2},{4,5},{5,4},{6,7},{7,6},{8,9},{9,8},{10,11... | collective-permute-start | bytes 5308424 | tf_op jit(solution)/shard_map/ppermute | solution.py:440
  504.2 26.2 %collective-permute-start.68 = (bf16[96,1536]{1,0:T(8,128)(2,1)S(1)}, bf16[96,1536]{1,0:T(8,128)(2,1)S(1)}, u32[]{:S(2)}, u32[]{:S(2)}) collective-permute-start(bf16[96,1536]{1,0:T(8,128)(2,1)S(1)} %add_convert_fusion.2), channel_id=1, source_target_pairs={{0,16},{4,20},{8,24},{12,28},{16,0},{20,4},{24,8},{28,12},{1,17},{... | collective-permute-start | bytes 884744 | tf_op jit(solution)/shard_map/ppermute | solution.py:440
  518.0 29.2 %collective-permute-start.44 = (bf16[192,3072]{1,0:T(8,128)(2,1)}, bf16[192,3072]{1,0:T(8,128)(2,1)S(1)}, u32[]{:S(2)}, u32[]{:S(2)}) collective-permute-start(bf16[192,3072]{1,0:T(8,128)(2,1)} %get-tuple-element.85), channel_id=1, source_target_pairs={{0,4},{4,0},{8,12},{12,8},{16,20},{20,16},{24,28},{28,24},{1,5},{5... | collective-permute-start | bytes 3538952 | tf_op jit(solution)/shard_map/ppermute | solution.py:440
  520.2 55.5 %collective-permute-start.55 = (bf16[192,3456]{1,0:T(8,128)(2,1)}, bf16[192,3456]{1,0:T(8,128)(2,1)S(1)}, u32[]{:S(2)}, u32[]{:S(2)}) collective-permute-start(bf16[192,3456]{1,0:T(8,128)(2,1)} %get-tuple-element.90), channel_id=1, source_target_pairs={{0,4},{4,0},{8,12},{12,8},{16,20},{20,16},{24,28},{28,24},{1,5},{5... | collective-permute-start | bytes 3981320 | tf_op jit(solution)/shard_map/ppermute | solution.py:440
  530.6 159.0 %collective-permute-start.70 = (bf16[4,96,1536]{2,1,0:T(8,128)(2,1)S(1)}, bf16[4,96,1536]{2,1,0:T(8,128)(2,1)}, u32[]{:S(2)}, u32[]{:S(2)}) collective-permute-start(bf16[4,96,1536]{2,1,0:T(8,128)(2,1)S(1)} %pad_maximum_fusion.3.refs_0_), channel_id=1, source_target_pairs={{0,4},{4,0},{8,12},{12,8},{16,20},{20,16},{24,28},{28,24},{1,5},{5... | collective-permute-start | bytes 3538952 | tf_op jit(solution)/shard_map/ppermute | solution.py:440
  538.1 148.4 %collective-permute-start.43 = (f32[1,5348]{1,0:T(1,128)S(1)}, f32[1,5348]{1,0:T(1,128)S(1)}, u32[]{:S(2)}, u32[]{:S(2)}) collective-permute-start(f32[1,5348]{1,0:T(1,128)S(1)} %add.561), channel_id=1, source_target_pairs={{0,4},{4,0},{8,12},{12,8},{16,20},{20,16},{24,28},{28,24},{1,5},{5... | collective-permute-start | bytes 64184 | tf_op jit(solution)/shard_map/ppermute | solution.py:440
  576.0 30.1 %collective-permute-start.58 = (bf16[48,3456]{1,0:T(8,128)(2,1)S(1)}, bf16[48,3456]{1,0:T(8,128)(2,1)S(1)}, u32[]{:S(2)}, u32[]{:S(2)}) collective-permute-start(bf16[48,3456]{1,0:T(8,128)(2,1)S(1)} %get-tuple-element.137), channel_id=1, source_target_pairs={{0,24},{4,28},{8,16},{12,20},{16,8},{20,12},{24,0},{28,4},{1,25},{... | collective-permute-start | bytes 995336 | tf_op jit(solution)/shard_map/ppermute | solution.py:440
  576.6 33.7 %collective-permute-start.57 = (bf16[48,3456]{1,0:T(8,128)(2,1)S(1)}, bf16[48,3456]{1,0:T(8,128)(2,1)S(1)}, u32[]{:S(2)}, u32[]{:S(2)}) collective-permute-start(bf16[48,3456]{1,0:T(8,128)(2,1)S(1)} %get-tuple-element.138), channel_id=1, source_target_pairs={{0,16},{4,20},{8,24},{12,28},{16,0},{20,4},{24,8},{28,12},{1,17},{... | collective-permute-start | bytes 995336 | tf_op jit(solution)/shard_map/ppermute | solution.py:440
  580.4 33.2 %collective-permute-start.56 = (bf16[48,3456]{1,0:T(8,128)(2,1)S(1)}, bf16[48,3456]{1,0:T(8,128)(2,1)S(1)}, u32[]{:S(2)}, u32[]{:S(2)}) collective-permute-start(bf16[48,3456]{1,0:T(8,128)(2,1)S(1)} %get-tuple-element.136), channel_id=1, source_target_pairs={{0,8},{4,12},{8,0},{12,4},{16,24},{20,28},{24,16},{28,20},{1,9},{5... | collective-permute-start | bytes 995336 | tf_op jit(solution)/shard_map/ppermute | solution.py:440
  606.1 26.9 %collective-permute-start.47 = (bf16[48,3072]{1,0:T(8,128)(2,1)S(1)}, bf16[48,3072]{1,0:T(8,128)(2,1)S(1)}, u32[]{:S(2)}, u32[]{:S(2)}) collective-permute-start(bf16[48,3072]{1,0:T(8,128)(2,1)S(1)} %get-tuple-element.143), channel_id=1, source_target_pairs={{0,24},{4,28},{8,16},{12,20},{16,8},{20,12},{24,0},{28,4},{1,25},{... | collective-permute-start | bytes 884744 | tf_op jit(solution)/shard_map/ppermute | solution.py:440
  610.2 26.1 %collective-permute-start.46 = (bf16[48,3072]{1,0:T(8,128)(2,1)S(1)}, bf16[48,3072]{1,0:T(8,128)(2,1)S(1)}, u32[]{:S(2)}, u32[]{:S(2)}) collective-permute-start(bf16[48,3072]{1,0:T(8,128)(2,1)S(1)} %get-tuple-element.144), channel_id=1, source_target_pairs={{0,16},{4,20},{8,24},{12,28},{16,0},{20,4},{24,8},{28,12},{1,17},{... | collective-permute-start | bytes 884744 | tf_op jit(solution)/shard_map/ppermute | solution.py:440
  632.9 26.9 %collective-permute-start.61 = (bf16[48,3456]{1,0:T(8,128)(2,1)S(1)}, bf16[48,3456]{1,0:T(8,128)(2,1)S(1)}, u32[]{:S(2)}, u32[]{:S(2)}) collective-permute-start(bf16[48,3456]{1,0:T(8,128)(2,1)S(1)} %add_convert_fusion.1), channel_id=1, source_target_pairs={{0,24},{4,28},{8,16},{12,20},{16,8},{20,12},{24,0},{28,4},{1,25},{... | collective-permute-start | bytes 995336 | tf_op jit(solution)/shard_map/ppermute | solution.py:440
  636.3 27.6 %collective-permute-start.60 = (bf16[48,3456]{1,0:T(8,128)(2,1)S(1)}, bf16[48,3456]{1,0:T(8,128)(2,1)S(1)}, u32[]{:S(2)}, u32[]{:S(2)}) collective-permute-start(bf16[48,3456]{1,0:T(8,128)(2,1)S(1)} %add_convert_fusion.1), channel_id=1, source_target_pairs={{0,16},{4,20},{8,24},{12,28},{16,0},{20,4},{24,8},{28,12},{1,17},{... | collective-permute-start | bytes 995336 | tf_op jit(solution)/shard_map/ppermute | solution.py:440
  639.7 27.6 %collective-permute-start.59 = (bf16[48,3456]{1,0:T(8,128)(2,1)S(1)}, bf16[48,3456]{1,0:T(8,128)(2,1)S(1)}, u32[]{:S(2)}, u32[]{:S(2)}) collective-permute-start(bf16[48,3456]{1,0:T(8,128)(2,1)S(1)} %add_convert_fusion.1), channel_id=1, source_target_pairs={{0,8},{4,12},{8,0},{12,4},{16,24},{20,28},{24,16},{28,20},{1,9},{5... | collective-permute-start | bytes 995336 | tf_op jit(solution)/shard_map/ppermute | solution.py:440
  679.5 52.9 %collective-permute-start.62 = (bf16[4,48,3456]{2,1,0:T(8,128)(2,1)S(1)}, bf16[4,48,3456]{2,1,0:T(8,128)(2,1)}, u32[]{:S(2)}, u32[]{:S(2)}) collective-permute-start(bf16[4,48,3456]{2,1,0:T(8,128)(2,1)S(1)} %pad_maximum_fusion.1.near_b_ref), channel_id=1, source_target_pairs={{0,4},{4,0},{8,12},{12,8},{16,20},{20,16},{24,28},{28,24},{1,5},{5... | collective-permute-start | bytes 3981320 | tf_op jit(solution)/shard_map/ppermute | solution.py:440
  683.3 49.1 %collective-permute-start.51 = (bf16[4,48,3072]{2,1,0:T(8,128)(2,1)}, bf16[4,48,3072]{2,1,0:T(8,128)(2,1)}, u32[]{:S(2)}, u32[]{:S(2)}) collective-permute-start(bf16[4,48,3072]{2,1,0:T(8,128)(2,1)} %pad_maximum_fusion.2.near_a_ref), channel_id=1, source_target_pairs={{0,4},{4,0},{8,12},{12,8},{16,20},{20,16},{24,28},{28,24},{1,5},{5... | collective-permute-start | bytes 3538952 | tf_op jit(solution)/shard_map/ppermute | solution.py:440
  (82 other events, 1117.2 us)

commit v3 on v2

--- a/solution.py
+++ b/solution.py
@@ -495,7 +495,8 @@
     return swapped(shard, axis, 1), arrived, direct
 
 
-def weight_gathered(shard, sent, axis, side):
+def weight_gathered(shard, sent, axis, side, earlier=None):
+    held_for = (lambda block: block) if earlier is None else (lambda block: after(block, earlier))
     count, rank = lax.axis_size(axis), lax.axis_index(axis)
     rows = shard.shape[0]
     offsets, sizes = weight_parts(shard, side)
@@ -511,14 +512,15 @@
             held[flip ^ mask] = (arrived, direct, swapped(arrived, side, 1))
         mask //= 2
     for flip, block in ((0, shard), (1, sent[0])):
-        whole = lax.dynamic_update_slice_in_dim(whole, block, (rank ^ flip) * rows, 0)
+        whole = lax.dynamic_update_slice_in_dim(whole, held_for(block), (rank ^ flip) * rows, 0)
     for flip, blocks in held.items():
         if flip:
             for block, offset in zip(blocks, offsets):
                 start = (rank ^ flip) * rows + offset
-                whole = lax.dynamic_update_slice_in_dim(whole, block, start, 0)
+                near = swapped(block, axis, 1)
+                whole = lax.dynamic_update_slice_in_dim(whole, held_for(block), start, 0)
                 start = (rank ^ flip ^ 1) * rows + offset
-                whole = lax.dynamic_update_slice_in_dim(whole, swapped(block, axis, 1), start, 0)
+                whole = lax.dynamic_update_slice_in_dim(whole, held_for(near), start, 0)
     return whole
 
 
@@ -786,7 +788,6 @@
     raw_t = stepped[:, conv_width:].T.astype(F32)
     rim_rows = passed_along(conv_in[tokens - taps + 1 :], "seq", 1)
     gate_sent = after(gate_sent, rim_rows)
-    w_gate = weight_gathered(gate_shard, gate_sent, "fsdp", "seq")
     padded = jnp.concatenate([rim_rows, conv_in], 0).astype(F32)
     pre_act = b_conv[None, :]
     for tap in range(taps):
@@ -813,11 +814,12 @@
     total_lanes = jnp.repeat(total_log, head_width)
 
     own_state = local_state(x_rows, b_rows.T, to_end, head_width)
-    home, _ = carried_states(own_state, total_lanes, "seq", False)
+    home, entering = carried_states(own_state, total_lanes, "seq", False)
     state_full = joined(home)
     state_in = host_halves(state_full)
     inner = inner_part(after(x_rows, own_state), b_rows, c_rows, decay_log, source_log, head_width)
-    out_sent = after(out_sent, inner)
+    out_sent = after(out_sent, (inner, entering))
+    w_gate = weight_gathered(gate_shard, gate_sent, "fsdp", "seq", entering)
     w_out = weight_gathered(out_weight, out_sent, "fsdp", "seq")
     sent = out_sent[-1]
     gate_in = plain_dot(normed_b, w_gate).astype(BF16)
@@ -895,18 +897,20 @@
     spare = jnp.zeros((tokens, -(conv_width + heads) % LANES), BF16)
     d_step_proj = jnp.concatenate([d_conv_in.astype(BF16), d_raw.T.astype(BF16), spare], 1)
     block_out = hidden_f + plain_dot(after(gated_b, d_step_proj), w_out)
-    d_step_all = passed_on(gathered(d_step_proj, "fsdp"), "fsdp", block_out)
+    d_pre = after(d_pre, d_step_proj)
+    grad_w_conv = jnp.stack(
+        [jnp.sum(d_pre * padded[tap : tap + tokens], axis=0) for tap in range(taps)]
+    )
+    grad_b_conv = jnp.sum(d_pre, axis=0)
+    d_step_all = passed_on(
+        gathered(d_step_proj, "fsdp"), "fsdp", (block_out, grad_w_conv, grad_b_conv)
+    )
     out_spread = seq_spread(seq_owned(out_near, out_arrived, "seq"), "seq")
     gate_arrived = after(gate_arrived, d_step_proj)
     gate_spread = seq_spread(seq_owned(gate_near, gate_arrived, "seq"), "seq")
     step_near, step_away = weight_product(normed_all, d_step_all, "seq")
     step_arrived = swapped(step_away, "seq", 1)
     step_spread = seq_spread(seq_owned(step_near, step_arrived, "seq"), "seq")
-    d_pre = after(d_pre, d_step_proj)
-    grad_w_conv = jnp.stack(
-        [jnp.sum(d_pre * padded[tap : tap + tokens], axis=0) for tap in range(taps)]
-    )
-    grad_b_conv = jnp.sum(d_pre, axis=0)
     d_normed = against_cols(after(d_gate, d_step_proj), w_gate)
     d_normed = d_normed + against_cols(d_step_proj[:, : conv_width + heads], w_conv_in)
     d_unit = d_normed * gain_n
@@ -931,6 +935,7 @@
     for part in by_owner:
         outs.append(mine[cursor : cursor + part.shape[1]])
         cursor += part.shape[1]
+    grad_w_out = placed((out_spread,), "seq", model)
     return (
         block_out[None],
         grad_hidden[None],
@@ -942,7 +947,7 @@
         outs[4],
         outs[5],
         outs[1],
-        placed((out_spread,), "seq", model),
+        grad_w_out,
     )
 
 

time: 758 us -> 743 us (0.980)
  waiting for transfers between devices: 269 us -> 254 us
  starting transfers between devices: 110 us -> 118 us
  matrix products: 54.7 us -> 47.1 us
    all_to_all x2, starting transfers between devices: 12.8 us -> 22.9 us  [carried_states(): held = lax.all_to_all(split, axis, split_axis=0, concat_axis=0, tiled=True)]
    dot_general x8, matrix products: 52.1 us -> 43.9 us  [dims(): lax.dot_general(left, right, (contract, ((), ())), preferred_element_type...]
    dynamic_update_slice x22 -> x23, local copies, waits for them, and re-layouts: 46.2 us -> 41.4 us  [the longest x9 15.7 us: weight_gathered(): whole = lax.dynamic_update_slice_in_dim(whole, held_for(block), start, 0)]
  transfers between devices with their start and end apart: 75 -> 75, of which waited for: 26 -> 24; matrix products, arithmetic and copies ran while one was open for 33% -> 33% of each run, Pallas kernels for 8% -> 8%
where the time goes in v3:
time: 743 us; the launch traced here: 731 us
  waiting for transfers between devices  254 us (34%)
  local copies, waits for them, and re-layouts  134 us (18%)
  starting transfers between devices  118 us (16%)
  Pallas kernels  95.7 us (13%)
  other arithmetic  79.7 us (11%)
  matrix products  47.1 us (6%)
    ppermute x69, waiting for transfers between devices, swapped(): lax.ppermute(value, axis, [(source, source ^ mask) for source in range(co...  254 us
    ppermute x69, starting transfers between devices, swapped(): lax.ppermute(value, axis, [(source, source ^ mask) for source in range(co...  76.1 us
    dot_general x8, matrix products, dims(): lax.dot_general(left, right, (contract, ((), ())), preferred_element_type...  43.9 us
    pallas_call x3, Pallas kernels, weight_product(): pl.pallas_call(product_kernel, out_shape=(jax.ShapeDtypeStruct((rows // 2...  26.3 us
    all_to_all x2, starting transfers between devices, carried_states(): held = lax.all_to_all(split, axis, split_axis=0, concat_axis=0, tiled=True)  22.9 us
    dynamic_update_slice x9, local copies, waits for them, and re-layouts, weight_gathered(): whole = lax.dynamic_update_slice_in_dim(whole, held_for(block), start, 0)  15.7 us
  transfers between devices with their start and end apart: 75, of which 24 were waited for; matrix products, arithmetic and copies ran while one was open for 33% of the time, Pallas kernels for 8%

profile of v3, /device:TPU:16, one launch (start us, length us, event | category | flops | bytes accessed | tf_op | source)
XLA Modules:
  0.0 730.6 jit_solution(11780215423725604285)
XLA Ops:
  1.4 4.1 concatenate.48
  7.5 5.1 broadcast_in_dim.46
  39.6 7.7 %collective-permute-done.4 = bf16[128,3376]{0,1:T(8,128)(2,1)} collective-permute-done((bf16[128,3376]{0,1:T(8,128)(2,1)}, bf16[128,3376]{0,1:T(8,128)(2,1)}, u32[]{:S(2)}, u32[]{:S(2)}) %collective-permute-start.4) | collective-permute-done | bytes 864288 | tf_op jit(solution)/shard_map/ppermute | solution.py:440
  54.8 11.0 %collective-permute-done.6 = bf16[128,3376]{0,1:T(8,128)(2,1)} collective-permute-done((bf16[128,3376]{0,1:T(8,128)(2,1)}, bf16[128,3376]{0,1:T(8,128)(2,1)}, u32[]{:S(2)}, u32[]{:S(2)}) %collective-permute-start.6) | collective-permute-done | bytes 864288 | tf_op jit(solution)/shard_map/ppermute | solution.py:440
  71.2 14.8 %collective-permute-done.8 = bf16[128,3376]{0,1:T(8,128)(2,1)S(1)} collective-permute-done((bf16[128,3376]{0,1:T(8,128)(2,1)}, bf16[128,3376]{0,1:T(8,128)(2,1)S(1)}, u32[]{:S(2)}, u32[]{:S(2)}) %collective-permute-start.8) | collective-permute-done | bytes 864288 | tf_op jit(solution)/shard_map/ppermute | solution.py:440
  89.4 7.0 convolution_convert_fusion
  114.1 7.0 local_state.1
  124.0 16.5 %all-to-all-start = ((f32[8,129,384]{2,1,0:T(8,128)}), f32[8,129,384]{2,1,0:T(8,128)}, u32[]{:S(2)}, u32[]{:S(2)}) async-start(f32[8,129,384]{2,1,0:T(8,128)} %maximum_bitcast_fusion), calls=%async_computation | async-start | bytes 3342336 | tf_op jit(solution)/shard_map/all_to_all | solution.py:417
  144.2 4.4 broadcast_in_dim.52
  171.1 8.6 %inner_part.1.inner_ref = f32[256,3072]{1,0:T(8,128)} custom-call(bf16[256,3072]{1,0:T(8,128)(2,1)} %slice.333.x_ref, bf16[256,128]{1,0:T(8,128)(2,1)} %get-tuple-element.167.b_ref, bf16[256,128]{1,0:T(8,128)(2,1)} %get-tuple-element.165.c_ref, f32[48,256]{1,0:T(8,128)} %copy-done.32, f32[48,256]{1,0:T(8,128)} %copy.101.source_ref), custom_call_target="tpu_custom_call" | custom-call | tf_op jit(solution)/shard_map/inner_part/pallas_call | solution.py:132
  185.8 5.0 collective-permute-done.16
  198.5 6.7 all-to-all-start.1
  218.3 4.2 convolution_convert_fusion.1.gate_ref
  237.5 8.0 %convolution_bitcast_fusion.dgated_ref = f32[256,3072]{1,0:T(8,128)} fusion(bf16[3072,1536]{1,0:T(8,128)(2,1)} %constant_dynamic-update-slice_fusion.3, bf16[1,256,1536]{2,1,0:T(8,128)(2,1)S(1)} %copy-done.13), kind=kOutput, calls=%fused_computation.3 | convolution fusion | flops 2415919104 | bytes 13369344 | tf_op jit(solution)/shard_map/dot_general | solution.py:21
  248.5 13.3 %middle.1 = (bf16[256,3072]{1,0:T(8,128)(2,1)}, bf16[256,3072]{1,0:T(8,128)(2,1)}, bf16[256,3072]{1,0:T(8,128)(2,1)}, f32[128,3072]{1,0:T(8,128)}, f32[256,48]{1...) custom-call(f32[256,3072]{1,0:T(8,128)} %inner_part.1.inner_ref, bf16[256,3072]{1,0:T(8,128)(2,1)} %slice.333.x_ref, ...), custom_call_target="tpu_custom_call" | custom-call | tf_op jit(solution)/shard_map/middle/pallas_call | solution.py:210
  264.5 6.4 all-to-all-start.2
  273.4 17.5 %collective-permute-done.28.refs_5_ = bf16[256,1536]{1,0:T(8,128)(2,1)} collective-permute-done((bf16[256,1536]{1,0:T(8,128)(2,1)}, bf16[256,1536]{1,0:T(8,128)(2,1)}, u32[]{:S(2)}, u32[]{:S(2)}) %collective-permute-start.28) | collective-permute-done | bytes 786464 | tf_op jit(solution)/shard_map/ppermute | solution.py:440
  292.1 11.8 %inner_grad.1 = (f32[256,3072]{1,0:T(8,128)}, f32[256,256]{1,0:T(8,128)}, f32[256,128]{1,0:T(8,128)}) custom-call(bf16[256,3072]{1,0:T(8,128)(2,1)} %slice.333.x_ref, bf16[256,3072]{1,0:T(8,128)(2,1)} %get-tuple-element.76.dy_ref, bf16[256,128]{1,0:T(8,128)(2,1)} %get-tuple-element.167.b_ref, bf16[256,128]{1,0:T(8,128)(2,1)} %get-tuple-element.165.c_ref, ...), custom_call_target="tpu_custom_call" | custom-call | tf_op jit(solution)/shard_map/inner_grad/pallas_call | solution.py:311
  311.4 6.2 all-to-all-start.3
  325.3 11.6 %collective-permute-done.25.refs_1_ = bf16[256,768]{1,0:T(8,128)(2,1)} collective-permute-done((bf16[256,768]{1,0:T(8,128)(2,1)}, bf16[256,768]{1,0:T(8,128)(2,1)}, u32[]{:S(2)}, u32[]{:S(2)}) %collective-permute-start.25) | collective-permute-done | bytes 393248 | tf_op jit(solution)/shard_map/ppermute | solution.py:440
  336.9 7.5 %collective-permute-done.27.refs_3_ = bf16[256,768]{1,0:T(8,128)(2,1)} collective-permute-done((bf16[256,768]{1,0:T(8,128)(2,1)}, bf16[256,768]{1,0:T(8,128)(2,1)}, u32[]{:S(2)}, u32[]{:S(2)}) %collective-permute-start.27) | collective-permute-done | bytes 393248 | tf_op jit(solution)/shard_map/ppermute | solution.py:440
  344.4 7.4 %weight_product.3 = (f32[384,1536]{1,0:T(8,128)}, bf16[384,1536]{1,0:T(8,128)(2,1)}) custom-call(s32[1]{0:T(128)} %bitcast.13.place_ref, bf16[256,768]{1,0:T(8,128)(2,1)} %get-tuple-element.171.refs_0_, bf16[256,768]{1,0:T(8,128)(2,1)} %collective-permute-done.25.refs_1_, bf16[256,768]{1,0:T(8,128)(2,1)} %collective-permute-done.26.refs_2_, ...), custom_call_target="tpu_custom_call" | custom-call | tf_op jit(solution)/shard_map/weight_product/pallas_call | solution.py:572
  370.3 8.4 %outer_grad.1 = (bf16[256,3072]{1,0:T(8,128)(2,1)}, f32[256,48]{1,0:T(8,128)}, f32[256,48]{1,0:T(8,128)}, f32[256,128]{1,0:T(8,128)}) custom-call(f32[256,3072]{1,0:T(8,128)} %get-tuple-element.77.inner_ref, bf16[256,3072]{1,0:T(8,128)(2,1)} %slice.333.x_ref, bf16[256,3072]{1,0:T(8,128)(2,1)} %get-tuple-element.76.dy_ref, ...), custom_call_target="tpu_custom_call" | custom-call | tf_op jit(solution)/shard_map/outer_grad/pallas_call | solution.py:372
  398.8 8.8 %weight_product.4 = (f32[192,3072]{1,0:T(8,128)}, bf16[192,3072]{1,0:T(8,128)(2,1)}) custom-call(s32[1]{0:T(128)} %bitcast.13.place_ref, bf16[256,384]{1,0:T(8,128)(2,1)} %get-tuple-element.177.refs_0_, bf16[256,384]{1,0:T(8,128)(2,1)} %collective-permute-done.31.refs_1_, bf16[256,384]{1,0:T(8,128)(2,1)} %collective-permute-done.32.refs_2_, ...), custom_call_target="tpu_custom_call" | custom-call | tf_op jit(solution)/shard_map/weight_product/pallas_call | solution.py:572
  422.5 7.8 %fusion.5 = bf16[256,3328]{1,0:T(8,128)(2,1)} fusion(f32[3,3328]{1,0:T(4,128)} %collective-permute-done.37, f32[256,3328]{1,0:T(8,128)} %copy-done, f32[3328]{0:T(1024)S(1)} %mul.480, f32[3328]{0:T(1024)} %mul.477, f32[3328]{0:T(1024)} %mul.474, f32[3328]{0:T(1024)} %mul.471), kind=kLoop, calls=%fused_computation.10 | loop fusion | flops 9371648 | bytes 5204992 | tf_op jit(solution)/shard_map/convert_element_type | solution.py:898
  435.7 3.9 multiply_reduce_fusion.3
  439.6 5.3 fusion.86
  445.0 7.5 %convolution_add_fusion = f32[256,1536]{1,0:T(8,128)} fusion(bf16[256,3072]{1,0:T(8,128)(2,1)S(1)} %copy-done.19, bf16[3072,1536]{1,0:T(8,128)(2,1)} %constant_dynamic-update-slice_fusion.3, bf16[1,256,1536]{2,1,0:T(8,128)(2,1)S(1)} %copy-done.6), kind=kOutput, calls=%fused_computation.23 | convolution fusion | flops 2416705536 | bytes 13369344 | tf_op jit(solution)/shard_map/dot_general | solution.py:21
  452.6 22.6 %collective-permute-done.52.refs_5_ = bf16[256,3456]{1,0:T(8,128)(2,1)} collective-permute-done((bf16[256,3456]{1,0:T(8,128)(2,1)}, bf16[256,3456]{1,0:T(8,128)(2,1)}, u32[]{:S(2)}, u32[]{:S(2)}) %collective-permute-start.52) | collective-permute-done | bytes 1769504 | tf_op jit(solution)/shard_map/ppermute | solution.py:440
  475.4 8.2 %fusion.23 = (f32[1536]{0:T(1024)S(1)}, f32[256]{0:T(256)S(1)}, f32[256,1536]{1,0:T(8,128)}) fusion(bf16[1,256,1536]{2,1,0:T(8,128)(2,1)S(1)} %copy-done.6, f32[256]{0:T(256)S(1)} %copy-done.56, f32[1536]{0:T(1024)S(1)} %copy-done.43, f32[256,1536]{1,0:T(8,128)S(1)} %fusion.86, bf16[1536,3376]{0,1:T(8,128)(2,1)} %constant_dynamic-update-slice_fusion.19, ...), kind=kOutput, calls=%fused_computation.48 | convolution fusion | flops 2661595392 | bytes 16046080 | tf_op jit(solution)/shard_map/dot_general | solution.py:21
  493.0 10.0 %weight_product.5 = (f32[192,3456]{1,0:T(8,128)}, bf16[192,3456]{1,0:T(8,128)(2,1)}) custom-call(s32[1]{0:T(128)} %bitcast.13.place_ref, bf16[256,384]{1,0:T(8,128)(2,1)} %get-tuple-element.177.refs_0_, bf16[256,384]{1,0:T(8,128)(2,1)} %collective-permute-done.31.refs_1_, bf16[256,384]{1,0:T(8,128)(2,1)} %collective-permute-done.32.refs_2_, ...), custom_call_target="tpu_custom_call" | custom-call | tf_op jit(solution)/shard_map/weight_product/pallas_call | solution.py:572
  506.8 4.6 collective-permute-done.69
  511.5 4.2 collective-permute-done.68
  525.4 6.9 collective-permute-done.44
  532.5 28.2 %collective-permute-done.55 = bf16[192,3456]{1,0:T(8,128)(2,1)S(1)} collective-permute-done((bf16[192,3456]{1,0:T(8,128)(2,1)}, bf16[192,3456]{1,0:T(8,128)(2,1)S(1)}, u32[]{:S(2)}, u32[]{:S(2)}) %collective-permute-start.55) | collective-permute-done | bytes 1327136 | tf_op jit(solution)/shard_map/ppermute | solution.py:440
  561.6 3.8 collective-permute-start.57
  565.6 25.6 %collective-permute-done.58 = bf16[48,3456]{1,0:T(8,128)(2,1)S(1)} collective-permute-done((bf16[48,3456]{1,0:T(8,128)(2,1)S(1)}, bf16[48,3456]{1,0:T(8,128)(2,1)S(1)}, u32[]{:S(2)}, u32[]{:S(2)}) %collective-permute-start.58) | collective-permute-done | bytes 331808 | tf_op jit(solution)/shard_map/ppermute | solution.py:440
  591.2 4.2 collective-permute-done.57
  598.7 5.4 collective-permute-start.45
  604.3 13.8 %collective-permute-done.47 = bf16[48,3072]{1,0:T(8,128)(2,1)S(1)} collective-permute-done((bf16[48,3072]{1,0:T(8,128)(2,1)S(1)}, bf16[48,3072]{1,0:T(8,128)(2,1)S(1)}, u32[]{:S(2)}, u32[]{:S(2)}) %collective-permute-start.47) | collective-permute-done | bytes 294944 | tf_op jit(solution)/shard_map/ppermute | solution.py:440
  624.8 6.2 collective-permute-start.59
  631.1 13.8 %collective-permute-done.61 = bf16[48,3456]{1,0:T(8,128)(2,1)S(1)} collective-permute-done((bf16[48,3456]{1,0:T(8,128)(2,1)S(1)}, bf16[48,3456]{1,0:T(8,128)(2,1)S(1)}, u32[]{:S(2)}, u32[]{:S(2)}) %collective-permute-start.61) | collective-permute-done | bytes 331808 | tf_op jit(solution)/shard_map/ppermute | solution.py:440
  644.9 4.2 collective-permute-done.60
  652.4 5.4 collective-permute-start.48
  658.0 6.6 collective-permute-done.50
  673.7 7.5 %placed.1 = f32[768,1536]{1,0:T(8,128)} custom-call(s32[2]{0:T(128)} %pad_add_fusion.1.ranks_ref, bf16[4,96,1536]{2,1,0:T(8,128)(2,1)} %pad_maximum_fusion.3.refs_0_, bf16[4,96,1536]{2,1,0:T(8,128)(2,1)} %collective-permute-done.70.refs_1_), custom_call_target="tpu_custom_call" | custom-call | tf_op jit(solution)/shard_map/placed/pallas_call | solution.py:645
  681.2 36.3 %collective-permute-done.51.far_a_ref = bf16[4,48,3072]{2,1,0:T(8,128)(2,1)} collective-permute-done((bf16[4,48,3072]{2,1,0:T(8,128)(2,1)S(1)}, bf16[4,48,3072]{2,1,0:T(8,128)(2,1)}, u32[]{:S(2)}, u32[]{:S(2)}) %collective-permute-start.51) | collective-permute-done | bytes 1179680 | tf_op jit(solution)/shard_map/ppermute | solution.py:440
  717.5 12.9 %placed_turned.1 = f32[6448,384]{1,0:T(8,128)} custom-call(s32[3]{0:T(128)} %pad_add_fusion.ranks_ref, bf16[4,48,3072]{2,1,0:T(8,128)(2,1)} %copy-done.10, bf16[4,48,3072]{2,1,0:T(8,128)(2,1)} %collective-permute-done.51.far_a_ref, bf16[4,48,3456]{2,1,0:T(8,128)(2,1)} %copy-done.9, bf16[4,48,3456]{2,1,0:T(8,128)(2,1)} %collective-permute-done.62.far_b_ref), custom_call_target="tpu_custom_call" | custom-call | tf_op jit(solution)/shard_map/placed_turned/pallas_call | solution.py:691
  (439 shorter events, 265.0 us)
Async XLA Ops:
  14.6 34.2 %collective-permute-start.3 = (bf16[384,3376]{0,1:T(8,128)(2,1)S(1)}, bf16[384,3376]{0,1:T(8,128)(2,1)}, u32[]{:S(2)}, u32[]{:S(2)}) collective-permute-start(bf16[384,3376]{0,1:T(8,128)(2,1)S(1)} %get-tuple-element.148), channel_id=1, source_target_pairs={{0,1},{1,0},{2,3},{3,2},{4,5},{5,4},{6,7},{7,6},{8,9},{9,8},{10,11... | collective-permute-start | bytes 7778312 | tf_op jit(solution)/shard_map/ppermute | solution.py:440
  16.6 152.9 %collective-permute-start.11 = (bf16[384,3072]{0,1:T(8,128)(2,1)}, bf16[384,3072]{0,1:T(8,128)(2,1)}, u32[]{:S(2)}, u32[]{:S(2)}) collective-permute-start(bf16[384,3072]{0,1:T(8,128)(2,1)} %slice.270), channel_id=1, source_target_pairs={{0,1},{1,0},{2,3},{3,2},{4,5},{5,4},{6,7},{7,6},{8,9},{9,8},{10,11... | collective-permute-start | bytes 7077896 | tf_op jit(solution)/shard_map/ppermute | solution.py:440
  24.9 22.4 %collective-permute-start.4 = (bf16[128,3376]{0,1:T(8,128)(2,1)}, bf16[128,3376]{0,1:T(8,128)(2,1)}, u32[]{:S(2)}, u32[]{:S(2)}) collective-permute-start(bf16[128,3376]{0,1:T(8,128)(2,1)} %constant_dynamic-slice_fusion.13), channel_id=1, source_target_pairs={{0,2},{1,3},{2,0},{3,1},{4,6},{5,7},{6,4},{7,5},{8,10},{9,11},{10,... | collective-permute-start | bytes 2592776 | tf_op jit(solution)/shard_map/ppermute | solution.py:440
  26.5 39.3 %collective-permute-start.6 = (bf16[128,3376]{0,1:T(8,128)(2,1)}, bf16[128,3376]{0,1:T(8,128)(2,1)}, u32[]{:S(2)}, u32[]{:S(2)}) collective-permute-start(bf16[128,3376]{0,1:T(8,128)(2,1)} %dynamic_slice.107), channel_id=1, source_target_pairs={{0,2},{1,3},{2,0},{3,1},{4,6},{5,7},{6,4},{7,5},{8,10},{9,11},{10,... | collective-permute-start | bytes 2592776 | tf_op jit(solution)/shard_map/ppermute | solution.py:440
  27.0 141.5 %collective-permute-start.12 = (bf16[128,3072]{0,1:T(8,128)(2,1)}, bf16[128,3072]{0,1:T(8,128)(2,1)}, u32[]{:S(2)}, u32[]{:S(2)}) collective-permute-start(bf16[128,3072]{0,1:T(8,128)(2,1)} %constant_dynamic-slice_fusion.12), channel_id=1, source_target_pairs={{0,2},{1,3},{2,0},{3,1},{4,6},{5,7},{6,4},{7,5},{8,10},{9,11},{10,... | collective-permute-start | bytes 2359304 | tf_op jit(solution)/shard_map/ppermute | solution.py:440
  47.3 122.3 %collective-permute-start.13 = (bf16[128,3072]{0,1:T(8,128)(2,1)}, bf16[128,3072]{0,1:T(8,128)(2,1)}, u32[]{:S(2)}, u32[]{:S(2)}) collective-permute-start(bf16[128,3072]{0,1:T(8,128)(2,1)} %dynamic_slice.109), channel_id=1, source_target_pairs={{0,2},{1,3},{2,0},{3,1},{4,6},{5,7},{6,4},{7,5},{8,10},{9,11},{10,... | collective-permute-start | bytes 2359304 | tf_op jit(solution)/shard_map/ppermute | solution.py:440
  65.8 20.2 %collective-permute-start.8 = (bf16[128,3376]{0,1:T(8,128)(2,1)}, bf16[128,3376]{0,1:T(8,128)(2,1)S(1)}, u32[]{:S(2)}, u32[]{:S(2)}) collective-permute-start(bf16[128,3376]{0,1:T(8,128)(2,1)} %collective-permute-done.4), channel_id=1, source_target_pairs={{0,4},{4,0},{8,12},{12,8},{16,20},{20,16},{24,28},{28,24},{1,5},{5... | collective-permute-start | bytes 2592776 | tf_op jit(solution)/shard_map/ppermute | solution.py:440
  70.7 127.0 %collective-permute-start.18 = (bf16[768,1536]{1,0:T(8,128)(2,1)}, bf16[768,1536]{1,0:T(8,128)(2,1)}, u32[]{:S(2)}, u32[]{:S(2)}) collective-permute-start(bf16[768,1536]{1,0:T(8,128)(2,1)} %param.21), channel_id=1, source_target_pairs={{0,1},{1,0},{2,3},{3,2},{4,5},{5,4},{6,7},{7,6},{8,9},{9,8},{10,11... | collective-permute-start | bytes 7077896 | tf_op jit(solution)/shard_map/ppermute | solution.py:440
  124.0 55.7 %all-to-all-start = ((f32[8,129,384]{2,1,0:T(8,128)}), f32[8,129,384]{2,1,0:T(8,128)}, u32[]{:S(2)}, u32[]{:S(2)}) async-start(f32[8,129,384]{2,1,0:T(8,128)} %maximum_bitcast_fusion), calls=%async_computation | async-start | bytes 3342336 | tf_op jit(solution)/shard_map/all_to_all | solution.py:417
  143.1 42.5 %collective-permute-start.19 = (bf16[256,1536]{1,0:T(8,128)(2,1)}, bf16[256,1536]{1,0:T(8,128)(2,1)}, u32[]{:S(2)}, u32[]{:S(2)}) collective-permute-start(bf16[256,1536]{1,0:T(8,128)(2,1)} %get-tuple-element.160), channel_id=1, source_target_pairs={{0,2},{1,3},{2,0},{3,1},{4,6},{5,7},{6,4},{7,5},{8,10},{9,11},{10,... | collective-permute-start | bytes 2359304 | tf_op jit(solution)/shard_map/ppermute | solution.py:440
  168.5 29.1 %collective-permute-start.20 = (bf16[256,1536]{1,0:T(8,128)(2,1)}, bf16[256,1536]{1,0:T(8,128)(2,1)}, u32[]{:S(2)}, u32[]{:S(2)}) collective-permute-start(bf16[256,1536]{1,0:T(8,128)(2,1)} %get-tuple-element.159), channel_id=1, source_target_pairs={{0,2},{1,3},{2,0},{3,1},{4,6},{5,7},{6,4},{7,5},{8,10},{9,11},{10,... | collective-permute-start | bytes 2359304 | tf_op jit(solution)/shard_map/ppermute | solution.py:440
  169.5 35.7 %collective-permute-start.14 = (bf16[128,3072]{0,1:T(8,128)(2,1)}, bf16[128,3072]{0,1:T(8,128)(2,1)}, u32[]{:S(2)}, u32[]{:S(2)}) collective-permute-start(bf16[128,3072]{0,1:T(8,128)(2,1)} %collective-permute-done.12), channel_id=1, source_target_pairs={{0,1},{1,0},{2,3},{3,2},{4,5},{5,4},{6,7},{7,6},{8,9},{9,8},{10,11... | collective-permute-start | bytes 2359304 | tf_op jit(solution)/shard_map/ppermute | solution.py:440
  169.5 21.3 %collective-permute-start.16 = (bf16[128,3072]{0,1:T(8,128)(2,1)}, bf16[128,3072]{0,1:T(8,128)(2,1)}, u32[]{:S(2)}, u32[]{:S(2)}) collective-permute-start(bf16[128,3072]{0,1:T(8,128)(2,1)} %collective-permute-done.12), channel_id=1, source_target_pairs={{0,4},{4,0},{8,12},{12,8},{16,20},{20,16},{24,28},{28,24},{1,5},{5... | collective-permute-start | bytes 2359304 | tf_op jit(solution)/shard_map/ppermute | solution.py:440
  197.6 31.8 %collective-permute-start.21 = (bf16[256,1536]{1,0:T(8,128)(2,1)}, bf16[256,1536]{1,0:T(8,128)(2,1)}, u32[]{:S(2)}, u32[]{:S(2)}) collective-permute-start(bf16[256,1536]{1,0:T(8,128)(2,1)} %collective-permute-done.19), channel_id=1, source_target_pairs={{0,1},{1,0},{2,3},{3,2},{4,5},{5,4},{6,7},{7,6},{8,9},{9,8},{10,11... | collective-permute-start | bytes 2359304 | tf_op jit(solution)/shard_map/ppermute | solution.py:440
  198.1 31.3 %collective-permute-start.23 = (bf16[256,1536]{1,0:T(8,128)(2,1)}, bf16[256,1536]{1,0:T(8,128)(2,1)}, u32[]{:S(2)}, u32[]{:S(2)}) collective-permute-start(bf16[256,1536]{1,0:T(8,128)(2,1)} %collective-permute-done.19), channel_id=1, source_target_pairs={{0,4},{4,0},{8,12},{12,8},{16,20},{20,16},{24,28},{28,24},{1,5},{5... | collective-permute-start | bytes 2359304 | tf_op jit(solution)/shard_map/ppermute | solution.py:440
  198.5 47.0 %all-to-all-start.1 = ((f32[8,128,384]{2,1,0:T(8,128)}), f32[8,128,384]{2,1,0:T(8,128)}, u32[]{:S(2)}, u32[]{:S(2)}) async-start(f32[8,128,384]{2,1,0:T(8,128)} %fusion.31), calls=%async_computation.1 | async-start | bytes 3145728 | tf_op jit(solution)/shard_map/all_to_all | solution.py:430
  264.5 39.4 %all-to-all-start.2 = ((bf16[8,131,384]{2,1,0:T(8,128)(2,1)}), bf16[8,131,384]{2,1,0:T(8,128)(2,1)}, u32[]{:S(2)}, u32[]{:S(2)}) async-start(bf16[8,131,384]{2,1,0:T(8,128)(2,1)} %maximum_bitcast_fusion.1), calls=%async_computation.2 | async-start | bytes 1671168 | tf_op jit(solution)/shard_map/all_to_all | solution.py:417
  273.4 48.5 %collective-permute-start.29 = (bf16[256,1536]{1,0:T(8,128)(2,1)}, bf16[256,1536]{1,0:T(8,128)(2,1)}, u32[]{:S(2)}, u32[]{:S(2)}) collective-permute-start(bf16[256,1536]{1,0:T(8,128)(2,1)} %bitcast.169), channel_id=1, source_target_pairs={{0,1},{1,0},{2,3},{3,2},{4,5},{5,4},{6,7},{7,6},{8,9},{9,8},{10,11... | collective-permute-start | bytes 2359304 | tf_op jit(solution)/shard_map/ppermute | solution.py:440
  290.9 31.0 %collective-permute-start.30 = (bf16[256,1536]{1,0:T(8,128)(2,1)}, bf16[256,1536]{1,0:T(8,128)(2,1)}, u32[]{:S(2)}, u32[]{:S(2)}) collective-permute-start(bf16[256,1536]{1,0:T(8,128)(2,1)} %collective-permute-done.28.refs_5_), channel_id=1, source_target_pairs={{0,1},{1,0},{2,3},{3,2},{4,5},{5,4},{6,7},{7,6},{8,9},{9,8},{10,11... | collective-permute-start | bytes 2359304 | tf_op jit(solution)/shard_map/ppermute | solution.py:440
  290.9 87.8 %collective-permute-start.34 = (bf16[256,3072]{1,0:T(8,128)(2,1)}, bf16[256,3072]{1,0:T(8,128)(2,1)}, u32[]{:S(2)}, u32[]{:S(2)}) collective-permute-start(bf16[256,3072]{1,0:T(8,128)(2,1)} %get-tuple-element.97.refs_4_), channel_id=1, source_target_pairs={{0,2},{1,3},{2,0},{3,1},{4,6},{5,7},{6,4},{7,5},{8,10},{9,11},{10,... | collective-permute-start | bytes 4718600 | tf_op jit(solution)/shard_map/ppermute | solution.py:440
  291.9 88.0 %collective-permute-start.35 = (bf16[256,3072]{1,0:T(8,128)(2,1)}, bf16[256,3072]{1,0:T(8,128)(2,1)}, u32[]{:S(2)}, u32[]{:S(2)}) collective-permute-start(bf16[256,3072]{1,0:T(8,128)(2,1)} %get-tuple-element.97.refs_4_), channel_id=1, source_target_pairs={{0,1},{1,0},{2,3},{3,2},{4,5},{5,4},{6,7},{7,6},{8,9},{9,8},{10,11... | collective-permute-start | bytes 4718600 | tf_op jit(solution)/shard_map/ppermute | solution.py:440
  311.4 56.7 %all-to-all-start.3 = ((bf16[8,128,384]{2,1,0:T(8,128)(2,1)}), bf16[8,128,384]{2,1,0:T(8,128)(2,1)}, u32[]{:S(2)}, u32[]{:S(2)}) async-start(bf16[8,128,384]{2,1,0:T(8,128)(2,1)} %broadcast_dynamic-update-slice_fusion.1), calls=%async_computation.3 | async-start | bytes 1572864 | tf_op jit(solution)/shard_map/all_to_all | solution.py:430
  321.9 22.5 %collective-permute-start.27 = (bf16[256,768]{1,0:T(8,128)(2,1)}, bf16[256,768]{1,0:T(8,128)(2,1)}, u32[]{:S(2)}, u32[]{:S(2)}) collective-permute-start(bf16[256,768]{1,0:T(8,128)(2,1)} %get-tuple-element.168), channel_id=1, source_target_pairs={{0,3},{1,2},{2,1},{3,0},{4,7},{5,6},{6,5},{7,4},{8,11},{9,10},{10,... | collective-permute-start | bytes 1179656 | tf_op jit(solution)/shard_map/ppermute | solution.py:440
  351.8 40.5 %collective-permute-start.63 = (bf16[384,1536]{1,0:T(8,128)(2,1)}, bf16[384,1536]{1,0:T(8,128)(2,1)}, u32[]{:S(2)}, u32[]{:S(2)}) collective-permute-start(bf16[384,1536]{1,0:T(8,128)(2,1)} %get-tuple-element.107), channel_id=1, source_target_pairs={{0,4},{4,0},{8,12},{12,8},{16,20},{20,16},{24,28},{28,24},{1,5},{5... | collective-permute-start | bytes 3538952 | tf_op jit(solution)/shard_map/ppermute | solution.py:440
  355.4 43.4 %collective-permute-start.31 = (bf16[256,384]{1,0:T(8,128)(2,1)}, bf16[256,384]{1,0:T(8,128)(2,1)}, u32[]{:S(2)}, u32[]{:S(2)}) collective-permute-start(bf16[256,384]{1,0:T(8,128)(2,1)} %get-tuple-element.176), channel_id=1, source_target_pairs={{0,2},{1,3},{2,0},{3,1},{4,6},{5,7},{6,4},{7,5},{8,10},{9,11},{10,... | collective-permute-start | bytes 589832 | tf_op jit(solution)/shard_map/ppermute | solution.py:440
  356.4 42.4 %collective-permute-start.32 = (bf16[256,384]{1,0:T(8,128)(2,1)}, bf16[256,384]{1,0:T(8,128)(2,1)}, u32[]{:S(2)}, u32[]{:S(2)}) collective-permute-start(bf16[256,384]{1,0:T(8,128)(2,1)} %get-tuple-element.175), channel_id=1, source_target_pairs={{0,1},{1,0},{2,3},{3,2},{4,5},{5,4},{6,7},{7,6},{8,9},{9,8},{10,11... | collective-permute-start | bytes 589832 | tf_op jit(solution)/shard_map/ppermute | solution.py:440
  418.7 67.5 %collective-permute-start.66 = (bf16[96,1536]{1,0:T(8,128)(2,1)}, bf16[96,1536]{1,0:T(8,128)(2,1)}, u32[]{:S(2)}, u32[]{:S(2)}) collective-permute-start(bf16[96,1536]{1,0:T(8,128)(2,1)} %get-tuple-element.154), channel_id=1, source_target_pairs={{0,24},{4,28},{8,16},{12,20},{16,8},{20,12},{24,0},{28,4},{1,25},{... | collective-permute-start | bytes 884744 | tf_op jit(solution)/shard_map/ppermute | solution.py:440
  419.2 67.1 %collective-permute-start.65 = (bf16[96,1536]{1,0:T(8,128)(2,1)}, bf16[96,1536]{1,0:T(8,128)(2,1)}, u32[]{:S(2)}, u32[]{:S(2)}) collective-permute-start(bf16[96,1536]{1,0:T(8,128)(2,1)} %get-tuple-element.155), channel_id=1, source_target_pairs={{0,16},{4,20},{8,24},{12,28},{16,0},{20,4},{24,8},{28,12},{1,17},{... | collective-permute-start | bytes 884744 | tf_op jit(solution)/shard_map/ppermute | solution.py:440
  422.5 64.8 %collective-permute-start.64 = (bf16[96,1536]{1,0:T(8,128)(2,1)}, bf16[96,1536]{1,0:T(8,128)(2,1)}, u32[]{:S(2)}, u32[]{:S(2)}) collective-permute-start(bf16[96,1536]{1,0:T(8,128)(2,1)} %get-tuple-element.153), channel_id=1, source_target_pairs={{0,8},{4,12},{8,0},{12,4},{16,24},{20,28},{24,16},{28,20},{1,9},{5... | collective-permute-start | bytes 884744 | tf_op jit(solution)/shard_map/ppermute | solution.py:440
  434.7 40.5 %collective-permute-start.52 = (bf16[256,3456]{1,0:T(8,128)(2,1)}, bf16[256,3456]{1,0:T(8,128)(2,1)}, u32[]{:S(2)}, u32[]{:S(2)}) collective-permute-start(bf16[256,3456]{1,0:T(8,128)(2,1)} %concatenate.61.refs_4_), channel_id=1, source_target_pairs={{0,2},{1,3},{2,0},{3,1},{4,6},{5,7},{6,4},{7,5},{8,10},{9,11},{10,... | collective-permute-start | bytes 5308424 | tf_op jit(solution)/shard_map/ppermute | solution.py:440
  435.7 39.5 %collective-permute-start.53 = (bf16[256,3456]{1,0:T(8,128)(2,1)}, bf16[256,3456]{1,0:T(8,128)(2,1)}, u32[]{:S(2)}, u32[]{:S(2)}) collective-permute-start(bf16[256,3456]{1,0:T(8,128)(2,1)} %concatenate.61.refs_4_), channel_id=1, source_target_pairs={{0,1},{1,0},{2,3},{3,2},{4,5},{5,4},{6,7},{7,6},{8,9},{9,8},{10,11... | collective-permute-start | bytes 5308424 | tf_op jit(solution)/shard_map/ppermute | solution.py:440
  488.8 22.7 %collective-permute-start.69 = (bf16[96,1536]{1,0:T(8,128)(2,1)S(1)}, bf16[96,1536]{1,0:T(8,128)(2,1)}, u32[]{:S(2)}, u32[]{:S(2)}) collective-permute-start(bf16[96,1536]{1,0:T(8,128)(2,1)S(1)} %add_convert_fusion.2), channel_id=1, source_target_pairs={{0,24},{4,28},{8,16},{12,20},{16,8},{20,12},{24,0},{28,4},{1,25},{... | collective-permute-start | bytes 884744 | tf_op jit(solution)/shard_map/ppermute | solution.py:440
  489.4 26.2 %collective-permute-start.68 = (bf16[96,1536]{1,0:T(8,128)(2,1)S(1)}, bf16[96,1536]{1,0:T(8,128)(2,1)}, u32[]{:S(2)}, u32[]{:S(2)}) collective-permute-start(bf16[96,1536]{1,0:T(8,128)(2,1)S(1)} %add_convert_fusion.2), channel_id=1, source_target_pairs={{0,16},{4,20},{8,24},{12,28},{16,0},{20,4},{24,8},{28,12},{1,17},{... | collective-permute-start | bytes 884744 | tf_op jit(solution)/shard_map/ppermute | solution.py:440
  503.1 29.2 %collective-permute-start.44 = (bf16[192,3072]{1,0:T(8,128)(2,1)}, bf16[192,3072]{1,0:T(8,128)(2,1)S(1)}, u32[]{:S(2)}, u32[]{:S(2)}) collective-permute-start(bf16[192,3072]{1,0:T(8,128)(2,1)} %get-tuple-element.101), channel_id=1, source_target_pairs={{0,4},{4,0},{8,12},{12,8},{16,20},{20,16},{24,28},{28,24},{1,5},{5... | collective-permute-start | bytes 3538952 | tf_op jit(solution)/shard_map/ppermute | solution.py:440
  505.9 54.9 %collective-permute-start.55 = (bf16[192,3456]{1,0:T(8,128)(2,1)}, bf16[192,3456]{1,0:T(8,128)(2,1)S(1)}, u32[]{:S(2)}, u32[]{:S(2)}) collective-permute-start(bf16[192,3456]{1,0:T(8,128)(2,1)} %get-tuple-element.106), channel_id=1, source_target_pairs={{0,4},{4,0},{8,12},{12,8},{16,20},{20,16},{24,28},{28,24},{1,5},{5... | collective-permute-start | bytes 3981320 | tf_op jit(solution)/shard_map/ppermute | solution.py:440
  517.9 155.9 %collective-permute-start.70 = (bf16[4,96,1536]{2,1,0:T(8,128)(2,1)}, bf16[4,96,1536]{2,1,0:T(8,128)(2,1)}, u32[]{:S(2)}, u32[]{:S(2)}) collective-permute-start(bf16[4,96,1536]{2,1,0:T(8,128)(2,1)} %pad_maximum_fusion.3.refs_0_), channel_id=1, source_target_pairs={{0,4},{4,0},{8,12},{12,8},{16,20},{20,16},{24,28},{28,24},{1,5},{5... | collective-permute-start | bytes 3538952 | tf_op jit(solution)/shard_map/ppermute | solution.py:440
  525.3 145.2 %collective-permute-start.43 = (f32[1,5348]{1,0:T(1,128)S(1)}, f32[1,5348]{1,0:T(1,128)S(1)}, u32[]{:S(2)}, u32[]{:S(2)}) collective-permute-start(f32[1,5348]{1,0:T(1,128)S(1)} %add.561), channel_id=1, source_target_pairs={{0,4},{4,0},{8,12},{12,8},{16,20},{20,16},{24,28},{28,24},{1,5},{5... | collective-permute-start | bytes 64184 | tf_op jit(solution)/shard_map/ppermute | solution.py:440
  561.1 30.1 %collective-permute-start.58 = (bf16[48,3456]{1,0:T(8,128)(2,1)S(1)}, bf16[48,3456]{1,0:T(8,128)(2,1)S(1)}, u32[]{:S(2)}, u32[]{:S(2)}) collective-permute-start(bf16[48,3456]{1,0:T(8,128)(2,1)S(1)} %get-tuple-element.151), channel_id=1, source_target_pairs={{0,24},{4,28},{8,16},{12,20},{16,8},{20,12},{24,0},{28,4},{1,25},{... | collective-permute-start | bytes 995336 | tf_op jit(solution)/shard_map/ppermute | solution.py:440
  561.6 33.7 %collective-permute-start.57 = (bf16[48,3456]{1,0:T(8,128)(2,1)S(1)}, bf16[48,3456]{1,0:T(8,128)(2,1)S(1)}, u32[]{:S(2)}, u32[]{:S(2)}) collective-permute-start(bf16[48,3456]{1,0:T(8,128)(2,1)S(1)} %get-tuple-element.152), channel_id=1, source_target_pairs={{0,16},{4,20},{8,24},{12,28},{16,0},{20,4},{24,8},{28,12},{1,17},{... | collective-permute-start | bytes 995336 | tf_op jit(solution)/shard_map/ppermute | solution.py:440
  565.5 33.2 %collective-permute-start.56 = (bf16[48,3456]{1,0:T(8,128)(2,1)S(1)}, bf16[48,3456]{1,0:T(8,128)(2,1)S(1)}, u32[]{:S(2)}, u32[]{:S(2)}) collective-permute-start(bf16[48,3456]{1,0:T(8,128)(2,1)S(1)} %get-tuple-element.150), channel_id=1, source_target_pairs={{0,8},{4,12},{8,0},{12,4},{16,24},{20,28},{24,16},{28,20},{1,9},{5... | collective-permute-start | bytes 995336 | tf_op jit(solution)/shard_map/ppermute | solution.py:440
  591.2 26.9 %collective-permute-start.47 = (bf16[48,3072]{1,0:T(8,128)(2,1)S(1)}, bf16[48,3072]{1,0:T(8,128)(2,1)S(1)}, u32[]{:S(2)}, u32[]{:S(2)}) collective-permute-start(bf16[48,3072]{1,0:T(8,128)(2,1)S(1)} %get-tuple-element.157), channel_id=1, source_target_pairs={{0,24},{4,28},{8,16},{12,20},{16,8},{20,12},{24,0},{28,4},{1,25},{... | collective-permute-start | bytes 884744 | tf_op jit(solution)/shard_map/ppermute | solution.py:440
  595.3 26.1 %collective-permute-start.46 = (bf16[48,3072]{1,0:T(8,128)(2,1)S(1)}, bf16[48,3072]{1,0:T(8,128)(2,1)S(1)}, u32[]{:S(2)}, u32[]{:S(2)}) collective-permute-start(bf16[48,3072]{1,0:T(8,128)(2,1)S(1)} %get-tuple-element.158), channel_id=1, source_target_pairs={{0,16},{4,20},{8,24},{12,28},{16,0},{20,4},{24,8},{28,12},{1,17},{... | collective-permute-start | bytes 884744 | tf_op jit(solution)/shard_map/ppermute | solution.py:440
  598.7 26.1 %collective-permute-start.45 = (bf16[48,3072]{1,0:T(8,128)(2,1)S(1)}, bf16[48,3072]{1,0:T(8,128)(2,1)S(1)}, u32[]{:S(2)}, u32[]{:S(2)}) collective-permute-start(bf16[48,3072]{1,0:T(8,128)(2,1)S(1)} %get-tuple-element.156), channel_id=1, source_target_pairs={{0,8},{4,12},{8,0},{12,4},{16,24},{20,28},{24,16},{28,20},{1,9},{5... | collective-permute-start | bytes 884744 | tf_op jit(solution)/shard_map/ppermute | solution.py:440
  618.0 26.9 %collective-permute-start.61 = (bf16[48,3456]{1,0:T(8,128)(2,1)S(1)}, bf16[48,3456]{1,0:T(8,128)(2,1)S(1)}, u32[]{:S(2)}, u32[]{:S(2)}) collective-permute-start(bf16[48,3456]{1,0:T(8,128)(2,1)S(1)} %add_convert_fusion.1), channel_id=1, source_target_pairs={{0,24},{4,28},{8,16},{12,20},{16,8},{20,12},{24,0},{28,4},{1,25},{... | collective-permute-start | bytes 995336 | tf_op jit(solution)/shard_map/ppermute | solution.py:440
  621.4 27.6 %collective-permute-start.60 = (bf16[48,3456]{1,0:T(8,128)(2,1)S(1)}, bf16[48,3456]{1,0:T(8,128)(2,1)S(1)}, u32[]{:S(2)}, u32[]{:S(2)}) collective-permute-start(bf16[48,3456]{1,0:T(8,128)(2,1)S(1)} %add_convert_fusion.1), channel_id=1, source_target_pairs={{0,16},{4,20},{8,24},{12,28},{16,0},{20,4},{24,8},{28,12},{1,17},{... | collective-permute-start | bytes 995336 | tf_op jit(solution)/shard_map/ppermute | solution.py:440
  624.8 27.6 %collective-permute-start.59 = (bf16[48,3456]{1,0:T(8,128)(2,1)S(1)}, bf16[48,3456]{1,0:T(8,128)(2,1)S(1)}, u32[]{:S(2)}, u32[]{:S(2)}) collective-permute-start(bf16[48,3456]{1,0:T(8,128)(2,1)S(1)} %add_convert_fusion.1), channel_id=1, source_target_pairs={{0,8},{4,12},{8,0},{12,4},{16,24},{20,28},{24,16},{28,20},{1,9},{5... | collective-permute-start | bytes 995336 | tf_op jit(solution)/shard_map/ppermute | solution.py:440
  664.6 52.9 %collective-permute-start.62 = (bf16[4,48,3456]{2,1,0:T(8,128)(2,1)S(1)}, bf16[4,48,3456]{2,1,0:T(8,128)(2,1)}, u32[]{:S(2)}, u32[]{:S(2)}) collective-permute-start(bf16[4,48,3456]{2,1,0:T(8,128)(2,1)S(1)} %pad_maximum_fusion.1.near_b_ref), channel_id=1, source_target_pairs={{0,4},{4,0},{8,12},{12,8},{16,20},{20,16},{24,28},{28,24},{1,5},{5... | collective-permute-start | bytes 3981320 | tf_op jit(solution)/shard_map/ppermute | solution.py:440
  667.3 50.2 %collective-permute-start.51 = (bf16[4,48,3072]{2,1,0:T(8,128)(2,1)S(1)}, bf16[4,48,3072]{2,1,0:T(8,128)(2,1)}, u32[]{:S(2)}, u32[]{:S(2)}) collective-permute-start(bf16[4,48,3072]{2,1,0:T(8,128)(2,1)S(1)} %pad_maximum_fusion.2.near_a_ref), channel_id=1, source_target_pairs={{0,4},{4,0},{8,12},{12,8},{16,20},{20,16},{24,28},{28,24},{1,5},{5... | collective-permute-start | bytes 3538952 | tf_op jit(solution)/shard_map/ppermute | solution.py:440
  (92 other events, 1116.5 us)
